TPU v7x, 512 devices: a whole 4x4x16 slice. The times are simulated.
512 devices in a mesh: row: 16 (over y, x), col: 32 (over z, core).
Axes of the slice: x: 4, y: 4, z: 16, core: 2. Of those that a mesh axis runs over, the one named last changes fastest.
Arguments:
- queries: bfloat16 [16, 1024, 3840], P('row', 'col'), may hold values from -240 to 240
- tree_latent: bfloat16 [16, 1024, 288], P('row', 'col'), may hold values from -6 to 6
- parents: int32 [16, 32, 32], P('row', 'col'), may hold values from -1 to 30, as said below
- cache: bfloat16 [16, 32, 256, 288], P('row', 'col'), may hold values from -6 to 6
- cache_lengths: int32 [16, 32], P('row', 'col'), may hold values from 1 to 256, 6144 in all within a row
- accepted: int32 [16, 32, 8], P('row', 'col'), may hold values from 0 to 31
- residual: bfloat16 [16, 1024, 2560], P(None, 'col', 'row'), may hold values from -6 to 6
- long_queries: bfloat16 [32, 32, 3840], P('col'), may hold values from -240 to 240
- long_tree_latent: bfloat16 [32, 32, 288], P('col'), may hold values from -6 to 6
- long_parents: int32 [32, 32], P('col'), may hold values from -1 to 30, as said below
- long_cache: bfloat16 [32, 4096, 288], P('col', 'row'), may hold values from -6 to 6
- long_plan: int32 [32, 16], P('col', 'row'), may hold values from 1 to 256, 3072 in all within a row
- long_residual: bfloat16 [32, 32, 2560], P('col', None, 'row'), may hold values from -6 to 6
- key_up: bfloat16 [2560, 256], P('col'), may hold values from -0.75 to 0.75
- value_up: bfloat16 [2560, 256], P('col'), may hold values from -0.375 to 0.375
- out_weight: bfloat16 [2560, 2560], P('col', 'row'), may hold values from -0.125 to 0.125
Outputs:
- hidden: bfloat16 [16, 1024, 2560], P(None, 'col', 'row')
- accepted_cache: bfloat16 [16, 32, 8, 288], P('row', 'col')
- long_hidden: bfloat16 [32, 32, 2560], P('col', None, 'row')
Inputs may be any that keep to these rules, and one draw needn't show every extreme that they name: parents[..., 0] = -1 (the root); every other position's parent lies before it. long_parents[..., 0] = -1 (the root); every other position's parent lies before it.
All inputs are finite; a program needn't handle non-finite values. No bound on the sum of `cache_lengths` or of `long_plan` on one device may be relied on, other than what follows from the above.
Results may differ from a plain program's by a relative error of at most 0.0095.
Values may be sent and summed in bfloat16 or wider, within the bound.
No kernel may reach another device: no remote copies, remote signals or barrier semaphores. Data moves between devices by JAX's collectives and lax.ppermute only.
A program may use at most 128 MiB of HBM per device.

v0:
```python
import jax
import jax.numpy as jnp
from jax import lax
from jax.sharding import PartitionSpec as P

HEADS = 40
NOPE = 64
ROPE = 32
VDIM = 64
KVR = 256


def combined_all(value, axis, join):
    pieces = jax.tree.map(lambda part: lax.all_gather(part, axis), value)
    head = jax.tree.map(lambda part: part[0], pieces)
    tail = jax.tree.map(lambda part: part[1:], pieces)
    subtotal, _ = lax.scan(lambda subtotal, piece: (join(subtotal, piece), None), head, tail)
    return subtotal


def tree_reach(parent_ids):
    tree_count = parent_ids.shape[-1]
    positions = jnp.arange(tree_count, dtype=jnp.int32)
    reach_mat = (parent_ids[..., :, None] == positions).astype(jnp.float32)
    reach_mat = reach_mat + (positions[:, None] == positions[None, :]).astype(jnp.float32)
    for square_turn in range(max(1, (tree_count - 1).bit_length())):
        product = jnp.einsum(
            "...ij,...jk->...ik", reach_mat, reach_mat, precision=lax.Precision.HIGHEST
        )
        reach_mat = jnp.minimum(reach_mat + product, 1.0)
    return reach_mat > 0.5


def query_cat(query_rows, key_full):
    per_head = query_rows.reshape(query_rows.shape[:-1] + (HEADS, NOPE + ROPE))
    key_heads = key_full.reshape(HEADS, NOPE, KVR)
    latent = jnp.einsum(
        "...hd,hdk->...hk", per_head[..., :NOPE], key_heads, preferred_element_type=jnp.float32
    )
    return jnp.concatenate([latent.astype(jnp.bfloat16), per_head[..., NOPE:]], axis=-1)


def block_terms(query_block, key_rows, allowed):
    score_scale = (NOPE + ROPE) ** (-0.5)
    scores = (
        jnp.einsum("thc,pc->thp", query_block, key_rows, preferred_element_type=jnp.float32)
        * score_scale
    )
    scores = jnp.where(allowed[:, None, :], scores, -jnp.inf)
    row_max = jnp.max(scores, axis=-1)
    weights_row = jnp.where(allowed[:, None, :], jnp.exp(scores - row_max[..., None]), 0.0).astype(
        jnp.bfloat16
    )
    row_total = jnp.sum(weights_row.astype(jnp.float32), axis=-1)
    row_acc = jnp.einsum(
        "thp,pk->thk", weights_row, key_rows[:, :KVR], preferred_element_type=jnp.float32
    )
    return (row_max, row_total, row_acc)


def combine_parts(earlier, later):
    overall = jnp.maximum(earlier[0], later[0])
    early_factor = jnp.exp(earlier[0] - overall)
    late_factor = jnp.exp(later[0] - overall)
    summed = earlier[1] * early_factor + later[1] * late_factor
    merged = earlier[2] * early_factor[..., None] + later[2] * late_factor[..., None]
    return (overall, summed, merged)


def on_device(
    queries,
    tree_latent,
    parents,
    cache,
    cache_lengths,
    accepted,
    residual,
    long_queries,
    long_tree_latent,
    long_parents,
    long_cache,
    long_plan,
    long_residual,
    key_up,
    value_up,
    out_weight,
):
    key_full, value_full, out_block = (
        lax.all_gather(key_up, "col", axis=0, tiled=True),
        lax.all_gather(value_up, "col", axis=0, tiled=True),
        lax.all_gather(out_weight, "col", axis=0, tiled=True),
    )
    requests = parents.shape[1]
    tree_size = parents.shape[2]
    cache_size = cache.shape[2]
    row_width = cache.shape[3]
    score_scale = (NOPE + ROPE) ** (-0.5)
    value_heads = value_full.reshape(HEADS, VDIM, KVR)
    query_block = query_cat(queries[0].reshape(requests, tree_size, queries.shape[-1]), key_full)
    latent_rows = tree_latent[0].reshape(requests, tree_size, row_width)
    key_rows = jnp.concatenate([cache[0], latent_rows], axis=1)
    cache_ok = (
        jnp.arange(cache_size, dtype=jnp.int32)[None, None, :] < cache_lengths[0][:, None, None]
    )
    cache_ok = jnp.broadcast_to(cache_ok, (requests, tree_size, cache_size))
    allowed = jnp.concatenate([cache_ok, tree_reach(parents[0])], axis=2)
    scores = (
        jnp.einsum("rthc,rpc->rthp", query_block, key_rows, preferred_element_type=jnp.float32)
        * score_scale
    )
    scores = jnp.where(allowed[:, :, None, :], scores, -jnp.inf)
    row_max = jnp.max(scores, axis=-1, keepdims=True)
    exponent = jnp.exp(scores - row_max)
    probability = (exponent / jnp.sum(exponent, axis=-1, keepdims=True)).astype(jnp.bfloat16)
    latent = jnp.einsum(
        "rthp,rpk->rthk", probability, key_rows[..., :KVR], preferred_element_type=jnp.float32
    ).astype(jnp.bfloat16)
    head_out = jnp.einsum(
        "rthk,hek->rthe", latent, value_heads, preferred_element_type=jnp.float32
    ).astype(jnp.bfloat16)
    head_out = head_out.reshape(requests * tree_size, HEADS * VDIM)
    projected = jnp.dot(
        lax.all_gather(head_out, "row", axis=0, tiled=True),
        out_block,
        preferred_element_type=jnp.float32,
    )
    hidden = (residual.astype(jnp.float32) + projected.reshape(residual.shape)).astype(jnp.bfloat16)
    accepted_cache = jnp.take_along_axis(latent_rows, accepted[0][..., None], axis=1)[None]
    long_block = query_cat(long_queries[0], key_full)
    piece_size = long_cache.shape[1]
    piece_ok = jnp.arange(piece_size, dtype=jnp.int32)[None, :] < long_plan[0, 0]
    piece_ok = jnp.broadcast_to(piece_ok, (tree_size, piece_size))
    piece_max, piece_total, piece_acc = block_terms(long_block, long_cache[0], piece_ok)
    tree_max, tree_total, tree_acc = block_terms(
        long_block, long_tree_latent[0], tree_reach(long_parents[0])
    )
    value_float = value_heads.astype(jnp.float32)
    merged_max, merged_total, merged_acc = combined_all(
        (piece_max, piece_total, piece_acc), "row", combine_parts
    )
    overall, denominator, numerator = combine_parts(
        (merged_max, merged_total, merged_acc), (tree_max, tree_total, tree_acc)
    )
    long_out = (
        jnp.einsum("thk,hek->the", numerator, value_float, precision=lax.Precision.HIGHEST)
        / denominator[..., None]
    )
    long_heads = long_out.astype(jnp.bfloat16).reshape(tree_size, HEADS * VDIM)
    long_projected = jnp.dot(long_heads, out_block, preferred_element_type=jnp.float32)
    long_hidden = (long_residual[0].astype(jnp.float32) + long_projected).astype(jnp.bfloat16)[None]
    return (hidden, accepted_cache, long_hidden)


def solution(mesh):
    return jax.shard_map(
        on_device,
        mesh=mesh,
        in_specs=(
            P("row", "col", None),
            P("row", "col", None),
            P("row", "col", None),
            P("row", "col", None, None),
            P("row", "col"),
            P("row", "col", None),
            P(None, "col", "row"),
            P("col", None, None),
            P("col", None, None),
            P("col", None),
            P("col", "row", None),
            P("col", "row"),
            P("col", None, "row"),
            P("col", None),
            P("col", None),
            P("col", "row"),
        ),
        out_specs=(P(None, "col", "row"), P("row", "col", None, None), P("col", None, "row")),
        check_vma=False,
    )
```

profile of v0, /device:TPU:1, one launch (start us, length us, event | category | flops | bytes accessed | tf_op | source)
XLA Modules:
  0.0 435.5 jit_solution(14481738731269412697)
XLA Ops:
  8.7 1.5 reshape_reshape_squeeze.3
  12.2 74.9 %all-gather.8.cloned.1.call-done = bf16[2560,256]{1,0:T(8,128)(2,1)} async-done(((bf16[80,256]{1,0:T(8,128)(2,1)}), bf16[2560,256]{1,0:T(8,128)(2,1)}) %all-gather.8.cloned.1.call-update) | async-done | bytes 1310736 | tf_op jit(solution)/shard_map/all_gather | solution.py:89
  87.0 1.6 fusion.10
  89.4 1.3 fusion.89
  90.9 66.4 %all-gather.10.cloned.1.call-done = bf16[2560,256]{1,0:T(8,128)(2,1)} async-done(((bf16[80,256]{1,0:T(8,128)(2,1)}), bf16[2560,256]{1,0:T(8,128)(2,1)}) %all-gather.10.cloned.1.call-update) | async-done | bytes 1310736 | tf_op jit(solution)/shard_map/all_gather | solution.py:90
  157.3 2.6 fusion.23
  160.0 0.9 reshape.363
  164.1 1.5 fusion.57
  168.4 33.0 %all_gather.33 = bf16[2560,160]{1,0:T(8,128)(2,1)S(1)} all-gather(bf16[80,160]{1,0:T(8,128)(2,1)S(1)} %copy-done.10), channel_id=1, replica_groups=mesh['row'=16,'col'=32] {'col'}, dimensions={0}, use_global_device_ids=true | all-gather | bytes 844800 | tf_op jit(solution)/shard_map/all_gather | solution.py:91
  201.9 20.4 %all-gather.1 = f32[512,40]{1,0:T(8,128)S(1)} all-gather(f32[32,40]{1,0:T(8,128)S(1)} %convert_reduce_fusion), channel_id=3, replica_groups=mesh['row'=16,'col'=32] {'row'}, dimensions={0}, use_global_device_ids=true | all-gather | bytes 87040 | tf_op jit(solution)/shard_map/all_gather | solution.py:14
  223.1 17.1 %all-gather = f32[512,40]{1,0:T(8,128)S(1)} all-gather(f32[32,40]{1,0:T(8,128)S(1)} %get-tuple-element.68), channel_id=2, replica_groups=mesh['row'=16,'col'=32] {'row'}, dimensions={0}, use_global_device_ids=true | all-gather | bytes 87040 | tf_op jit(solution)/shard_map/all_gather | solution.py:14
  241.0 1.3 fusion.95
  242.6 2.6 fusion.96
  245.3 0.8 add_convert_fusion
  246.1 124.1 %all-gather.14.cloned.1.call-done = f32[512,40,256]{2,1,0:T(8,128)} async-done(((f32[32,40,256]{2,1,0:T(8,128)}), f32[512,40,256]{2,1,0:T(8,128)}) %all-gather.14.cloned.1.call-update) | async-done | bytes 20971536 | tf_op jit(solution)/shard_map/all_gather | solution.py:14
  370.2 15.0 %slice.72 = f32[480,40,256]{2,1,0:T(8,128)} slice(f32[512,40,256]{2,1,0:T(8,128)} %all-gather.14.cloned.1.call-done), slice={[32:512], [0:40], [0:256]} | slice | bytes 39321600 | tf_op jit(solution)/shard_map/slice | solution.py:16
  385.2 1.3 slice-done
  386.5 38.3 %while.14 = (s32[]{:T(128)}, f32[32,40]{1,0:T(8,128)S(1)}, f32[32,40]{1,0:T(8,128)S(1)}, f32[32,40,256]{2,1,0:T(8,128)S(1)}, f32[15,32,40]{2,1,0:T(8,128)}, /*in...) while((s32[]{:T(128)}, f32[32,40]{1,0:T(8,128)S(1)}, f32[32,40]{1,0:T(8,128)S(1)}, ...), condition=%wide.region_5.6_spmd, body=%wide.region_4.5_spmd.sunk | while | flops 990722 | bytes 3983453 | solution.py:17
  387.2 1.8 fusion.126
  389.0 0.8 fusion.125
  389.8 1.8 fusion.126
  391.6 0.8 fusion.125
  392.3 1.8 fusion.126
  394.1 0.8 fusion.125
  394.9 1.8 fusion.126
  396.7 0.8 fusion.125
  397.4 1.8 fusion.126
  399.2 0.8 fusion.125
  400.0 1.8 fusion.126
  401.8 0.8 fusion.125
  402.6 1.8 fusion.126
  404.4 0.8 fusion.125
  405.1 1.8 fusion.126
  406.9 0.8 fusion.125
  407.7 1.8 fusion.126
  409.5 0.8 fusion.125
  410.2 1.8 fusion.126
  412.0 0.8 fusion.125
  412.8 1.8 fusion.126
  414.6 0.8 fusion.125
  415.3 1.8 fusion.126
  417.1 0.8 fusion.125
  417.9 1.8 fusion.126
  419.7 0.8 fusion.125
  420.4 1.8 fusion.126
  423.0 1.8 fusion.126
  426.2 1.5 fusion.19
  428.1 0.9 fusion.25
  (92 shorter events, 14.5 us)
Async XLA Ops:
  7.2 3.9 copy-start.7
  7.2 4.1 copy-start.13
  7.2 79.8 %all-gather.8.cloned.1.call-start = ((), (), s32[]{:S(2)}) async-start(), calls=%async_computation | async-start | bytes 1351680 | tf_op jit(solution)/shard_map/all_gather | solution.py:89
  7.9 149.4 %all-gather.10.cloned.1.call-start = ((), (), s32[]{:S(2)}) async-start(), calls=%async_computation.1 | async-start | bytes 1351680 | tf_op jit(solution)/shard_map/all_gather | solution.py:90
  8.7 233.9 %all-gather.12.cloned.1.call-start = ((), (), s32[]{:S(2)}) async-start(), calls=%async_computation.2 | async-start | bytes 2785280 | tf_op jit(solution)/shard_map/all_gather | solution.py:123
  88.7 0.7 copy-start.9
  159.9 1.1 copy-start.6
  160.0 2.4 copy-start.8
  161.0 1.7 copy-start
  161.0 209.2 %all-gather.14.cloned.1.call-start = ((), (), s32[]{:S(2)}) async-start(), calls=%async_computation.3 | async-start | bytes 22282240 | tf_op jit(solution)/shard_map/all_gather | solution.py:14
  163.1 1.0 copy-start.3
  165.6 0.7 copy-start.15
  165.6 1.9 copy-start.16
  165.6 2.8 copy-start.10
  201.4 39.6 %copy-start.4 = (bf16[32,40,288]{2,0,1:T(8,128)(2,1)S(1)}, bf16[32,40,288]{2,0,1:T(8,128)(2,1)}, u32[]{:S(2)}) copy-start(bf16[32,40,288]{2,0,1:T(8,128)(2,1)} %copy-done.3) | copy-start | bytes 2211844
  201.4 39.6 %copy-start.12 = (bf16[1,32,288]{2,1,0:T(8,128)(2,1)S(1)}, bf16[1,32,288]{2,1,0:T(8,128)(2,1)}, u32[]{:S(2)}) copy-start(bf16[1,32,288]{2,1,0:T(8,128)(2,1)} %param.26) | copy-start | bytes 55300
  222.3 22.9 %copy-start.1 = (f32[512,40]{1,0:T(8,128)}, f32[512,40]{1,0:T(8,128)S(1)}, u32[]{:S(2)}) copy-start(f32[512,40]{1,0:T(8,128)S(1)} %all-gather.1) | copy-start | bytes 245764
  240.2 0.8 copy-start.2
  242.6 2.7 copy-start.5
  385.1 1.3 slice-start
  385.1 1.3 slice-start.1
  385.1 1.3 slice-start.2
  424.9 1.3 copy-start.14
  426.2 1.9 copy-start.11
Sparse Core Ops, SparseCore 0:
  10.1 76.8 all-gather.7
  89.1 68.1 all-gather.9
  161.1 58.0 all-gather.11
  222.1 148.0 all-gather.13
where the time goes:
time: 439 us; the launch traced here: 436 us
  waiting for transfers between devices  267 us (61%)
  blocking collectives  70.5 us (16%)
  other arithmetic  40.8 us (9%)
  local copies, waits for them, and re-layouts  24.8 us (6%)
  matrix products  16.7 us (4%)
  between operations  15.5 us (4%)
    all_gather x1, waiting for transfers between devices, combined_all(): pieces = jax.tree.map(lambda part: lax.all_gather(part, axis), value)  124 us
    all_gather x1, waiting for transfers between devices, on_device(): lax.all_gather(key_up, 'col', axis=0, tiled=True)  74.9 us
    all_gather x1, waiting for transfers between devices, on_device(): lax.all_gather(value_up, 'col', axis=0, tiled=True)  66.4 us
    all_gather x2, blocking collectives, combined_all(): pieces = jax.tree.map(lambda part: lax.all_gather(part, axis), value)  37.5 us
    all_gather x1, blocking collectives, on_device(): lax.all_gather(out_weight, 'col', axis=0, tiled=True)  33 us
    add x15, other arithmetic, combine_parts(): earlier[2] * early_factor[..., None] + later[2] * late_factor[..., None]  26.6 us
    slice x3, local copies, waits for them, and re-layouts, combined_all(): tail = jax.tree.map(lambda part: part[1:], pieces)  16.5 us
    add x16, other arithmetic, combine_parts(): summed = earlier[1] * early_factor + later[1] * late_factor  11.4 us
  transfers between devices with their start and end apart: 4, of which 3 were waited for; matrix products, arithmetic and copies ran while one was open for 4% of the time, Pallas kernels for 0%

commit v1 on v0

v1 whole, which is shorter than its diff:
```python
import jax
import jax.numpy as jnp
from jax import lax
from jax.experimental import pallas as pl
from jax.experimental.pallas import tpu as pltpu
from jax.sharding import Mesh, PartitionSpec as P

HEADS = 40
NOPE = 64
ROPE = 32
VDIM = 64
KVR = 256
TREE = 32
ROWS = ("y", "x")
COLS = ("z", "c")
SWAP = [(0, 1), (1, 0)]
BF = jnp.bfloat16
F32 = jnp.float32


def tree_reach(parent_ids):
    tree_count = parent_ids.shape[-1]
    positions = jnp.arange(tree_count, dtype=jnp.int32)
    reach = (parent_ids[..., :, None] == positions).astype(F32)
    reach = reach + (positions[:, None] == positions[None, :]).astype(F32)
    for _ in range(max(1, (tree_count - 1).bit_length())):
        product = jnp.einsum("...ij,...jk->...ik", reach, reach, preferred_element_type=F32)
        reach = jnp.minimum(reach + product, 1.0)
    return reach > 0.5


def spread(value, axes, count):
    return lax.all_to_all(jnp.broadcast_to(value[None], (count,) + value.shape), axes, 0, 0)


def split3(value):
    high = value.astype(BF)
    rest = value - high.astype(F32)
    mid = rest.astype(BF)
    return high, mid, (rest - mid.astype(F32)).astype(BF)


def attend_kernel(place, qn, qr, keys, bias, mine, twin, out, kv, lat, sems):
    z, c = place[0], place[1]
    nz, shard = mine.shape[0], mine.shape[1]
    copies = []
    for i in range(nz):
        for k, (source, part) in enumerate(((mine, c), (twin, 1 - c))):
            row = pl.multiple_of(lax.rem(z + i, nz) * (2 * shard) + part * shard, 16)
            copies.append(pltpu.make_async_copy(source.at[i], kv.at[pl.ds(row, shard)], sems.at[k * nz + i]))
    for copy in copies:
        copy.start()
    for copy in copies:
        copy.wait()
    for h in range(HEADS):
        part = jnp.dot(qn[h], kv[NOPE * h : NOPE * (h + 1), :KVR], preferred_element_type=F32).astype(BF)
        lat[0, TREE * h : TREE * (h + 1)] = part[:TREE]
        lat[1, TREE * h : TREE * (h + 1)] = part[TREE:]
    lanes = lax.broadcasted_iota(jnp.int32, (TREE, 128), 1)
    logs = jnp.zeros((TREE, 128), F32)
    group = 8
    size = group * TREE
    over_last = (((1,), (1,)), ((), ()))
    for g in range(2):
        for i in range(HEADS // group):
            rows = slice(size * i, size * (i + 1))
            scores = lax.dot_general(lat[g, rows], keys[g, :, :KVR], over_last, preferred_element_type=F32)
            scores += lax.dot_general(qr[g, rows], keys[g, :, KVR:], over_last, preferred_element_type=F32)
            scores = scores * (NOPE + ROPE) ** -0.5
            scores = (scores.reshape(group, TREE, -1) + bias[g][None]).reshape(size, -1)
            top = jnp.max(scores, axis=-1, keepdims=True)
            weights = jnp.exp(scores - top)
            total = jnp.sum(weights, axis=-1, keepdims=True)
            acc = jnp.dot(weights.astype(BF), keys[g, :, :KVR], preferred_element_type=F32)
            lat[g, rows] = (acc / total).astype(BF)
            if g == 1:
                column = top + jnp.log(total)
                for k in range(group):
                    logs = jnp.where(lanes == group * i + k, column[TREE * k : TREE * (k + 1)], logs)
    count = out.shape[0]
    for j in range(HEADS // 4):
        quad = []
        for h in range(4 * j, 4 * j + 4):
            both = jnp.concatenate([lat[g, TREE * h : TREE * (h + 1)] for g in range(2)], axis=0)
            rows = kv[VDIM * h : VDIM * (h + 1), KVR:]
            quad.append(lax.dot_general(both, rows, over_last, preferred_element_type=F32))
        heads = jnp.concatenate(quad, axis=1).astype(BF)
        for d in range(count):
            out[d, 2 * TREE * j : 2 * TREE * (j + 1)] = heads
    high, mid, low = split3(logs)
    base = 2 * TREE * (HEADS // 4)
    for d in range(count):
        out[d, base : base + TREE, :128] = high
        out[d, base : base + TREE, 128:] = mid
        out[d, base + TREE : base + 2 * TREE, :128] = low
        out[d, base + TREE : base + 2 * TREE, 128:] = low


def read_logs(parts, base):
    high = parts[:, base : base + TREE, :128].astype(F32)
    mid = parts[:, base : base + TREE, 128:].astype(F32)
    return high + mid + parts[:, base + TREE : base + 2 * TREE, :128].astype(F32)


def join_pieces(parts, base, pick):
    logs = read_logs(parts, base)
    count = logs.shape[0]
    top = jnp.max(logs, axis=0)
    share = jnp.exp(logs - top[None])
    total = jnp.sum(share, axis=0)
    share = (share / total[None]).reshape(count * TREE, 128)
    high = share.astype(BF)
    low = (share - high.astype(F32)).astype(BF)
    joined = []
    for j in range(HEADS // 4):
        owner = lax.broadcasted_iota(jnp.int32, (128, 256), 1) // VDIM + 4 * j
        select = jnp.where(lax.broadcasted_iota(jnp.int32, (128, 256), 0) == owner, 1.0, 0.0).astype(BF)
        wide = jnp.dot(high, select, preferred_element_type=F32) + jnp.dot(low, select, preferred_element_type=F32)
        piece = pick(j).astype(F32) * wide.reshape(count, TREE, 256)
        joined.append(jnp.sum(piece, axis=0).astype(BF))
    return joined, top + jnp.log(total)


def project(rows, weight):
    span = HEADS * VDIM // 4
    lanes = lax.broadcasted_iota(jnp.int32, (rows.shape[0], 128), 1) // 32
    tail = weight[16:20].reshape(span, 128)
    main = jnp.zeros((rows.shape[0], 128), F32)
    rest = jnp.zeros((rows.shape[0], 128), F32)
    for g in range(4):
        left = rows[:, span * g : span * (g + 1)]
        block = weight[4 * g : 4 * (g + 1)].reshape(span, 128)
        main += jnp.dot(left, block, preferred_element_type=F32)
        rest += jnp.where(lanes == g, jnp.dot(left, tail, preferred_element_type=F32), 0.0)
    rest = rest + pltpu.roll(rest, 64, 1)
    return main, rest + pltpu.roll(rest, 32, 1)


def project_kernel(place, got, *refs):
    owns, twins, (send, weight, rows, sems) = refs[:4], refs[4:8], refs[8:]
    c, x = place[1], place[2]
    copies = []
    for k in range(4):
        copies.append(pltpu.make_async_copy(owns[k], weight.at[k, :, c], sems.at[k]))
        copies.append(pltpu.make_async_copy(twins[k], weight.at[k, :, 1 - c], sems.at[4 + k]))
    for copy in copies:
        copy.start()
    chunks = HEADS // 4
    for j in range(chunks):
        rows[:, 256 * j : 256 * (j + 1)] = got[:, 2 * TREE * j : 2 * TREE * j + TREE].reshape(4 * TREE, 256)
    base = 2 * TREE * chunks
    joined, logs = join_pieces(got, base, lambda j: got[:, 2 * TREE * j + TREE : 2 * TREE * (j + 1)])
    high, mid, low = split3(logs)
    first = 4 * TREE
    last = first + TREE * chunks
    for d in range(4):
        for j in range(chunks):
            send[d, first + TREE * j : first + TREE * (j + 1)] = joined[j]
        send[d, last : last + TREE, :128] = high
        send[d, last : last + TREE, 128:] = mid
        send[d, last + TREE :, :128] = low
        send[d, last + TREE :, 128:] = low
    for copy in copies:
        copy.wait()
    for k in range(4):
        main, rest = project(rows[...], weight[k])
        target = lax.rem(x + k, 4)
        send[target, :first, :128] = main.astype(BF)
        send[target, :first, 128:] = rest.astype(BF)


def finish_kernel(place, got, own, twin, residual, long_residual, hidden, long_hidden, weight, rows, sems):
    c = place[1]
    copies = [
        pltpu.make_async_copy(own, weight.at[:, c], sems.at[0]),
        pltpu.make_async_copy(twin, weight.at[:, 1 - c], sems.at[1]),
    ]
    for copy in copies:
        copy.start()
    for y in range(4):
        for x in range(4):
            piece = got[x, TREE * y : TREE * (y + 1)]
            for part in (slice(0, 128), slice(128, 160)):
                total = residual[4 * y + x, :, part].astype(F32) + piece[:, part].astype(F32)
                hidden[4 * y + x, :, part] = total.astype(BF)
    first = 4 * TREE
    chunks = HEADS // 4
    joined, _ = join_pieces(got, first + TREE * chunks, lambda j: got[:, first + TREE * j : first + TREE * (j + 1)])
    for j in range(chunks):
        rows[:, 256 * j : 256 * (j + 1)] = joined[j]
    for copy in copies:
        copy.wait()
    main, rest = project(rows[...], weight[...])
    long_hidden[0, :, :128] = (long_residual[0, :, :128].astype(F32) + main).astype(BF)
    long_hidden[0, :, 128:160] = (long_residual[0, :, 128:160].astype(F32) + rest[:, :32]).astype(BF)


SMEM = pl.BlockSpec(memory_space=pltpu.SMEM)
VMEM = pl.BlockSpec(memory_space=pltpu.VMEM)
ANY = pl.BlockSpec(memory_space=pl.ANY)
PARAMS = pltpu.CompilerParams(vmem_limit_bytes=48 << 20)


def on_device(
    queries, tree_latent, parents, cache, cache_lengths, accepted, residual,
    long_queries, long_tree_latent, long_parents, long_cache, long_plan, long_residual,
    key_up, value_up, out_weight,
):
    ny, nx, nz = lax.axis_size("y"), lax.axis_size("x"), lax.axis_size("z")
    nr = ny * nx
    x, z, c = lax.axis_index("x"), lax.axis_index("z"), lax.axis_index("c")
    r = lax.axis_index(ROWS)
    place = jnp.stack([z, c, x]).astype(jnp.int32)
    kv = jnp.concatenate([key_up, value_up], axis=1)
    pairs = [(i * nz + (j + i) % nz, i * nz + j) for i in range(nr) for j in range(nz)]
    kv = lax.ppermute(kv, ("y", "x", "z"), pairs)
    mine = spread(kv, ROWS, nr)
    twin = lax.ppermute(mine, "c", SWAP)
    held, step = out_weight[None], nz // 2
    while step:
        more = lax.ppermute(held, "z", [((j + step) % nz, j) for j in range(nz)])
        held = jnp.stack([held, more], axis=1).reshape((-1,) + out_weight.shape)
        step //= 2
    held = jnp.roll(held, z, axis=0)
    shard = out_weight.shape[0]
    tail = held[:, :, 128:].reshape(4, 4 * shard, 32).transpose(1, 0, 2).reshape(4, shard, 128)
    held = jnp.concatenate([held[:, :, :128], tail], axis=0)
    owns = [held] + [lax.ppermute(held, "x", [((j + k) % nx, j) for j in range(nx)]) for k in range(1, nx)]
    twins = [lax.ppermute(block, "c", SWAP) for block in owns]

    per_head = jnp.concatenate([queries[0], long_queries[0]], axis=0).reshape(2 * TREE, HEADS, NOPE + ROPE)
    per_head = per_head.transpose(1, 0, 2)
    rope = per_head[..., NOPE:].reshape(HEADS, 2, TREE, ROPE).transpose(1, 0, 2, 3)
    rope = rope.reshape(2, HEADS * TREE, ROPE)
    keys = jnp.stack([
        jnp.concatenate([cache[0, 0], tree_latent[0]], axis=0),
        jnp.concatenate([long_cache[0], long_tree_latent[0]], axis=0),
    ])
    slots = cache.shape[2]
    lengths = jnp.stack([cache_lengths[0, 0], long_plan[0, 0]])
    cache_ok = jnp.arange(slots, dtype=jnp.int32)[None, None, :] < lengths[:, None, None]
    reach = tree_reach(jnp.concatenate([parents[0], long_parents], axis=0))
    reach = reach & ((jnp.arange(2) == 0) | (r == 0))[:, None, None]
    allowed = jnp.concatenate([jnp.broadcast_to(cache_ok, (2, TREE, slots)), reach], axis=2)
    bias = jnp.where(allowed, 0.0, -jnp.inf).astype(F32)

    chunks = HEADS // 4
    heads = pl.pallas_call(
        attend_kernel,
        out_shape=jax.ShapeDtypeStruct((ny, 2 * TREE * (chunks + 1), 256), BF),
        in_specs=[SMEM, VMEM, VMEM, VMEM, VMEM, ANY, ANY],
        out_specs=VMEM,
        scratch_shapes=[
            pltpu.VMEM((HEADS * NOPE, 2 * KVR), BF),
            pltpu.VMEM((2, HEADS * TREE, KVR), BF),
            pltpu.SemaphoreType.DMA((2 * nz,)),
        ],
        compiler_params=PARAMS,
    )(place, per_head[..., :NOPE], rope, keys, bias, mine, twin)
    got = lax.all_to_all(heads, "y", 0, 0)
    send = pl.pallas_call(
        project_kernel,
        out_shape=jax.ShapeDtypeStruct((nx, (ny + chunks + 2) * TREE, 256), BF),
        in_specs=[SMEM, VMEM] + [ANY] * 8,
        out_specs=VMEM,
        scratch_shapes=[
            pltpu.VMEM((nx, 20, 2, shard, 128), BF),
            pltpu.VMEM((ny * TREE, HEADS * VDIM), BF),
            pltpu.SemaphoreType.DMA((8,)),
        ],
        compiler_params=PARAMS,
    )(place, got, *owns, *twins)
    back = lax.all_to_all(send, "x", 0, 0)
    hidden, long_hidden = pl.pallas_call(
        finish_kernel,
        out_shape=(
            jax.ShapeDtypeStruct(residual.shape, BF),
            jax.ShapeDtypeStruct(long_residual.shape, BF),
        ),
        in_specs=[SMEM, VMEM, ANY, ANY, VMEM, VMEM],
        out_specs=(VMEM, VMEM),
        scratch_shapes=[
            pltpu.VMEM((20, 2, shard, 128), BF),
            pltpu.VMEM((TREE, HEADS * VDIM), BF),
            pltpu.SemaphoreType.DMA((2,)),
        ],
        compiler_params=PARAMS,
    )(place, back, owns[0], twins[0], residual, long_residual)
    accepted_cache = jnp.take_along_axis(tree_latent[0], accepted[0, 0][:, None], axis=0)[None, None]
    return hidden, accepted_cache, long_hidden


def solution(mesh):
    split = Mesh(mesh.devices.reshape(4, 4, 16, 2), ("y", "x", "z", "c"))
    return jax.shard_map(
        on_device,
        mesh=split,
        in_specs=(
            P(ROWS, COLS, None),
            P(ROWS, COLS, None),
            P(ROWS, COLS, None),
            P(ROWS, COLS, None, None),
            P(ROWS, COLS),
            P(ROWS, COLS, None),
            P(None, COLS, ROWS),
            P(COLS, None, None),
            P(COLS, None, None),
            P(COLS, None),
            P(COLS, ROWS, None),
            P(COLS, ROWS),
            P(COLS, None, ROWS),
            P(COLS, None),
            P(COLS, None),
            P(COLS, ROWS),
        ),
        out_specs=(P(None, COLS, ROWS), P(ROWS, COLS, None, None), P(COLS, None, ROWS)),
        check_vma=False,
    )
```

time: 439 us -> 169 us (0.38)
  waiting for transfers between devices: 267 us -> 52.2 us
  starting transfers between devices: 0.16 us -> 83.1 us
  blocking collectives: 70.5 us -> 0 us
  other arithmetic: 40.8 us -> 3.63 us
  matrix products: 16.7 us -> 0.71 us
  Pallas kernels: 0 us -> 15.6 us
  local copies, waits for them, and re-layouts: 24.8 us -> 9.79 us
  between operations: 15.5 us -> 2.51 us
    all_gather x4 -> x0, waiting for transfers between devices: 265 us -> none  [the longest x1 124 us: combined_all(): pieces = jax.tree.map(lambda part: lax.all_gather(part, axis), value)]
    all_gather x3 -> x0, blocking collectives: 70.5 us -> none  [the longest x2 37.5 us: combined_all(): pieces = jax.tree.map(lambda part: lax.all_gather(part, axis), value)]
    ppermute x0 -> x13, starting transfers between devices: none -> 57.6 us  [the longest x4 30.3 us: on_device(): more = lax.ppermute(held, 'z', [((j + step) % nz, j) for j in range(nz)])]
    add x32 -> x0, other arithmetic: 38.1 us -> none  [the longest x15 26.6 us: combine_parts(): earlier[2] * early_factor[..., None] + later[2] * late_factor[..., None]]
    all_to_all x0 -> x3, waiting for transfers between devices: none -> 31.5 us  [the longest x1 17.7 us: spread(): lax.all_to_all(jnp.broadcast_to(value[None], (count,) + value.shape), axe...]
    all_to_all x0 -> x3, starting transfers between devices: none -> 25.5 us  [the longest x1 18.3 us: spread(): lax.all_to_all(jnp.broadcast_to(value[None], (count,) + value.shape), axe...]
    ppermute x0 -> x13, waiting for transfers between devices: none -> 20.7 us  [the longest x4 14.3 us: on_device(): more = lax.ppermute(held, 'z', [((j + step) % nz, j) for j in range(nz)])]
    slice x11 -> x3, local copies, waits for them, and re-layouts: 18.1 us -> 0.37 us  [the longest x1 0.25 us: on_device(): per_head[..., NOPE:].reshape(HEADS, 2, TREE, ROPE).transpose(1, 0, 2, 3)]
  transfers between devices with their start and end apart: 4 -> 16, of which waited for: 3 -> 6; matrix products, arithmetic and copies ran while one was open for 4% -> 5% of each run, Pallas kernels for 0% -> 6%
where the time goes in v1:
time: 169 us; the launch traced here: 168 us
  starting transfers between devices  83.1 us (49%)
  waiting for transfers between devices  52.2 us (31%)
  Pallas kernels  15.6 us (9%)
  local copies, waits for them, and re-layouts  9.79 us (6%)
  other arithmetic  3.63 us (2%)
  between operations  2.51 us (1%)
    ppermute x4, starting transfers between devices, on_device(): more = lax.ppermute(held, 'z', [((j + step) % nz, j) for j in range(nz)])  30.3 us
    all_to_all x1, starting transfers between devices, spread(): lax.all_to_all(jnp.broadcast_to(value[None], (count,) + value.shape), axe...  18.3 us
    all_to_all x1, waiting for transfers between devices, spread(): lax.all_to_all(jnp.broadcast_to(value[None], (count,) + value.shape), axe...  17.7 us
    ppermute x4, waiting for transfers between devices, on_device(): more = lax.ppermute(held, 'z', [((j + step) % nz, j) for j in range(nz)])  14.3 us
    ppermute x4, starting transfers between devices, on_device(): twins = [lax.ppermute(block, 'c', SWAP) for block in owns]  14.2 us
    all_to_all x1, waiting for transfers between devices, on_device(): back = lax.all_to_all(send, 'x', 0, 0)  13.7 us
    pallas_call x1, Pallas kernels, on_device(): pl.pallas_call(attend_kernel, out_shape=jax.ShapeDtypeStruct((ny, 2 * TRE...  9.26 us
    ppermute x3, starting transfers between devices, on_device(): lax.ppermute(held, 'x', [((j + k) % nx, j) for j in range(nx)])  7.2 us
  transfers between devices with their start and end apart: 16, of which 6 were waited for; matrix products, arithmetic and copies ran while one was open for 5% of the time, Pallas kernels for 6%

profile of v1, /device:TPU:1, one launch (start us, length us, event | category | flops | bytes accessed | tf_op | source)
XLA Modules:
  0.0 167.6 jit_solution(1265008391933467469)
XLA Ops:
  0.6 0.8 pad_maximum_fusion.5
  1.4 0.7 collective-permute-start
  2.1 16.3 %collective-permute-start.2 = (bf16[1,80,160]{2,1,0:T(8,128)(2,1)}, bf16[1,80,160]{2,1,0:T(8,128)(2,1)S(1)}, u32[]{:S(2)}, u32[]{:S(2)}) collective-permute-start(bf16[1,80,160]{2,1,0:T(8,128)(2,1)} %bitcast.76), channel_id=1, source_target_pairs={{16,0},{18,2},{20,4},{22,6},{24,8},{26,10},{28,12},{30,14},{0,16},... | collective-permute-start | bytes 76808 | tf_op jit(solution)/shard_map/ppermute | solution.py:221
  19.7 1.2 broadcast_in_dim.42
  20.9 18.3 %all-to-all-start = ((bf16[16,80,512]{2,1,0:T(8,128)(2,1)}), bf16[16,80,512]{2,1,0:T(8,128)(2,1)S(1)}, u32[]{:S(2)}, u32[]{:S(2)}) async-start(bf16[16,80,512]{2,1,0:T(8,128)(2,1)} %broadcast_in_dim.42), calls=%async_computation | async-start | bytes 2621440 | tf_op jit(solution)/shard_map/all_to_all | solution.py:33
  39.4 0.2 fusion
  39.8 0.1 fusion.3
  39.9 17.7 %all-to-all-done.mine = bf16[16,80,512]{2,1,0:T(8,128)(2,1)S(1)} async-done(((bf16[16,80,512]{2,1,0:T(8,128)(2,1)}), bf16[16,80,512]{2,1,0:T(8,128)(2,1)S(1)}, u32[]{:S(2)}, u32[]{:S(2)}) %all-to-all-start) | async-done | bytes 1310752 | tf_op jit(solution)/shard_map/all_to_all | solution.py:33
  57.7 5.2 %collective-permute-start.1 = (bf16[16,80,512]{2,1,0:T(8,128)(2,1)S(1)}, bf16[16,80,512]{2,1,0:T(8,128)(2,1)}, u32[]{:S(2)}, u32[]{:S(2)}) collective-permute-start(bf16[16,80,512]{2,1,0:T(8,128)(2,1)S(1)} %all-to-all-done.mine), channel_id=1, source_target_pairs={{0,1},{1,0},{2,3},{3,2},{4,5},{5,4},{6,7},{7,6},{8,9},{9,8},{10,11... | collective-permute-start | bytes 3932168 | tf_op jit(solution)/shard_map/ppermute | solution.py:218
  62.9 0.5 concatenate.31
  63.5 0.5 concatenate.30
  64.2 0.1 fusion.6
  64.3 0.2 maximum_bitcast_fusion
  64.5 0.2 copy.34
  64.7 0.3 copy-done.12
  65.0 0.2 copy.35
  65.2 4.0 %collective-permute-start.3 = (bf16[2,80,160]{2,1,0:T(8,128)(2,1)S(1)}, bf16[2,80,160]{2,1,0:T(8,128)(2,1)S(1)}, u32[]{:S(2)}, u32[]{:S(2)}) collective-permute-start(bf16[2,80,160]{2,1,0:T(8,128)(2,1)S(1)} %get-tuple-element.8), channel_id=1, source_target_pairs={{8,0},{10,2},{12,4},{14,6},{16,8},{18,10},{20,12},{22,14},{24,16},... | collective-permute-start | bytes 153608 | tf_op jit(solution)/shard_map/ppermute | solution.py:221
  69.4 0.3 slice.19
  69.7 7.8 %collective-permute-done.3 = bf16[2,80,160]{2,1,0:T(8,128)(2,1)S(1)} collective-permute-done((bf16[2,80,160]{2,1,0:T(8,128)(2,1)S(1)}, bf16[2,80,160]{2,1,0:T(8,128)(2,1)S(1)}, u32[]{:S(2)}, u32[]{:S(2)}) %collective-permute-start.3) | collective-permute-done | bytes 51232 | tf_op jit(solution)/shard_map/ppermute | solution.py:221
  77.5 3.8 %collective-permute-start.4 = (bf16[4,80,160]{2,1,0:T(8,128)(2,1)S(1)}, bf16[4,80,160]{2,1,0:T(8,128)(2,1)S(1)}, u32[]{:S(2)}, u32[]{:S(2)}) collective-permute-start(bf16[4,80,160]{2,1,0:T(8,128)(2,1)S(1)} %bitcast.69), channel_id=1, source_target_pairs={{4,0},{6,2},{8,4},{10,6},{12,8},{14,10},{16,12},{18,14},{20,16},{2... | collective-permute-start | bytes 307208 | tf_op jit(solution)/shard_map/ppermute | solution.py:221
  81.4 6.5 %collective-permute-done.4 = bf16[4,80,160]{2,1,0:T(8,128)(2,1)S(1)} collective-permute-done((bf16[4,80,160]{2,1,0:T(8,128)(2,1)S(1)}, bf16[4,80,160]{2,1,0:T(8,128)(2,1)S(1)}, u32[]{:S(2)}, u32[]{:S(2)}) %collective-permute-start.4) | collective-permute-done | bytes 102432 | tf_op jit(solution)/shard_map/ppermute | solution.py:221
  88.0 6.2 %collective-permute-start.5 = (bf16[8,80,160]{2,1,0:T(8,128)(2,1)S(1)}, bf16[8,80,160]{2,1,0:T(8,128)(2,1)}, u32[]{:S(2)}, u32[]{:S(2)}) collective-permute-start(bf16[8,80,160]{2,1,0:T(8,128)(2,1)S(1)} %bitcast.64), channel_id=1, source_target_pairs={{2,0},{4,2},{6,4},{8,6},{10,8},{12,10},{14,12},{16,14},{18,16},{20... | collective-permute-start | bytes 614408 | tf_op jit(solution)/shard_map/ppermute | solution.py:221
  94.4 9.3 %shard_map.175 = bf16[4,704,256]{2,1,0:T(8,128)(2,1)} custom-call(s32[3]{0:T(128)S(1)} %pad_add_fusion.1.place, bf16[40,64,64]{2,1,0:T(8,128)(2,1)S(1)} %bitcast.60, bf16[2,1280,32]{2,1,0:T(8,128)(2,1)S(1)} %bitcast.61, bf16[2,288,288]{2,1,0:T(8,128)(2,1)S(1)} %pad_maximum_fusion.1.keys, f32[2,32,288]{2,1,0:T(8,128)S(1)} %add_select_fusion.bias, ...), custom_call_target="tpu_custom_call" | custom-call | tf_op jit(solution)/shard_map/pallas_call | solution.py:248
  103.6 3.6 %all-to-all-start.1 = ((bf16[4,704,256]{2,1,0:T(8,128)(2,1)}), bf16[4,704,256]{2,1,0:T(8,128)(2,1)S(1)}, u32[]{:S(2)}, u32[]{:S(2)}) async-start(bf16[4,704,256]{2,1,0:T(8,128)(2,1)} %shard_map.175), calls=%async_computation.1 | async-start | bytes 2883584 | tf_op jit(solution)/shard_map/all_to_all | solution.py:260
  107.2 1.1 pad_maximum_fusion
  108.4 0.3 fusion.7
  108.8 0.2 copy.40
  109.3 1.9 %collective-permute-start.6 = (bf16[20,80,128]{2,1,0:T(8,128)(2,1)S(1)}, bf16[20,80,128]{2,1,0:T(8,128)(2,1)S(1)}, u32[]{:S(2)}, u32[]{:S(2)}) collective-permute-start(bf16[20,80,128]{2,1,0:T(8,128)(2,1)S(1)} %pad_maximum_fusion.2.refs_0_.own), channel_id=1, source_target_pairs={{32,0},{64,32},{96,64},{0,96},{33,1},{65,33},{97,65},{1,97},{34,2}... | collective-permute-start | bytes 1228808 | tf_op jit(solution)/shard_map/ppermute | solution.py:228
  111.2 3.0 %collective-permute-start.7 = (bf16[20,80,128]{2,1,0:T(8,128)(2,1)S(1)}, bf16[20,80,128]{2,1,0:T(8,128)(2,1)S(1)}, u32[]{:S(2)}, u32[]{:S(2)}) collective-permute-start(bf16[20,80,128]{2,1,0:T(8,128)(2,1)S(1)} %pad_maximum_fusion.2.refs_0_.own), channel_id=1, source_target_pairs={{64,0},{96,32},{0,64},{32,96},{65,1},{97,33},{1,65},{33,97},{66,2}... | collective-permute-start | bytes 1228808 | tf_op jit(solution)/shard_map/ppermute | solution.py:228
  114.3 2.2 %collective-permute-start.8 = (bf16[20,80,128]{2,1,0:T(8,128)(2,1)S(1)}, bf16[20,80,128]{2,1,0:T(8,128)(2,1)S(1)}, u32[]{:S(2)}, u32[]{:S(2)}) collective-permute-start(bf16[20,80,128]{2,1,0:T(8,128)(2,1)S(1)} %pad_maximum_fusion.2.refs_0_.own), channel_id=1, source_target_pairs={{96,0},{0,32},{32,64},{64,96},{97,1},{1,33},{33,65},{65,97},{98,2}... | collective-permute-start | bytes 1228808 | tf_op jit(solution)/shard_map/ppermute | solution.py:228
  116.5 3.3 %collective-permute-start.9 = (bf16[20,80,128]{2,1,0:T(8,128)(2,1)S(1)}, bf16[20,80,128]{2,1,0:T(8,128)(2,1)S(1)}, u32[]{:S(2)}, u32[]{:S(2)}) collective-permute-start(bf16[20,80,128]{2,1,0:T(8,128)(2,1)S(1)} %pad_maximum_fusion.2.refs_0_.own), channel_id=1, source_target_pairs={{0,1},{1,0},{2,3},{3,2},{4,5},{5,4},{6,7},{7,6},{8,9},{9,8},{10,11... | collective-permute-start | bytes 1228808 | tf_op jit(solution)/shard_map/ppermute | solution.py:229
  119.9 1.4 collective-permute-done.6.refs_1_
  121.3 5.0 %collective-permute-start.10 = (bf16[20,80,128]{2,1,0:T(8,128)(2,1)S(1)}, bf16[20,80,128]{2,1,0:T(8,128)(2,1)S(1)}, u32[]{:S(2)}, u32[]{:S(2)}) collective-permute-start(bf16[20,80,128]{2,1,0:T(8,128)(2,1)S(1)} %collective-permute-done.6.refs_1_), channel_id=1, source_target_pairs={{0,1},{1,0},{2,3},{3,2},{4,5},{5,4},{6,7},{7,6},{8,9},{9,8},{10,11... | collective-permute-start | bytes 1228808 | tf_op jit(solution)/shard_map/ppermute | solution.py:229
  126.3 3.5 %collective-permute-start.11 = (bf16[20,80,128]{2,1,0:T(8,128)(2,1)S(1)}, bf16[20,80,128]{2,1,0:T(8,128)(2,1)S(1)}, u32[]{:S(2)}, u32[]{:S(2)}) collective-permute-start(bf16[20,80,128]{2,1,0:T(8,128)(2,1)S(1)} %collective-permute-done.7.refs_2_), channel_id=1, source_target_pairs={{0,1},{1,0},{2,3},{3,2},{4,5},{5,4},{6,7},{7,6},{8,9},{9,8},{10,11... | collective-permute-start | bytes 1228808 | tf_op jit(solution)/shard_map/ppermute | solution.py:229
  129.8 5.0 %collective-permute-done.8.refs_3_ = bf16[20,80,128]{2,1,0:T(8,128)(2,1)S(1)} collective-permute-done((bf16[20,80,128]{2,1,0:T(8,128)(2,1)S(1)}, bf16[20,80,128]{2,1,0:T(8,128)(2,1)S(1)}, u32[]{:S(2)}, u32[]{:S(2)}) %collective-permute-start.8) | collective-permute-done | bytes 409632 | tf_op jit(solution)/shard_map/ppermute | solution.py:228
  134.8 2.4 %collective-permute-start.12 = (bf16[20,80,128]{2,1,0:T(8,128)(2,1)S(1)}, bf16[20,80,128]{2,1,0:T(8,128)(2,1)S(1)}, u32[]{:S(2)}, u32[]{:S(2)}) collective-permute-start(bf16[20,80,128]{2,1,0:T(8,128)(2,1)S(1)} %collective-permute-done.8.refs_3_), channel_id=1, source_target_pairs={{0,1},{1,0},{2,3},{3,2},{4,5},{5,4},{6,7},{7,6},{8,9},{9,8},{10,11... | collective-permute-start | bytes 1228808 | tf_op jit(solution)/shard_map/ppermute | solution.py:229
  137.2 0.8 copy-done
  138.0 0.8 copy-done.2
  138.7 0.8 copy-done.4
  139.5 1.0 copy-done.1
  140.5 1.0 copy-done.3
  141.5 1.0 copy-done.5
  142.5 4.1 %shard_map.176 = bf16[4,512,256]{2,1,0:T(8,128)(2,1)} custom-call(s32[3]{0:T(128)S(1)} %pad_add_fusion.1.place, bf16[4,704,256]{2,1,0:T(8,128)(2,1)S(1)} %all-to-all-done.1.got, bf16[20,80,128]{2,1,0:T(8,128)(2,1)S(1)} %pad_maximum_fusion.2.refs_0_.own, bf16[20,80,128]{2,1,0:T(8,128)(2,1)S(1)} %collective-permute-done.6.refs_1_, ...), custom_call_target="tpu_custom_call" | custom-call | tf_op jit(solution)/shard_map/pallas_call | solution.py:261
  146.6 3.7 %all-to-all-start.2 = ((bf16[4,512,256]{2,1,0:T(8,128)(2,1)}), bf16[4,512,256]{2,1,0:T(8,128)(2,1)S(1)}, u32[]{:S(2)}, u32[]{:S(2)}) async-start(bf16[4,512,256]{2,1,0:T(8,128)(2,1)} %shard_map.176), calls=%async_computation.2 | async-start | bytes 2097152 | tf_op jit(solution)/shard_map/all_to_all | solution.py:273
  150.3 0.6 gather_fusion
  150.9 0.7 bitcast_select_fusion
  151.6 13.7 %all-to-all-done.2.got = bf16[4,512,256]{2,1,0:T(8,128)(2,1)S(1)} async-done(((bf16[4,512,256]{2,1,0:T(8,128)(2,1)}), bf16[4,512,256]{2,1,0:T(8,128)(2,1)S(1)}, u32[]{:S(2)}, u32[]{:S(2)}) %all-to-all-start.2) | async-done | bytes 1048608 | tf_op jit(solution)/shard_map/all_to_all | solution.py:273
  165.3 2.3 %shard_map.177 = (bf16[16,32,160]{2,1,0:T(8,128)(2,1)}, bf16[1,32,160]{2,1,0:T(8,128)(2,1)}) custom-call(s32[3]{0:T(128)S(1)} %pad_add_fusion.1.place, bf16[4,512,256]{2,1,0:T(8,128)(2,1)S(1)} %all-to-all-done.2.got, bf16[20,80,128]{2,1,0:T(8,128)(2,1)S(1)} %pad_maximum_fusion.2.refs_0_.own, bf16[20,80,128]{2,1,0:T(8,128)(2,1)S(1)} %collective-permute-done.9.refs_4_.twin, ...), custom_call_target="tpu_custom_call" | custom-call | tf_op jit(solution)/shard_map/pallas_call | solution.py:274
  (67 shorter events, 1.5 us)
Async XLA Ops:
  1.4 18.2 %collective-permute-start = (bf16[80,512]{1,0:T(8,128)(2,1)S(1)}, bf16[80,512]{1,0:T(8,128)(2,1)S(1)}, u32[]{:S(2)}, u32[]{:S(2)}) collective-permute-start(bf16[80,512]{1,0:T(8,128)(2,1)S(1)} %pad_maximum_fusion.5), channel_id=1, source_target_pairs={{0,0},{2,2},{4,4},{6,6},{8,8},{10,10},{12,12},{14,14},{16,16},{18,... | collective-permute-start | bytes 245768 | tf_op jit(solution)/shard_map/ppermute | solution.py:216
  2.1 63.1 %collective-permute-start.2 = (bf16[1,80,160]{2,1,0:T(8,128)(2,1)}, bf16[1,80,160]{2,1,0:T(8,128)(2,1)S(1)}, u32[]{:S(2)}, u32[]{:S(2)}) collective-permute-start(bf16[1,80,160]{2,1,0:T(8,128)(2,1)} %bitcast.76), channel_id=1, source_target_pairs={{16,0},{18,2},{20,4},{22,6},{24,8},{26,10},{28,12},{30,14},{0,16},... | collective-permute-start | bytes 76808 | tf_op jit(solution)/shard_map/ppermute | solution.py:221
  20.9 18.4 %copy-start.15 = (s32[1,32]{1,0:T(1,128)S(1)}, s32[1,32]{1,0:T(1,128)}, u32[]{:S(2)}) copy-start(s32[1,32]{1,0:T(1,128)} %param.25) | copy-start | bytes 388
  20.9 18.4 %copy-start.16 = (s32[1,1,32]{2,1,0:T(1,128)S(1)}, s32[1,1,32]{2,1,0:T(1,128)}, u32[]{:S(2)}) copy-start(s32[1,1,32]{2,1,0:T(1,128)} %param.18) | copy-start | bytes 388
  20.9 42.0 %copy-start.8 = (bf16[1,32,3840]{2,1,0:T(8,128)(2,1)S(1)}, bf16[1,32,3840]{2,1,0:T(8,128)(2,1)}, u32[]{:S(2)}) copy-start(bf16[1,32,3840]{2,1,0:T(8,128)(2,1)} %param.23) | copy-start | bytes 737284
  20.9 36.8 %all-to-all-start = ((bf16[16,80,512]{2,1,0:T(8,128)(2,1)}), bf16[16,80,512]{2,1,0:T(8,128)(2,1)S(1)}, u32[]{:S(2)}, u32[]{:S(2)}) async-start(bf16[16,80,512]{2,1,0:T(8,128)(2,1)} %broadcast_in_dim.42), calls=%async_computation | async-start | bytes 2621440 | tf_op jit(solution)/shard_map/all_to_all | solution.py:33
  39.2 24.3 %copy-start.9 = (bf16[1,32,3840]{2,1,0:T(8,128)(2,1)S(1)}, bf16[1,32,3840]{2,1,0:T(8,128)(2,1)}, u32[]{:S(2)}) copy-start(bf16[1,32,3840]{2,1,0:T(8,128)(2,1)} %param.16) | copy-start | bytes 737284
  57.7 36.7 %collective-permute-start.1 = (bf16[16,80,512]{2,1,0:T(8,128)(2,1)S(1)}, bf16[16,80,512]{2,1,0:T(8,128)(2,1)}, u32[]{:S(2)}, u32[]{:S(2)}) collective-permute-start(bf16[16,80,512]{2,1,0:T(8,128)(2,1)S(1)} %all-to-all-done.mine), channel_id=1, source_target_pairs={{0,1},{1,0},{2,3},{3,2},{4,5},{5,4},{6,7},{7,6},{8,9},{9,8},{10,11... | collective-permute-start | bytes 3932168 | tf_op jit(solution)/shard_map/ppermute | solution.py:218
  63.5 1.0 copy-start.11
  64.1 0.9 copy-start.12
  64.1 1.1 copy-start.13
  64.2 5.1 %copy-start.10 = (bf16[1,32,288]{2,1,0:T(8,128)(2,1)S(1)}, bf16[1,32,288]{2,1,0:T(8,128)(2,1)}, u32[]{:S(2)}) copy-start(bf16[1,32,288]{2,1,0:T(8,128)(2,1)} %param.17) | copy-start | bytes 55300
  64.2 5.1 %copy-start.14 = (bf16[1,32,288]{2,1,0:T(8,128)(2,1)S(1)}, bf16[1,32,288]{2,1,0:T(8,128)(2,1)}, u32[]{:S(2)}) copy-start(bf16[1,32,288]{2,1,0:T(8,128)(2,1)} %param.24) | copy-start | bytes 55300
  65.2 12.3 %collective-permute-start.3 = (bf16[2,80,160]{2,1,0:T(8,128)(2,1)S(1)}, bf16[2,80,160]{2,1,0:T(8,128)(2,1)S(1)}, u32[]{:S(2)}, u32[]{:S(2)}) collective-permute-start(bf16[2,80,160]{2,1,0:T(8,128)(2,1)S(1)} %get-tuple-element.8), channel_id=1, source_target_pairs={{8,0},{10,2},{12,4},{14,6},{16,8},{18,10},{20,12},{22,14},{24,16},... | collective-permute-start | bytes 153608 | tf_op jit(solution)/shard_map/ppermute | solution.py:221
  77.5 10.3 %collective-permute-start.4 = (bf16[4,80,160]{2,1,0:T(8,128)(2,1)S(1)}, bf16[4,80,160]{2,1,0:T(8,128)(2,1)S(1)}, u32[]{:S(2)}, u32[]{:S(2)}) collective-permute-start(bf16[4,80,160]{2,1,0:T(8,128)(2,1)S(1)} %bitcast.69), channel_id=1, source_target_pairs={{4,0},{6,2},{8,4},{10,6},{12,8},{14,10},{16,12},{18,14},{20,16},{2... | collective-permute-start | bytes 307208 | tf_op jit(solution)/shard_map/ppermute | solution.py:221
  88.0 19.2 %collective-permute-start.5 = (bf16[8,80,160]{2,1,0:T(8,128)(2,1)S(1)}, bf16[8,80,160]{2,1,0:T(8,128)(2,1)}, u32[]{:S(2)}, u32[]{:S(2)}) collective-permute-start(bf16[8,80,160]{2,1,0:T(8,128)(2,1)S(1)} %bitcast.64), channel_id=1, source_target_pairs={{2,0},{4,2},{6,4},{8,6},{10,8},{12,10},{14,12},{16,14},{18,16},{20... | collective-permute-start | bytes 614408 | tf_op jit(solution)/shard_map/ppermute | solution.py:221
  103.6 35.8 %all-to-all-start.1 = ((bf16[4,704,256]{2,1,0:T(8,128)(2,1)}), bf16[4,704,256]{2,1,0:T(8,128)(2,1)S(1)}, u32[]{:S(2)}, u32[]{:S(2)}) async-start(bf16[4,704,256]{2,1,0:T(8,128)(2,1)} %shard_map.175), calls=%async_computation.1 | async-start | bytes 2883584 | tf_op jit(solution)/shard_map/all_to_all | solution.py:260
  109.3 12.0 %collective-permute-start.6 = (bf16[20,80,128]{2,1,0:T(8,128)(2,1)S(1)}, bf16[20,80,128]{2,1,0:T(8,128)(2,1)S(1)}, u32[]{:S(2)}, u32[]{:S(2)}) collective-permute-start(bf16[20,80,128]{2,1,0:T(8,128)(2,1)S(1)} %pad_maximum_fusion.2.refs_0_.own), channel_id=1, source_target_pairs={{32,0},{64,32},{96,64},{0,96},{33,1},{65,33},{97,65},{1,97},{34,2}... | collective-permute-start | bytes 1228808 | tf_op jit(solution)/shard_map/ppermute | solution.py:228
  111.2 15.1 %collective-permute-start.7 = (bf16[20,80,128]{2,1,0:T(8,128)(2,1)S(1)}, bf16[20,80,128]{2,1,0:T(8,128)(2,1)S(1)}, u32[]{:S(2)}, u32[]{:S(2)}) collective-permute-start(bf16[20,80,128]{2,1,0:T(8,128)(2,1)S(1)} %pad_maximum_fusion.2.refs_0_.own), channel_id=1, source_target_pairs={{64,0},{96,32},{0,64},{32,96},{65,1},{97,33},{1,65},{33,97},{66,2}... | collective-permute-start | bytes 1228808 | tf_op jit(solution)/shard_map/ppermute | solution.py:228
  114.3 20.5 %collective-permute-start.8 = (bf16[20,80,128]{2,1,0:T(8,128)(2,1)S(1)}, bf16[20,80,128]{2,1,0:T(8,128)(2,1)S(1)}, u32[]{:S(2)}, u32[]{:S(2)}) collective-permute-start(bf16[20,80,128]{2,1,0:T(8,128)(2,1)S(1)} %pad_maximum_fusion.2.refs_0_.own), channel_id=1, source_target_pairs={{96,0},{0,32},{32,64},{64,96},{97,1},{1,33},{33,65},{65,97},{98,2}... | collective-permute-start | bytes 1228808 | tf_op jit(solution)/shard_map/ppermute | solution.py:228
  116.5 20.7 %collective-permute-start.9 = (bf16[20,80,128]{2,1,0:T(8,128)(2,1)S(1)}, bf16[20,80,128]{2,1,0:T(8,128)(2,1)S(1)}, u32[]{:S(2)}, u32[]{:S(2)}) collective-permute-start(bf16[20,80,128]{2,1,0:T(8,128)(2,1)S(1)} %pad_maximum_fusion.2.refs_0_.own), channel_id=1, source_target_pairs={{0,1},{1,0},{2,3},{3,2},{4,5},{5,4},{6,7},{7,6},{8,9},{9,8},{10,11... | collective-permute-start | bytes 1228808 | tf_op jit(solution)/shard_map/ppermute | solution.py:229
  121.3 15.9 %collective-permute-start.10 = (bf16[20,80,128]{2,1,0:T(8,128)(2,1)S(1)}, bf16[20,80,128]{2,1,0:T(8,128)(2,1)S(1)}, u32[]{:S(2)}, u32[]{:S(2)}) collective-permute-start(bf16[20,80,128]{2,1,0:T(8,128)(2,1)S(1)} %collective-permute-done.6.refs_1_), channel_id=1, source_target_pairs={{0,1},{1,0},{2,3},{3,2},{4,5},{5,4},{6,7},{7,6},{8,9},{9,8},{10,11... | collective-permute-start | bytes 1228808 | tf_op jit(solution)/shard_map/ppermute | solution.py:229
  126.3 11.6 %collective-permute-start.11 = (bf16[20,80,128]{2,1,0:T(8,128)(2,1)S(1)}, bf16[20,80,128]{2,1,0:T(8,128)(2,1)S(1)}, u32[]{:S(2)}, u32[]{:S(2)}) collective-permute-start(bf16[20,80,128]{2,1,0:T(8,128)(2,1)S(1)} %collective-permute-done.7.refs_2_), channel_id=1, source_target_pairs={{0,1},{1,0},{2,3},{3,2},{4,5},{5,4},{6,7},{7,6},{8,9},{9,8},{10,11... | collective-permute-start | bytes 1228808 | tf_op jit(solution)/shard_map/ppermute | solution.py:229
  134.8 3.9 %collective-permute-start.12 = (bf16[20,80,128]{2,1,0:T(8,128)(2,1)S(1)}, bf16[20,80,128]{2,1,0:T(8,128)(2,1)S(1)}, u32[]{:S(2)}, u32[]{:S(2)}) collective-permute-start(bf16[20,80,128]{2,1,0:T(8,128)(2,1)S(1)} %collective-permute-done.8.refs_3_), channel_id=1, source_target_pairs={{0,1},{1,0},{2,3},{3,2},{4,5},{5,4},{6,7},{7,6},{8,9},{9,8},{10,11... | collective-permute-start | bytes 1228808 | tf_op jit(solution)/shard_map/ppermute | solution.py:229
  137.2 0.8 copy-start
  138.0 0.8 copy-start.2
  138.7 0.8 copy-start.4
  139.5 1.0 copy-start.1
  140.5 1.0 copy-start.3
  141.5 1.0 copy-start.5
  146.6 3.7 %copy-start.17 = (s32[1,1,8]{2,1,0:T(1,128)S(1)}, s32[1,1,8]{2,1,0:T(1,128)}, u32[]{:S(2)}) copy-start(s32[1,1,8]{2,1,0:T(1,128)} %param.21) | copy-start | bytes 100
  146.6 18.7 %copy-start.6 = (bf16[16,32,160]{2,1,0:T(8,128)(2,1)S(1)}, bf16[16,32,160]{2,1,0:T(8,128)(2,1)}, u32[]{:S(2)}) copy-start(bf16[16,32,160]{2,1,0:T(8,128)(2,1)} %residual.1) | copy-start | bytes 491524
  146.6 18.7 %copy-start.7 = (bf16[1,32,160]{2,1,0:T(8,128)(2,1)S(1)}, bf16[1,32,160]{2,1,0:T(8,128)(2,1)}, u32[]{:S(2)}) copy-start(bf16[1,32,160]{2,1,0:T(8,128)(2,1)} %long_residual.1) | copy-start | bytes 30724
  146.6 18.7 %all-to-all-start.2 = ((bf16[4,512,256]{2,1,0:T(8,128)(2,1)}), bf16[4,512,256]{2,1,0:T(8,128)(2,1)S(1)}, u32[]{:S(2)}, u32[]{:S(2)}) async-start(bf16[4,512,256]{2,1,0:T(8,128)(2,1)} %shard_map.176), calls=%async_computation.2 | async-start | bytes 2097152 | tf_op jit(solution)/shard_map/all_to_all | solution.py:273

commit v2 on v1

v2 whole, which is shorter than its diff:
```python
import jax
import jax.numpy as jnp
from jax import lax
from jax.experimental import pallas as pl
from jax.experimental.pallas import tpu as pltpu
from jax.sharding import Mesh, PartitionSpec as P

HEADS = 40
NOPE = 64
ROPE = 32
VDIM = 64
KVR = 256
TREE = 32
ROWS = ("y", "x")
COLS = ("z", "c")
SWAP = [(0, 1), (1, 0)]
BF = jnp.bfloat16
F32 = jnp.float32


def tree_reach(parent_ids):
    tree_count = parent_ids.shape[-1]
    positions = jnp.arange(tree_count, dtype=jnp.int32)
    reach = (parent_ids[..., :, None] == positions).astype(F32)
    reach = reach + (positions[:, None] == positions[None, :]).astype(F32)
    for _ in range(max(1, (tree_count - 1).bit_length())):
        product = jnp.einsum("...ij,...jk->...ik", reach, reach, preferred_element_type=F32)
        reach = jnp.minimum(reach + product, 1.0)
    return reach > 0.5


OVER_LAST = (((1,), (1,)), ((), ()))
SLICE = HEADS // 4
SPAN = SLICE * VDIM
LONG_AT, TREE_AT, QUERY_AT, BLOCK = 576, 1152, 1280, 1536
TOKENS = 16 * TREE + TREE
QUARTER = TOKENS // 4


def split3(value):
    high = value.astype(BF)
    rest = value - high.astype(F32)
    mid = rest.astype(BF)
    return high, mid, (rest - mid.astype(F32)).astype(BF)


def dot(left, right):
    return jnp.dot(left, right, preferred_element_type=F32)


def dot_t(left, right):
    return lax.dot_general(left, right, OVER_LAST, preferred_element_type=F32)


def place_shards(z, c, mine, twin, target, sems):
    copies = []
    for j in range(4):
        at = lax.rem(lax.rem(z, 4) + 4 - j, 4)
        copies.append(pltpu.make_async_copy(mine.at[j], target.at[at, c], sems.at[j]))
        copies.append(pltpu.make_async_copy(twin.at[j], target.at[at, 1 - c], sems.at[4 + j]))
    for copy in copies:
        copy.start()
    return copies


def attend_kernel(place, got, query_l, tree_l, mine, twin, out, kv, lat, sems):
    copies = place_shards(place[0], place[1], mine, twin, kv, sems)
    lanes = lax.broadcasted_iota(jnp.int32, (TREE, 128), 1)
    slots = lax.broadcasted_iota(jnp.int32, (1, 256), 1).astype(F32)
    scale = (NOPE + ROPE) ** -0.5
    size = SLICE * TREE

    def rope_rows(chunk):
        zero = jnp.zeros((TREE, 128), BF)
        return jnp.concatenate([jnp.where(lanes // 32 == h % 4, chunk(5 + h // 4), zero) for h in range(SLICE)], axis=0)

    def cached(query, rope, block, at, length):
        keys = jnp.concatenate([block[at : at + 288], block[at + 288 : at + 576]], axis=1)
        scores = dot(query, keys[:KVR]) + dot(rope, jnp.concatenate([keys[KVR:]] * 4, axis=0))
        return jnp.where(slots < length, scores * scale, -jnp.inf), keys[:KVR]

    def treed(query, rope, block, at):
        keys = jnp.concatenate([block[at : at + TREE], block[at + TREE : at + 2 * TREE]], axis=1)
        scores = dot_t(query, keys) + dot_t(rope, block[at + 2 * TREE : at + 3 * TREE])
        reach = block[at + 3 * TREE : at + 4 * TREE, :TREE].astype(F32)
        reach = jnp.concatenate([reach] * SLICE, axis=0)
        return jnp.where(reach > 0.5, scores * scale, -jnp.inf), keys

    for copy in copies:
        copy.wait()
    for p in range(SLICE // 2):
        at = TREE * p
        rows = [got[k, QUERY_AT + at : QUERY_AT + at + TREE] for k in range(4)] + [query_l[at : at + TREE]]
        even = [jnp.where(lanes < NOPE, row, jnp.zeros_like(row)) for row in rows]
        odd = [jnp.where(lanes < NOPE, jnp.zeros_like(row), row) for row in rows]
        weight = kv[...][:, :, :, :KVR].reshape(SPAN, KVR)[128 * p : 128 * (p + 1)]
        part = dot(jnp.concatenate(even + odd, axis=0), weight).astype(BF)
        for s in range(2):
            for k in range(5):
                lat[k, TREE * (2 * p + s) : TREE * (2 * p + s + 1)] = part[TREE * (5 * s + k) : TREE * (5 * s + k + 1)]

    for k in range(4):
        block = got.at[k]
        query = lat[k]
        rope = rope_rows(lambda i: block[QUERY_AT + TREE * i : QUERY_AT + TREE * (i + 1)])
        length = block[TREE_AT + 3 * TREE : TREE_AT + 3 * TREE + 1, 32:33].astype(F32)
        first, keys = cached(query, rope, block, 0, length)
        second, tree = treed(query, rope, block, TREE_AT)
        top = jnp.maximum(jnp.max(first, axis=-1, keepdims=True), jnp.max(second, axis=-1, keepdims=True))
        first, second = jnp.exp(first - top), jnp.exp(second - top)
        total = jnp.sum(first, axis=-1, keepdims=True) + jnp.sum(second, axis=-1, keepdims=True)
        acc = dot_t(first.astype(BF), keys) + dot(second.astype(BF), tree)
        lat[k] = (acc / total).astype(BF)

    query = lat[4]
    rope = rope_rows(lambda i: query_l[TREE * i : TREE * (i + 1)])
    second, tree = treed(query, rope, tree_l, 0)
    scored = []
    for k in range(4):
        block = got.at[k]
        length = block[TREE_AT + 3 * TREE : TREE_AT + 3 * TREE + 1, 33:34].astype(F32)
        scored.append(cached(query, rope, block, LONG_AT, length))
    top = jnp.max(second, axis=-1, keepdims=True)
    for scores, _ in scored:
        top = jnp.maximum(top, jnp.max(scores, axis=-1, keepdims=True))
    second = jnp.exp(second - top)
    total = jnp.sum(second, axis=-1, keepdims=True)
    acc = dot(second.astype(BF), tree)
    for scores, keys in scored:
        weights = jnp.exp(scores - top)
        total += jnp.sum(weights, axis=-1, keepdims=True)
        acc += dot_t(weights.astype(BF), keys)
    lat[4] = (acc / total).astype(BF)
    column = top + jnp.log(total)
    logs = jnp.zeros((TREE, 128), F32)
    for h in range(SLICE):
        logs = jnp.where(lanes == h, column[TREE * h : TREE * (h + 1)], logs)

    for p in range(SLICE // 2):
        pair = []
        for h in (2 * p, 2 * p + 1):
            rows = jnp.concatenate([lat[k, TREE * h : TREE * (h + 1)] for k in range(5)], axis=0)
            weight = kv[...][:, :, :, KVR:].reshape(SPAN, KVR)[VDIM * h : VDIM * (h + 1)]
            pair.append(dot_t(rows, weight))
        heads = jnp.concatenate(pair, axis=1).astype(BF)
        for d in range(4):
            out[d, 5 * TREE * p : 5 * TREE * (p + 1)] = heads
    base = 5 * TREE * (SLICE // 2)
    for i, part in enumerate(split3(logs)):
        for d in range(4):
            out[d, base + TREE * i : base + TREE * (i + 1)] = part


def project_kernel(place, got, mine, twin, send, weight, rows, sems):
    copies = place_shards(place[0], place[1], mine, twin, weight, sems)
    base = 5 * TREE * (SLICE // 2)
    logs = sum(got[:, base + TREE * i : base + TREE * (i + 1)].astype(F32) for i in range(3))
    share = jnp.exp(logs - jnp.max(logs, axis=0)[None])
    share = (share / jnp.sum(share, axis=0)[None]).reshape(4 * TREE, 128)
    high = share.astype(BF)
    low = (share - high.astype(F32)).astype(BF)
    for p in range(SLICE // 2):
        at = 5 * TREE * p
        cols = slice(128 * p, 128 * (p + 1))
        for y in range(4):
            rows[4 * TREE * y : 4 * TREE * (y + 1), cols] = got[y, at : at + 4 * TREE]
        owner = lax.broadcasted_iota(jnp.int32, (128, 128), 1) // VDIM + 2 * p
        select = jnp.where(lax.broadcasted_iota(jnp.int32, (128, 128), 0) == owner, 1.0, 0.0).astype(BF)
        wide = (dot(high, select) + dot(low, select)).reshape(4, TREE, 128)
        piece = got[:, at + 4 * TREE : at + 5 * TREE].astype(F32) * wide
        rows[16 * TREE : 17 * TREE, cols] = jnp.sum(piece, axis=0).astype(BF)
    for copy in copies:
        copy.wait()
    full = weight[...].reshape(SPAN, 640)
    for x in range(4):
        send[x, :TOKENS] = dot(rows[...], full[:, 128 * x : 128 * (x + 1)]).astype(BF)
    rest = dot(rows[...], full[:, 512:])
    lanes = lax.broadcasted_iota(jnp.int32, (QUARTER, 128), 1) // 32
    for x in range(4):
        packed = jnp.zeros((QUARTER, 128), F32)
        for g in range(4):
            part = rest[QUARTER * g : QUARTER * (g + 1)]
            shift = (32 * (g - x)) % 128
            part = pltpu.roll(part, shift, 1) if shift else part
            packed = jnp.where(lanes == g, part, packed)
        send[x, TOKENS : TOKENS + QUARTER] = packed.astype(BF)
        send[x, TOKENS + QUARTER :] = jnp.zeros((send.shape[1] - TOKENS - QUARTER, 128), BF)


def finish_kernel(got, residual, long_residual, hidden, long_hidden, tail):
    rest = jnp.sum(got[:, TOKENS : TOKENS + QUARTER].astype(F32), axis=0)
    for g in range(4):
        tail[QUARTER * g : QUARTER * (g + 1)] = pltpu.roll(rest, (-32 * g) % 128, 1) if g else rest
    for i in range(17):
        at = slice(TREE * i, TREE * (i + 1))
        main = jnp.sum(got[:, at].astype(F32), axis=0)
        source, target, k = (residual, hidden, i) if i < 16 else (long_residual, long_hidden, 0)
        target[k, :, :128] = (source[k, :, :128].astype(F32) + main).astype(BF)
        target[k, :, 128:160] = (source[k, :, 128:160].astype(F32) + tail[at, :32]).astype(BF)


SMEM = pl.BlockSpec(memory_space=pltpu.SMEM)
VMEM = pl.BlockSpec(memory_space=pltpu.VMEM)
ANY = pl.BlockSpec(memory_space=pl.ANY)
PARAMS = pltpu.CompilerParams(vmem_limit_bytes=48 << 20)


def slice_queries(queries):
    heads = queries.reshape(TREE, 4, SLICE, NOPE + ROPE)
    nope = heads[..., :NOPE].reshape(TREE, 4, SLICE // 2, 128).transpose(1, 2, 0, 3)
    rope = heads[..., NOPE:].reshape(TREE, 4, SLICE * ROPE)
    rope = jnp.pad(rope, ((0, 0), (0, 0), (0, 64))).reshape(TREE, 4, 3, 128).transpose(1, 2, 0, 3)
    return jnp.concatenate([nope, rope], axis=1).reshape(4, 8 * TREE, 128)


def tree_block(rows, reach, lengths):
    extra = jnp.concatenate([reach.astype(BF), jnp.broadcast_to(lengths.astype(BF)[None], (TREE, 2))], axis=1)
    extra = jnp.pad(extra, ((0, 0), (0, 128 - extra.shape[1])))
    rope = jnp.concatenate([rows[:, KVR:]] * 4, axis=1)
    return jnp.concatenate([rows[:, :128], rows[:, 128:KVR], rope, extra], axis=0)


def fetch_slice(value, nx, nz):
    parts = []
    for j in range(4):
        pairs = [
            (i * nz + 4 * k + m, k * nz + 4 * i + (m + j) % 4) for i in range(nx) for k in range(nx) for m in range(4)
        ]
        parts.append(lax.ppermute(value, ("x", "z"), pairs))
    return jnp.stack(parts)


def on_device(
    queries, tree_latent, parents, cache, cache_lengths, accepted, residual,
    long_queries, long_tree_latent, long_parents, long_cache, long_plan, long_residual,
    key_up, value_up, out_weight,
):
    nx, nz = lax.axis_size("x"), lax.axis_size("z")
    y, x, z, c = lax.axis_index("y"), lax.axis_index("x"), lax.axis_index("z"), lax.axis_index("c")
    place = jnp.stack([z, c]).astype(jnp.int32)
    kv = fetch_slice(jnp.concatenate([key_up, value_up], axis=1), nx, nz)
    kv_twin = lax.ppermute(kv, "c", SWAP)
    cols = lax.all_gather(out_weight, "x")
    cols = jnp.concatenate([cols[k, :, :128] for k in range(nx)] + [cols[k, :, 128:] for k in range(nx)], axis=1)
    out_rows = fetch_slice(cols, nx, nz)
    out_twin = lax.ppermute(out_rows, "c", SWAP)

    reach = tree_reach(jnp.concatenate([parents[0], long_parents], axis=0))
    lengths = jnp.concatenate([cache_lengths[0], long_plan[0]])
    short_t, long_t = cache[0, 0].T, long_cache[0].T
    keys = jnp.concatenate([short_t[:, :128], short_t[:, 128:], long_t[:, :128], long_t[:, 128:]], axis=0)
    keys = jnp.concatenate([keys, tree_block(tree_latent[0], reach[0], lengths)], axis=0)
    block = jnp.concatenate(
        [jnp.broadcast_to(keys[None], (nx,) + keys.shape), slice_queries(queries[0])], axis=1
    )
    got = lax.all_to_all(block, "x", 0, 0)
    query_l = lax.dynamic_index_in_dim(slice_queries(long_queries[0]), x, 0, keepdims=False)
    tree_l = tree_block(long_tree_latent[0], reach[1] & (y == 0), lengths)
    shard = key_up.shape[0]

    heads = pl.pallas_call(
        attend_kernel,
        out_shape=jax.ShapeDtypeStruct((4, 5 * TREE * (SLICE // 2) + 3 * TREE, 128), BF),
        in_specs=[SMEM, VMEM, VMEM, VMEM, ANY, ANY],
        out_specs=VMEM,
        scratch_shapes=[
            pltpu.VMEM((4, 2, shard, 2 * KVR), BF),
            pltpu.VMEM((5, SLICE * TREE, KVR), BF),
            pltpu.SemaphoreType.DMA((8,)),
        ],
        compiler_params=PARAMS,
    )(place, got, query_l, tree_l, kv, kv_twin)
    shared = lax.all_to_all(heads, "y", 0, 0)
    send = pl.pallas_call(
        project_kernel,
        out_shape=jax.ShapeDtypeStruct((4, 688, 128), BF),
        in_specs=[SMEM, VMEM, ANY, ANY],
        out_specs=VMEM,
        scratch_shapes=[
            pltpu.VMEM((4, 2, shard, 640), BF),
            pltpu.VMEM((TOKENS, SPAN), BF),
            pltpu.SemaphoreType.DMA((8,)),
        ],
        compiler_params=PARAMS,
    )(place, shared, out_rows, out_twin)
    back = lax.all_to_all(send, "x", 0, 0)
    hidden, long_hidden = pl.pallas_call(
        finish_kernel,
        out_shape=(
            jax.ShapeDtypeStruct(residual.shape, BF),
            jax.ShapeDtypeStruct(long_residual.shape, BF),
        ),
        in_specs=[VMEM, VMEM, VMEM],
        out_specs=(VMEM, VMEM),
        scratch_shapes=[pltpu.VMEM((TOKENS, 128), F32)],
        compiler_params=PARAMS,
    )(back, residual, long_residual)
    accepted_cache = jnp.take_along_axis(tree_latent[0], accepted[0, 0][:, None], axis=0)[None, None]
    return hidden, accepted_cache, long_hidden


def solution(mesh):
    split = Mesh(mesh.devices.reshape(4, 4, 16, 2), ("y", "x", "z", "c"))
    return jax.shard_map(
        on_device,
        mesh=split,
        in_specs=(
            P(ROWS, COLS, None),
            P(ROWS, COLS, None),
            P(ROWS, COLS, None),
            P(ROWS, COLS, None, None),
            P(ROWS, COLS),
            P(ROWS, COLS, None),
            P(None, COLS, ROWS),
            P(COLS, None, None),
            P(COLS, None, None),
            P(COLS, None),
            P(COLS, ROWS, None),
            P(COLS, ROWS),
            P(COLS, None, ROWS),
            P(COLS, None),
            P(COLS, None),
            P(COLS, ROWS),
        ),
        out_specs=(P(None, COLS, ROWS), P(ROWS, COLS, None, None), P(COLS, None, ROWS)),
        check_vma=False,
    )
```

time: 169 us -> 164 us (0.970)
  waiting for transfers between devices: 52.2 us -> 16.6 us
  blocking collectives: 0 us -> 31.8 us
  starting transfers between devices: 83.1 us -> 92.4 us
  Pallas kernels: 15.6 us -> 10.9 us
  local copies, waits for them, and re-layouts: 9.79 us -> 5.48 us
    all_to_all x1, starting transfers between devices: 3.66 us -> 45.5 us  [on_device(): back = lax.all_to_all(send, 'x', 0, 0)]
    all_gather x0 -> x1, blocking collectives: none -> 31.8 us  [on_device(): cols = lax.all_gather(out_weight, 'x')]
    ppermute x13 -> x10, starting transfers between devices: 57.6 us -> 37.7 us  [the longest x8 22.5 us: fetch_slice(): parts.append(lax.ppermute(value, ('x', 'z'), pairs))]
    all_to_all x2, waiting for transfers between devices: 17.8 us -> 0.01 us  [the longest x1 0.01 us: on_device(): got = lax.all_to_all(block, 'x', 0, 0)]
    ppermute x13 -> x10, waiting for transfers between devices: 20.7 us -> 7.05 us  [the longest x8 4.61 us: fetch_slice(): parts.append(lax.ppermute(value, ('x', 'z'), pairs))]
    all_to_all x2, starting transfers between devices: 21.9 us -> 9.17 us  [the longest x1 4.97 us: on_device(): got = lax.all_to_all(block, 'x', 0, 0)]
    unnamed x38 -> x33, local copies, waits for them, and re-layouts: 5.97 us -> 0.47 us
    all_to_all x1, waiting for transfers between devices: 13.7 us -> 9.58 us  [on_device(): back = lax.all_to_all(send, 'x', 0, 0)]
  transfers between devices with their start and end apart: 16 -> 13, of which waited for: 6 -> 5; matrix products, arithmetic and copies ran while one was open for 5% -> 2% of each run, Pallas kernels for 6% -> 0%
where the time goes in v2:
time: 164 us; the launch traced here: 163 us
  starting transfers between devices  92.4 us (56%)
  blocking collectives  31.8 us (19%)
  waiting for transfers between devices  16.6 us (10%)
  Pallas kernels  10.9 us (7%)
  local copies, waits for them, and re-layouts  5.48 us (3%)
  other arithmetic  2.72 us (2%)
  between operations  2.48 us (2%)
    all_to_all x1, starting transfers between devices, on_device(): back = lax.all_to_all(send, 'x', 0, 0)  45.5 us
    all_gather x1, blocking collectives, on_device(): cols = lax.all_gather(out_weight, 'x')  31.8 us
    ppermute x8, starting transfers between devices, fetch_slice(): parts.append(lax.ppermute(value, ('x', 'z'), pairs))  22.5 us
    all_to_all x1, waiting for transfers between devices, on_device(): back = lax.all_to_all(send, 'x', 0, 0)  9.58 us
    ppermute x1, starting transfers between devices, on_device(): out_twin = lax.ppermute(out_rows, 'c', SWAP)  8.4 us
    ppermute x1, starting transfers between devices, on_device(): kv_twin = lax.ppermute(kv, 'c', SWAP)  6.81 us
    pallas_call x1, Pallas kernels, on_device(): pl.pallas_call(attend_kernel, out_shape=jax.ShapeDtypeStruct((4, 5 * TREE...  5.92 us
    all_to_all x1, starting transfers between devices, on_device(): got = lax.all_to_all(block, 'x', 0, 0)  4.97 us
  transfers between devices with their start and end apart: 13, of which 5 were waited for; matrix products, arithmetic and copies ran while one was open for 2% of the time, Pallas kernels for 0%

profile of v2, /device:TPU:1, one launch (start us, length us, event | category | flops | bytes accessed | tf_op | source)
XLA Modules:
  0.0 163.1 jit_solution(4576420179576710226)
XLA Ops:
  0.6 1.5 reshape_squeeze.6
  2.2 0.2 slice.107
  2.4 0.3 reshape.156
  2.9 0.3 reshape.137
  3.2 0.1 pad_maximum_fusion.3
  3.3 0.1 copy.27
  3.4 0.2 copy-done.4
  3.8 0.2 fusion
  4.0 0.1 fusion.1
  4.1 0.1 fusion.2
  4.3 0.1 fusion.3
  4.4 0.1 fusion.5
  5.8 0.1 constant_dynamic-update-slice_fusion.1
  6.1 0.2 broadcast_in_dim.11
  6.2 1.3 pad_maximum_fusion
  7.5 5.0 %all-to-all-start = ((bf16[4,1536,128]{2,1,0:T(8,128)(2,1)}), bf16[4,1536,128]{2,1,0:T(8,128)(2,1)S(1)}, u32[]{:S(2)}, u32[]{:S(2)}) async-start(bf16[4,1536,128]{2,1,0:T(8,128)(2,1)} %pad_maximum_fusion), calls=%async_computation | async-start | bytes 3145728 | tf_op jit(solution)/shard_map/all_to_all | solution.py:256
  12.5 6.3 %collective-permute-start.3 = (bf16[80,512]{1,0:T(8,128)(2,1)S(1)}, bf16[80,512]{1,0:T(8,128)(2,1)S(1)}, u32[]{:S(2)}, u32[]{:S(2)}) collective-permute-start(bf16[80,512]{1,0:T(8,128)(2,1)S(1)} %constant_dynamic-update-slice_fusion.4), channel_id=1, source_target_pairs={{0,6},{2,0},{4,2},{6,4},{8,38},{10,32},{12,34},{14,36},{16,70},{18... | collective-permute-start | bytes 245768 | tf_op jit(solution)/shard_map/ppermute | solution.py:229
  18.8 1.9 %collective-permute-start.2 = (bf16[80,512]{1,0:T(8,128)(2,1)S(1)}, bf16[80,512]{1,0:T(8,128)(2,1)S(1)}, u32[]{:S(2)}, u32[]{:S(2)}) collective-permute-start(bf16[80,512]{1,0:T(8,128)(2,1)S(1)} %constant_dynamic-update-slice_fusion.4), channel_id=1, source_target_pairs={{0,4},{2,6},{4,0},{6,2},{8,36},{10,38},{12,32},{14,34},{16,68},{18... | collective-permute-start | bytes 245768 | tf_op jit(solution)/shard_map/ppermute | solution.py:229
  20.7 2.2 %collective-permute-start.1 = (bf16[80,512]{1,0:T(8,128)(2,1)S(1)}, bf16[80,512]{1,0:T(8,128)(2,1)S(1)}, u32[]{:S(2)}, u32[]{:S(2)}) collective-permute-start(bf16[80,512]{1,0:T(8,128)(2,1)S(1)} %constant_dynamic-update-slice_fusion.4), channel_id=1, source_target_pairs={{0,2},{2,4},{4,6},{6,0},{8,34},{10,36},{12,38},{14,32},{16,66},{18... | collective-permute-start | bytes 245768 | tf_op jit(solution)/shard_map/ppermute | solution.py:229
  22.9 0.7 collective-permute-start
  23.6 0.6 reshape_squeeze.7
  24.2 0.2 slice.109
  24.4 0.3 reshape.157
  24.9 0.3 reshape.141
  25.2 0.1 pad_maximum_fusion.4
  25.3 0.1 copy.30
  25.5 31.8 %all-gather = bf16[320,160]{1,0:T(8,128)(2,1)S(1)} all-gather(bf16[80,160]{1,0:T(8,128)(2,1)S(1)} %copy-done.8), channel_id=2, replica_groups=mesh['y'=4,'x'=4,'z'=16,'c'=2] {'x'}, dimensions={0}, use_global_device_ids=true | all-gather | bytes 128000 | tf_op jit(solution)/shard_map/all_gather | solution.py:243
  57.4 0.1 fusion.7.tree_l
  57.6 6.8 %collective-permute-start.4 = (bf16[4,80,512]{2,1,0:T(8,128)(2,1)S(1)}, bf16[4,80,512]{2,1,0:T(8,128)(2,1)S(1)}, u32[]{:S(2)}, u32[]{:S(2)}) collective-permute-start(bf16[4,80,512]{2,1,0:T(8,128)(2,1)S(1)} %pad_maximum_fusion.2.mine), channel_id=1, source_target_pairs={{0,1},{1,0},{2,3},{3,2},{4,5},{5,4},{6,7},{7,6},{8,9},{9,8},{10,11... | collective-permute-start | bytes 983048 | tf_op jit(solution)/shard_map/ppermute | solution.py:242
  64.4 0.1 pad_add_fusion.1.place
  64.5 1.1 collective-permute-done.4.twin
  65.6 5.9 %shard_map.175 = bf16[4,896,128]{2,1,0:T(8,128)(2,1)} custom-call(s32[2]{0:T(128)S(1)} %pad_add_fusion.1.place, bf16[4,1536,128]{2,1,0:T(8,128)(2,1)S(1)} %all-to-all-done.got, bf16[256,128]{1,0:T(8,128)(2,1)S(1)} %dynamic-slice_bitcast_fusion.query_l, bf16[128,128]{1,0:T(8,128)(2,1)S(1)} %fusion.7.tree_l, bf16[4,80,512]{2,1,0:T(8,128)(2,1)S(1)} %pad_maximum_fusion.2.mine, ...), custom_call_target="tpu_custom_call" | custom-call | tf_op jit(solution)/shard_map/pallas_call | solution.py:261
  71.6 4.2 %all-to-all-start.1 = ((bf16[4,896,128]{2,1,0:T(8,128)(2,1)}), bf16[4,896,128]{2,1,0:T(8,128)(2,1)S(1)}, u32[]{:S(2)}, u32[]{:S(2)}) async-start(bf16[4,896,128]{2,1,0:T(8,128)(2,1)} %shard_map.175), calls=%async_computation.1 | async-start | bytes 1835008 | tf_op jit(solution)/shard_map/all_to_all | solution.py:273
  75.8 0.1 concatenate.62
  75.9 2.5 %collective-permute-start.8 = (bf16[80,640]{1,0:T(8,128)(2,1)S(1)}, bf16[80,640]{1,0:T(8,128)(2,1)S(1)}, u32[]{:S(2)}, u32[]{:S(2)}) collective-permute-start(bf16[80,640]{1,0:T(8,128)(2,1)S(1)} %concatenate.62), channel_id=1, source_target_pairs={{0,6},{2,0},{4,2},{6,4},{8,38},{10,32},{12,34},{14,36},{16,70},{18... | collective-permute-start | bytes 307208 | tf_op jit(solution)/shard_map/ppermute | solution.py:229
  78.4 4.9 %collective-permute-start.7 = (bf16[80,640]{1,0:T(8,128)(2,1)S(1)}, bf16[80,640]{1,0:T(8,128)(2,1)S(1)}, u32[]{:S(2)}, u32[]{:S(2)}) collective-permute-start(bf16[80,640]{1,0:T(8,128)(2,1)S(1)} %concatenate.62), channel_id=1, source_target_pairs={{0,4},{2,6},{4,0},{6,2},{8,36},{10,38},{12,32},{14,34},{16,68},{18... | collective-permute-start | bytes 307208 | tf_op jit(solution)/shard_map/ppermute | solution.py:229
  83.3 3.4 %collective-permute-start.6 = (bf16[80,640]{1,0:T(8,128)(2,1)S(1)}, bf16[80,640]{1,0:T(8,128)(2,1)S(1)}, u32[]{:S(2)}, u32[]{:S(2)}) collective-permute-start(bf16[80,640]{1,0:T(8,128)(2,1)S(1)} %concatenate.62), channel_id=1, source_target_pairs={{0,2},{2,4},{4,6},{6,0},{8,34},{10,36},{12,38},{14,32},{16,66},{18... | collective-permute-start | bytes 307208 | tf_op jit(solution)/shard_map/ppermute | solution.py:229
  86.7 0.7 collective-permute-start.5
  87.4 1.4 collective-permute-done.7
  88.7 3.2 %collective-permute-done.6 = bf16[80,640]{1,0:T(8,128)(2,1)S(1)} collective-permute-done((bf16[80,640]{1,0:T(8,128)(2,1)S(1)}, bf16[80,640]{1,0:T(8,128)(2,1)S(1)}, u32[]{:S(2)}, u32[]{:S(2)}) %collective-permute-start.6) | collective-permute-done | bytes 102432 | tf_op jit(solution)/shard_map/ppermute | solution.py:229
  92.0 8.4 %collective-permute-start.9 = (bf16[4,80,640]{2,1,0:T(8,128)(2,1)S(1)}, bf16[4,80,640]{2,1,0:T(8,128)(2,1)S(1)}, u32[]{:S(2)}, u32[]{:S(2)}) collective-permute-start(bf16[4,80,640]{2,1,0:T(8,128)(2,1)S(1)} %pad_maximum_fusion.1.mine), channel_id=1, source_target_pairs={{0,1},{1,0},{2,3},{3,2},{4,5},{5,4},{6,7},{7,6},{8,9},{9,8},{10,11... | collective-permute-start | bytes 1228808 | tf_op jit(solution)/shard_map/ppermute | solution.py:246
  100.5 1.3 collective-permute-done.9.twin
  101.8 4.1 %shard_map.176 = bf16[4,688,128]{2,1,0:T(8,128)(2,1)} custom-call(s32[2]{0:T(128)S(1)} %pad_add_fusion.1.place, bf16[4,896,128]{2,1,0:T(8,128)(2,1)S(1)} %all-to-all-done.1.got, bf16[4,80,640]{2,1,0:T(8,128)(2,1)S(1)} %pad_maximum_fusion.1.mine, bf16[4,80,640]{2,1,0:T(8,128)(2,1)S(1)} %collective-permute-done.9.twin), custom_call_target="tpu_custom_call" | custom-call | tf_op jit(solution)/shard_map/pallas_call | solution.py:274
  105.9 45.5 %all-to-all-start.2 = ((bf16[4,688,128]{2,1,0:T(8,128)(2,1)}), bf16[4,688,128]{2,1,0:T(8,128)(2,1)S(1)}, u32[]{:S(2)}, u32[]{:S(2)}) async-start(bf16[4,688,128]{2,1,0:T(8,128)(2,1)} %shard_map.176), calls=%async_computation.2 | async-start | bytes 1409024 | tf_op jit(solution)/shard_map/all_to_all | solution.py:286
  151.4 0.6 gather_fusion
  152.0 0.7 bitcast_select_fusion
  152.7 9.6 %all-to-all-done.2.got = bf16[4,688,128]{2,1,0:T(8,128)(2,1)S(1)} async-done(((bf16[4,688,128]{2,1,0:T(8,128)(2,1)}), bf16[4,688,128]{2,1,0:T(8,128)(2,1)S(1)}, u32[]{:S(2)}, u32[]{:S(2)}) %all-to-all-start.2) | async-done | bytes 704544 | tf_op jit(solution)/shard_map/all_to_all | solution.py:286
  162.3 0.9 shard_map.177
  (66 shorter events, 0.8 us)
Async XLA Ops:
  2.7 0.9 copy-start.4
  2.7 1.0 copy-start.5
  2.8 1.0 copy-start.3
  2.8 1.0 copy-start.10
  2.8 1.0 copy-start.11
  7.5 5.0 %copy-start.6 = (bf16[80,256]{1,0:T(8,128)(2,1)S(1)}, bf16[80,256]{1,0:T(8,128)(2,1)}, u32[]{:S(2)}) copy-start(bf16[80,256]{1,0:T(8,128)(2,1)} %param.29) | copy-start | bytes 122884
  7.5 5.0 %copy-start.7 = (bf16[80,256]{1,0:T(8,128)(2,1)S(1)}, bf16[80,256]{1,0:T(8,128)(2,1)}, u32[]{:S(2)}) copy-start(bf16[80,256]{1,0:T(8,128)(2,1)} %param.30) | copy-start | bytes 122884
  7.5 16.1 %copy-start.2 = (bf16[1,32,3840]{2,1,0:T(8,128)(2,1)S(1)}, bf16[1,32,3840]{2,1,0:T(8,128)(2,1)}, u32[]{:S(2)}) copy-start(bf16[1,32,3840]{2,1,0:T(8,128)(2,1)} %param.23) | copy-start | bytes 737284
  7.5 58.1 %all-to-all-start = ((bf16[4,1536,128]{2,1,0:T(8,128)(2,1)}), bf16[4,1536,128]{2,1,0:T(8,128)(2,1)S(1)}, u32[]{:S(2)}, u32[]{:S(2)}) async-start(bf16[4,1536,128]{2,1,0:T(8,128)(2,1)} %pad_maximum_fusion), calls=%async_computation | async-start | bytes 3145728 | tf_op jit(solution)/shard_map/all_to_all | solution.py:256
  12.5 44.9 %collective-permute-start.3 = (bf16[80,512]{1,0:T(8,128)(2,1)S(1)}, bf16[80,512]{1,0:T(8,128)(2,1)S(1)}, u32[]{:S(2)}, u32[]{:S(2)}) collective-permute-start(bf16[80,512]{1,0:T(8,128)(2,1)S(1)} %constant_dynamic-update-slice_fusion.4), channel_id=1, source_target_pairs={{0,6},{2,0},{4,2},{6,4},{8,38},{10,32},{12,34},{14,36},{16,70},{18... | collective-permute-start | bytes 245768 | tf_op jit(solution)/shard_map/ppermute | solution.py:229
  18.8 38.7 %collective-permute-start.2 = (bf16[80,512]{1,0:T(8,128)(2,1)S(1)}, bf16[80,512]{1,0:T(8,128)(2,1)S(1)}, u32[]{:S(2)}, u32[]{:S(2)}) collective-permute-start(bf16[80,512]{1,0:T(8,128)(2,1)S(1)} %constant_dynamic-update-slice_fusion.4), channel_id=1, source_target_pairs={{0,4},{2,6},{4,0},{6,2},{8,36},{10,38},{12,32},{14,34},{16,68},{18... | collective-permute-start | bytes 245768 | tf_op jit(solution)/shard_map/ppermute | solution.py:229
  20.7 36.8 %collective-permute-start.1 = (bf16[80,512]{1,0:T(8,128)(2,1)S(1)}, bf16[80,512]{1,0:T(8,128)(2,1)S(1)}, u32[]{:S(2)}, u32[]{:S(2)}) collective-permute-start(bf16[80,512]{1,0:T(8,128)(2,1)S(1)} %constant_dynamic-update-slice_fusion.4), channel_id=1, source_target_pairs={{0,2},{2,4},{4,6},{6,0},{8,34},{10,36},{12,38},{14,32},{16,66},{18... | collective-permute-start | bytes 245768 | tf_op jit(solution)/shard_map/ppermute | solution.py:229
  22.9 34.6 %collective-permute-start = (bf16[80,512]{1,0:T(8,128)(2,1)S(1)}, bf16[80,512]{1,0:T(8,128)(2,1)S(1)}, u32[]{:S(2)}, u32[]{:S(2)}) collective-permute-start(bf16[80,512]{1,0:T(8,128)(2,1)S(1)} %constant_dynamic-update-slice_fusion.4), channel_id=1, source_target_pairs={{0,0},{2,2},{4,4},{6,6},{8,32},{10,34},{12,36},{14,38},{16,64},{18... | collective-permute-start | bytes 245768 | tf_op jit(solution)/shard_map/ppermute | solution.py:229
  24.7 0.7 copy-start.9
  24.7 0.8 copy-start.8
  57.6 8.0 %collective-permute-start.4 = (bf16[4,80,512]{2,1,0:T(8,128)(2,1)S(1)}, bf16[4,80,512]{2,1,0:T(8,128)(2,1)S(1)}, u32[]{:S(2)}, u32[]{:S(2)}) collective-permute-start(bf16[4,80,512]{2,1,0:T(8,128)(2,1)S(1)} %pad_maximum_fusion.2.mine), channel_id=1, source_target_pairs={{0,1},{1,0},{2,3},{3,2},{4,5},{5,4},{6,7},{7,6},{8,9},{9,8},{10,11... | collective-permute-start | bytes 983048 | tf_op jit(solution)/shard_map/ppermute | solution.py:242
  71.5 28.9 %copy-start.12 = (s32[1,1,8]{2,1,0:T(1,128)S(1)}, s32[1,1,8]{2,1,0:T(1,128)}, u32[]{:S(2)}) copy-start(s32[1,1,8]{2,1,0:T(1,128)} %param.21) | copy-start | bytes 100
  71.6 30.2 %all-to-all-start.1 = ((bf16[4,896,128]{2,1,0:T(8,128)(2,1)}), bf16[4,896,128]{2,1,0:T(8,128)(2,1)S(1)}, u32[]{:S(2)}, u32[]{:S(2)}) async-start(bf16[4,896,128]{2,1,0:T(8,128)(2,1)} %shard_map.175), calls=%async_computation.1 | async-start | bytes 1835008 | tf_op jit(solution)/shard_map/all_to_all | solution.py:273
  75.9 11.5 %collective-permute-start.8 = (bf16[80,640]{1,0:T(8,128)(2,1)S(1)}, bf16[80,640]{1,0:T(8,128)(2,1)S(1)}, u32[]{:S(2)}, u32[]{:S(2)}) collective-permute-start(bf16[80,640]{1,0:T(8,128)(2,1)S(1)} %concatenate.62), channel_id=1, source_target_pairs={{0,6},{2,0},{4,2},{6,4},{8,38},{10,32},{12,34},{14,36},{16,70},{18... | collective-permute-start | bytes 307208 | tf_op jit(solution)/shard_map/ppermute | solution.py:229
  78.4 10.3 %collective-permute-start.7 = (bf16[80,640]{1,0:T(8,128)(2,1)S(1)}, bf16[80,640]{1,0:T(8,128)(2,1)S(1)}, u32[]{:S(2)}, u32[]{:S(2)}) collective-permute-start(bf16[80,640]{1,0:T(8,128)(2,1)S(1)} %concatenate.62), channel_id=1, source_target_pairs={{0,4},{2,6},{4,0},{6,2},{8,36},{10,38},{12,32},{14,34},{16,68},{18... | collective-permute-start | bytes 307208 | tf_op jit(solution)/shard_map/ppermute | solution.py:229
  83.3 8.6 %collective-permute-start.6 = (bf16[80,640]{1,0:T(8,128)(2,1)S(1)}, bf16[80,640]{1,0:T(8,128)(2,1)S(1)}, u32[]{:S(2)}, u32[]{:S(2)}) collective-permute-start(bf16[80,640]{1,0:T(8,128)(2,1)S(1)} %concatenate.62), channel_id=1, source_target_pairs={{0,2},{2,4},{4,6},{6,0},{8,34},{10,36},{12,38},{14,32},{16,66},{18... | collective-permute-start | bytes 307208 | tf_op jit(solution)/shard_map/ppermute | solution.py:229
  86.7 5.3 %collective-permute-start.5 = (bf16[80,640]{1,0:T(8,128)(2,1)S(1)}, bf16[80,640]{1,0:T(8,128)(2,1)S(1)}, u32[]{:S(2)}, u32[]{:S(2)}) collective-permute-start(bf16[80,640]{1,0:T(8,128)(2,1)S(1)} %concatenate.62), channel_id=1, source_target_pairs={{0,0},{2,2},{4,4},{6,6},{8,32},{10,34},{12,36},{14,38},{16,64},{18... | collective-permute-start | bytes 307208 | tf_op jit(solution)/shard_map/ppermute | solution.py:229
  92.0 9.8 %collective-permute-start.9 = (bf16[4,80,640]{2,1,0:T(8,128)(2,1)S(1)}, bf16[4,80,640]{2,1,0:T(8,128)(2,1)S(1)}, u32[]{:S(2)}, u32[]{:S(2)}) collective-permute-start(bf16[4,80,640]{2,1,0:T(8,128)(2,1)S(1)} %pad_maximum_fusion.1.mine), channel_id=1, source_target_pairs={{0,1},{1,0},{2,3},{3,2},{4,5},{5,4},{6,7},{7,6},{8,9},{9,8},{10,11... | collective-permute-start | bytes 1228808 | tf_op jit(solution)/shard_map/ppermute | solution.py:246
  100.5 61.8 %copy-start = (bf16[16,32,160]{2,1,0:T(8,128)(2,1)S(1)}, bf16[16,32,160]{2,1,0:T(8,128)(2,1)}, u32[]{:S(2)}) copy-start(bf16[16,32,160]{2,1,0:T(8,128)(2,1)} %residual.1) | copy-start | bytes 491524
  100.5 61.8 %copy-start.1 = (bf16[1,32,160]{2,1,0:T(8,128)(2,1)S(1)}, bf16[1,32,160]{2,1,0:T(8,128)(2,1)}, u32[]{:S(2)}) copy-start(bf16[1,32,160]{2,1,0:T(8,128)(2,1)} %long_residual.1) | copy-start | bytes 30724
  105.9 56.4 %all-to-all-start.2 = ((bf16[4,688,128]{2,1,0:T(8,128)(2,1)}), bf16[4,688,128]{2,1,0:T(8,128)(2,1)S(1)}, u32[]{:S(2)}, u32[]{:S(2)}) async-start(bf16[4,688,128]{2,1,0:T(8,128)(2,1)} %shard_map.176), calls=%async_computation.2 | async-start | bytes 1409024 | tf_op jit(solution)/shard_map/all_to_all | solution.py:286

commit v3 on v2

--- a/solution.py
+++ b/solution.py
@@ -12,7 +12,7 @@
 KVR = 256
 TREE = 32
 ROWS = ("y", "x")
-COLS = ("z", "c")
+COLS = ("a", "b", "c")
 SWAP = [(0, 1), (1, 0)]
 BF = jnp.bfloat16
 F32 = jnp.float32
@@ -52,19 +52,18 @@
     return lax.dot_general(left, right, OVER_LAST, preferred_element_type=F32)
 
 
-def place_shards(z, c, mine, twin, target, sems):
-    copies = []
-    for j in range(4):
-        at = lax.rem(lax.rem(z, 4) + 4 - j, 4)
-        copies.append(pltpu.make_async_copy(mine.at[j], target.at[at, c], sems.at[j]))
-        copies.append(pltpu.make_async_copy(twin.at[j], target.at[at, 1 - c], sems.at[4 + j]))
+def place_shards(c, mine, twin, target, sems):
+    copies = [
+        pltpu.make_async_copy(mine, target.at[..., c, :, :], sems.at[0]),
+        pltpu.make_async_copy(twin, target.at[..., 1 - c, :, :], sems.at[1]),
+    ]
     for copy in copies:
         copy.start()
     return copies
 
 
 def attend_kernel(place, got, query_l, tree_l, mine, twin, out, kv, lat, sems):
-    copies = place_shards(place[0], place[1], mine, twin, kv, sems)
+    copies = place_shards(place[0], mine, twin, kv, sems)
     lanes = lax.broadcasted_iota(jnp.int32, (TREE, 128), 1)
     slots = lax.broadcasted_iota(jnp.int32, (1, 256), 1).astype(F32)
     scale = (NOPE + ROPE) ** -0.5
@@ -152,7 +151,7 @@
 
 
 def project_kernel(place, got, mine, twin, send, weight, rows, sems):
-    copies = place_shards(place[0], place[1], mine, twin, weight, sems)
+    copies = place_shards(place[0], mine, twin, weight, sems)
     base = 5 * TREE * (SLICE // 2)
     logs = sum(got[:, base + TREE * i : base + TREE * (i + 1)].astype(F32) for i in range(3))
     share = jnp.exp(logs - jnp.max(logs, axis=0)[None])
@@ -171,10 +170,10 @@
         rows[16 * TREE : 17 * TREE, cols] = jnp.sum(piece, axis=0).astype(BF)
     for copy in copies:
         copy.wait()
-    full = weight[...].reshape(SPAN, 640)
+    full = [weight[x].reshape(SPAN, 160) for x in range(4)]
     for x in range(4):
-        send[x, :TOKENS] = dot(rows[...], full[:, 128 * x : 128 * (x + 1)]).astype(BF)
-    rest = dot(rows[...], full[:, 512:])
+        send[x, :TOKENS] = dot(rows[...], full[x][:, :128]).astype(BF)
+    rest = dot(rows[...], jnp.concatenate([part[:, 128:] for part in full], axis=1))
     lanes = lax.broadcasted_iota(jnp.int32, (QUARTER, 128), 1) // 32
     for x in range(4):
         packed = jnp.zeros((QUARTER, 128), F32)
@@ -220,29 +219,23 @@
     return jnp.concatenate([rows[:, :128], rows[:, 128:KVR], rope, extra], axis=0)
 
 
-def fetch_slice(value, nx, nz):
-    parts = []
-    for j in range(4):
-        pairs = [
-            (i * nz + 4 * k + m, k * nz + 4 * i + (m + j) % 4) for i in range(nx) for k in range(nx) for m in range(4)
-        ]
-        parts.append(lax.ppermute(value, ("x", "z"), pairs))
-    return jnp.stack(parts)
-
-
 def on_device(
     queries, tree_latent, parents, cache, cache_lengths, accepted, residual,
     long_queries, long_tree_latent, long_parents, long_cache, long_plan, long_residual,
     key_up, value_up, out_weight,
 ):
-    nx, nz = lax.axis_size("x"), lax.axis_size("z")
-    y, x, z, c = lax.axis_index("y"), lax.axis_index("x"), lax.axis_index("z"), lax.axis_index("c")
-    place = jnp.stack([z, c]).astype(jnp.int32)
-    kv = fetch_slice(jnp.concatenate([key_up, value_up], axis=1), nx, nz)
+    nx = 4
+    y, x, c = lax.axis_index("y"), lax.axis_index("x"), lax.axis_index("c")
+    place = c.reshape(1).astype(jnp.int32)
+    kv = jnp.concatenate([key_up, value_up], axis=1)
+    pairs = [(r * 16 + z, ((z % 4) * 4 + z // 4) * 16 + (z + r) % 16) for r in range(16) for z in range(16)]
+    kv = lax.ppermute(kv, ("y", "x", "a", "b"), pairs)
+    swapped = lax.ppermute(out_weight, ("x", "a"), [(4 * i + k, 4 * k + i) for i in range(4) for k in range(4)])
+    out_rows = lax.all_gather(swapped, "b")
+    kv, out_rows = lax.optimization_barrier((kv, out_rows))
+    kv = lax.all_gather(kv, "y")
     kv_twin = lax.ppermute(kv, "c", SWAP)
-    cols = lax.all_gather(out_weight, "x")
-    cols = jnp.concatenate([cols[k, :, :128] for k in range(nx)] + [cols[k, :, 128:] for k in range(nx)], axis=1)
-    out_rows = fetch_slice(cols, nx, nz)
+    out_rows = lax.all_gather(out_rows, "a")
     out_twin = lax.ppermute(out_rows, "c", SWAP)
 
     reach = tree_reach(jnp.concatenate([parents[0], long_parents], axis=0))
@@ -253,6 +246,7 @@
     block = jnp.concatenate(
         [jnp.broadcast_to(keys[None], (nx,) + keys.shape), slice_queries(queries[0])], axis=1
     )
+    block, _ = lax.optimization_barrier((block, swapped))
     got = lax.all_to_all(block, "x", 0, 0)
     query_l = lax.dynamic_index_in_dim(slice_queries(long_queries[0]), x, 0, keepdims=False)
     tree_l = tree_block(long_tree_latent[0], reach[1] & (y == 0), lengths)
@@ -266,7 +260,7 @@
         scratch_shapes=[
             pltpu.VMEM((4, 2, shard, 2 * KVR), BF),
             pltpu.VMEM((5, SLICE * TREE, KVR), BF),
-            pltpu.SemaphoreType.DMA((8,)),
+            pltpu.SemaphoreType.DMA((2,)),
         ],
         compiler_params=PARAMS,
     )(place, got, query_l, tree_l, kv, kv_twin)
@@ -277,9 +271,9 @@
         in_specs=[SMEM, VMEM, ANY, ANY],
         out_specs=VMEM,
         scratch_shapes=[
-            pltpu.VMEM((4, 2, shard, 640), BF),
+            pltpu.VMEM((4, 4, 2, shard, 160), BF),
             pltpu.VMEM((TOKENS, SPAN), BF),
-            pltpu.SemaphoreType.DMA((8,)),
+            pltpu.SemaphoreType.DMA((2,)),
         ],
         compiler_params=PARAMS,
     )(place, shared, out_rows, out_twin)
@@ -300,7 +294,7 @@
 
 
 def solution(mesh):
-    split = Mesh(mesh.devices.reshape(4, 4, 16, 2), ("y", "x", "z", "c"))
+    split = Mesh(mesh.devices.reshape(4, 4, 4, 4, 2), ("y", "x", "a", "b", "c"))
     return jax.shard_map(
         on_device,
         mesh=split,

time: 164 us -> 140 us (0.85)
  starting transfers between devices: 92.4 us -> 40 us
  blocking collectives: 31.8 us -> 61.7 us
  local copies, waits for them, and re-layouts: 5.48 us -> 10.6 us
  waiting for transfers between devices: 16.6 us -> 12.1 us
  Pallas kernels: 10.9 us -> 7.89 us
    all_to_all x1, starting transfers between devices: 45.5 us -> 4.72 us  [on_device(): back = lax.all_to_all(send, 'x', 0, 0)]
    all_gather x1 -> x3, blocking collectives: 31.8 us -> 61.7 us  [the longest x1 33.4 us: on_device(): out_rows = lax.all_gather(out_rows, 'a')]
    ppermute x8 -> x2, starting transfers between devices: 22.5 us -> 2.1 us  [the longest x1 1.44 us: on_device(): lax.ppermute(out_weight, ('x', 'a'), [(4 * i + k, 4 * k + i) for i in ran...]
    all_to_all x1, starting transfers between devices: 4.97 us -> 19 us  [on_device(): got = lax.all_to_all(block, 'x', 0, 0)]
    ppermute x1, starting transfers between devices: 8.4 us -> 2.53 us  [on_device(): out_twin = lax.ppermute(out_rows, 'c', SWAP)]
    ppermute x8 -> x2, waiting for transfers between devices: 4.61 us -> 0.01 us  [the longest x1 0.01 us: on_device(): lax.ppermute(out_weight, ('x', 'a'), [(4 * i + k, 4 * k + i) for i in ran...]
    unnamed x33 -> x22, local copies, waits for them, and re-layouts: 0.47 us -> 5.03 us
  transfers between devices with their start and end apart: 13 -> 7, of which waited for: 5 -> 3; matrix products, arithmetic and copies ran while one was open for 2% -> 10% of each run, Pallas kernels for 0% -> 0%
where the time goes in v3:
time: 140 us; the launch traced here: 139 us
  blocking collectives  61.7 us (44%)
  starting transfers between devices  40 us (29%)
  waiting for transfers between devices  12.1 us (9%)
  local copies, waits for them, and re-layouts  10.6 us (8%)
  Pallas kernels  7.89 us (6%)
  other arithmetic  3.2 us (2%)
  between operations  2.3 us (2%)
    all_gather x1, blocking collectives, on_device(): out_rows = lax.all_gather(out_rows, 'a')  33.4 us
    all_to_all x1, starting transfers between devices, on_device(): got = lax.all_to_all(block, 'x', 0, 0)  19 us
    all_gather x1, blocking collectives, on_device(): out_rows = lax.all_gather(swapped, 'b')  14.7 us
    all_gather x1, blocking collectives, on_device(): kv = lax.all_gather(kv, 'y')  13.7 us
    all_to_all x1, waiting for transfers between devices, on_device(): back = lax.all_to_all(send, 'x', 0, 0)  9.56 us
    ppermute x1, starting transfers between devices, on_device(): kv_twin = lax.ppermute(kv, 'c', SWAP)  8.2 us
    unnamed x22, local copies, waits for them, and re-layouts  5.03 us
    all_to_all x1, starting transfers between devices, on_device(): back = lax.all_to_all(send, 'x', 0, 0)  4.72 us
  transfers between devices with their start and end apart: 7, of which 3 were waited for; matrix products, arithmetic and copies ran while one was open for 10% of the time, Pallas kernels for 0%

profile of v3, /device:TPU:1, one launch (start us, length us, event | category | flops | bytes accessed | tf_op | source)
XLA Modules:
  0.0 138.5 jit_solution(1785625009156957108)
XLA Ops:
  0.6 1.4 %collective-permute-start = (bf16[80,160]{1,0:T(8,128)(2,1)}, bf16[80,160]{1,0:T(8,128)(2,1)S(1)}, u32[]{:S(2)}, u32[]{:S(2)}) collective-permute-start(bf16[80,160]{1,0:T(8,128)(2,1)} %param.31), channel_id=1, source_target_pairs={{0,0},{8,32},{16,64},{24,96},{32,8},{40,40},{48,72},{56,104},{64,1... | collective-permute-start | bytes 76808 | tf_op jit(solution)/shard_map/ppermute | solution.py:233
  2.1 0.9 slice_dynamic-update-slice_fusion.3
  3.0 0.9 slice_dynamic-update-slice_fusion.2
  3.9 0.9 slice_dynamic-update-slice_fusion.1
  4.8 0.9 slice_dynamic-update-slice_fusion
  5.7 0.7 slice.72
  6.4 0.7 constant_dynamic-update-slice_fusion.3
  7.1 0.7 constant_dynamic-update-slice_fusion.2
  7.8 0.7 pad_add_fusion
  8.4 0.2 fusion
  8.7 0.1 fusion.1
  8.8 0.1 fusion.2
  8.9 0.1 fusion.3
  9.0 0.1 fusion.5
  10.5 1.5 %reshape_squeeze.6 = bf16[32,4,10,96]{3,2,1,0:T(8,128)(2,1)S(1)} reshape(bf16[1,32,3840]{2,1,0:T(8,128)(2,1)} %param.16) | data formatting | bytes 491520 | tf_op jit(solution)/shard_map/reshape;squeeze | solution.py:208
  12.0 0.2 slice.75
  12.2 0.3 reshape.162
  12.7 0.3 reshape.141
  12.9 0.1 pad_maximum_fusion.1
  13.1 0.1 copy.33
  13.2 0.1 constant_dynamic-update-slice_fusion.1
  13.3 0.1 pad_maximum_fusion.6
  13.4 0.2 broadcast_in_dim.11
  13.6 1.3 pad_maximum_fusion
  14.9 19.0 %all-to-all-start = ((bf16[4,1536,128]{2,1,0:T(8,128)(2,1)}), bf16[4,1536,128]{2,1,0:T(8,128)(2,1)S(1)}, u32[]{:S(2)}, u32[]{:S(2)}) async-start(bf16[4,1536,128]{2,1,0:T(8,128)(2,1)} %pad_maximum_fusion), calls=%async_computation | async-start | bytes 3145728 | tf_op jit(solution)/shard_map/all_to_all | solution.py:250
  33.9 0.7 collective-permute-start.1
  34.6 0.6 reshape_squeeze.7
  35.2 0.2 slice.77
  35.4 0.3 reshape.163
  35.8 0.3 reshape.145
  36.1 14.7 %all-gather = bf16[320,160]{1,0:T(8,128)(2,1)S(1)} all-gather(bf16[80,160]{1,0:T(8,128)(2,1)S(1)} %collective-permute-done), channel_id=2, replica_groups=mesh['y'=4,'x'=4,'a'=4,'b'=4,'c'=2] {'b'}, dimensions={0}, use_global_device_ids=true | all-gather | bytes 128000 | tf_op jit(solution)/shard_map/all_gather | solution.py:234
  50.8 13.7 %all-gather.1 = bf16[320,512]{1,0:T(8,128)(2,1)S(1)} all-gather(bf16[80,512]{1,0:T(8,128)(2,1)S(1)} %collective-permute-done.1), channel_id=3, replica_groups=mesh['y'=4,'x'=4,'a'=4,'b'=4,'c'=2] {'y'}, dimensions={0}, use_global_device_ids=true | all-gather | bytes 409600 | tf_op jit(solution)/shard_map/all_gather | solution.py:236
  64.5 8.2 %collective-permute-start.2 = (bf16[4,80,512]{2,1,0:T(8,128)(2,1)S(1)}, bf16[4,80,512]{2,1,0:T(8,128)(2,1)S(1)}, u32[]{:S(2)}, u32[]{:S(2)}) collective-permute-start(bf16[4,80,512]{2,1,0:T(8,128)(2,1)S(1)} %bitcast.55), channel_id=1, source_target_pairs={{0,1},{1,0},{2,3},{3,2},{4,5},{5,4},{6,7},{7,6},{8,9},{9,8},{10,11... | collective-permute-start | bytes 983048 | tf_op jit(solution)/shard_map/ppermute | solution.py:237
  72.7 0.1 pad_maximum_fusion.2
  72.8 0.1 copy.36
  72.9 0.1 fusion.7.tree_l
  73.0 0.9 collective-permute-done.2.twin
  73.9 4.5 %shard_map.175 = bf16[4,896,128]{2,1,0:T(8,128)(2,1)} custom-call(s32[1]{0:T(128)} %bitcast.place, bf16[4,1536,128]{2,1,0:T(8,128)(2,1)S(1)} %all-to-all-done.got, bf16[256,128]{1,0:T(8,128)(2,1)S(1)} %dynamic-slice_bitcast_fusion.query_l, bf16[128,128]{1,0:T(8,128)(2,1)S(1)} %fusion.7.tree_l, bf16[4,80,512]{2,1,0:T(8,128)(2,1)S(1)} %bitcast.56, ...), custom_call_target="tpu_custom_call" | custom-call | tf_op jit(solution)/shard_map/pallas_call | solution.py:255
  78.5 3.5 %all-to-all-start.1 = ((bf16[4,896,128]{2,1,0:T(8,128)(2,1)}), bf16[4,896,128]{2,1,0:T(8,128)(2,1)S(1)}, u32[]{:S(2)}, u32[]{:S(2)}) async-start(bf16[4,896,128]{2,1,0:T(8,128)(2,1)} %shard_map.175), calls=%async_computation.1 | async-start | bytes 1835008 | tf_op jit(solution)/shard_map/all_to_all | solution.py:267
  82.0 33.4 %all-gather.2 = bf16[16,80,160]{2,1,0:T(8,128)(2,1)S(1)} all-gather(bf16[4,80,160]{2,1,0:T(8,128)(2,1)S(1)} %bitcast.62), channel_id=4, replica_groups=mesh['y'=4,'x'=4,'a'=4,'b'=4,'c'=2] {'a'}, dimensions={0}, use_global_device_ids=true | all-gather | bytes 512000 | tf_op jit(solution)/shard_map/all_gather | solution.py:238
  115.3 2.5 %collective-permute-start.3 = (bf16[4,4,80,160]{3,2,1,0:T(8,128)(2,1)S(1)}, bf16[4,4,80,160]{3,2,1,0:T(8,128)(2,1)S(1)}, u32[]{:S(2)}, u32[]{:S(2)}) collective-permute-start(bf16[4,4,80,160]{3,2,1,0:T(8,128)(2,1)S(1)} %bitcast.53), channel_id=1, source_target_pairs={{0,1},{1,0},{2,3},{3,2},{4,5},{5,4},{6,7},{7,6},{8,9},{9,8},{10,11... | collective-permute-start | bytes 1228808 | tf_op jit(solution)/shard_map/ppermute | solution.py:239
  117.9 1.6 %collective-permute-done.3.twin = bf16[4,4,80,160]{3,2,1,0:T(8,128)(2,1)S(1)} collective-permute-done((bf16[4,4,80,160]{3,2,1,0:T(8,128)(2,1)S(1)}, bf16[4,4,80,160]{3,2,1,0:T(8,128)(2,1)S(1)}, u32[]{:S(2)}, u32[]{:S(2)}) %collective-permute-start.3) | collective-permute-done | bytes 409632 | tf_op jit(solution)/shard_map/ppermute | solution.py:239
  119.6 2.5 %shard_map.176 = bf16[4,688,128]{2,1,0:T(8,128)(2,1)} custom-call(s32[1]{0:T(128)} %bitcast.place, bf16[4,896,128]{2,1,0:T(8,128)(2,1)S(1)} %all-to-all-done.1.got, bf16[4,4,80,160]{3,2,1,0:T(8,128)(2,1)S(1)} %bitcast.54, bf16[4,4,80,160]{3,2,1,0:T(8,128)(2,1)S(1)} %collective-permute-done.3.twin), custom_call_target="tpu_custom_call" | custom-call | tf_op jit(solution)/shard_map/pallas_call | solution.py:268
  122.1 4.7 %all-to-all-start.2 = ((bf16[4,688,128]{2,1,0:T(8,128)(2,1)}), bf16[4,688,128]{2,1,0:T(8,128)(2,1)S(1)}, u32[]{:S(2)}, u32[]{:S(2)}) async-start(bf16[4,688,128]{2,1,0:T(8,128)(2,1)} %shard_map.176), calls=%async_computation.2 | async-start | bytes 1409024 | tf_op jit(solution)/shard_map/all_to_all | solution.py:280
  126.8 0.6 gather_fusion
  127.4 0.7 bitcast_select_fusion
  128.1 9.6 %all-to-all-done.2.got = bf16[4,688,128]{2,1,0:T(8,128)(2,1)S(1)} async-done(((bf16[4,688,128]{2,1,0:T(8,128)(2,1)}), bf16[4,688,128]{2,1,0:T(8,128)(2,1)S(1)}, u32[]{:S(2)}, u32[]{:S(2)}) %all-to-all-start.2) | async-done | bytes 704544 | tf_op jit(solution)/shard_map/all_to_all | solution.py:280
  137.7 0.9 shard_map.177
  (39 shorter events, 0.3 us)
Async XLA Ops:
  0.6 14.3 %collective-permute-start = (bf16[80,160]{1,0:T(8,128)(2,1)}, bf16[80,160]{1,0:T(8,128)(2,1)S(1)}, u32[]{:S(2)}, u32[]{:S(2)}) collective-permute-start(bf16[80,160]{1,0:T(8,128)(2,1)} %param.31), channel_id=1, source_target_pairs={{0,0},{8,32},{16,64},{24,96},{32,8},{40,40},{48,72},{56,104},{64,1... | collective-permute-start | bytes 76808 | tf_op jit(solution)/shard_map/ppermute | solution.py:233
  14.9 19.0 %copy-start.4 = (bf16[80,256]{1,0:T(8,128)(2,1)S(1)}, bf16[80,256]{1,0:T(8,128)(2,1)}, u32[]{:S(2)}) copy-start(bf16[80,256]{1,0:T(8,128)(2,1)} %param.30) | copy-start | bytes 122884
  14.9 19.0 %copy-start.5 = (bf16[80,256]{1,0:T(8,128)(2,1)S(1)}, bf16[80,256]{1,0:T(8,128)(2,1)}, u32[]{:S(2)}) copy-start(bf16[80,256]{1,0:T(8,128)(2,1)} %param.29) | copy-start | bytes 122884
  14.9 19.7 %copy-start.6 = (bf16[1,32,288]{2,1,0:T(8,128)(2,1)S(1)}, bf16[1,32,288]{2,1,0:T(8,128)(2,1)}, u32[]{:S(2)}) copy-start(bf16[1,32,288]{2,1,0:T(8,128)(2,1)} %param.24) | copy-start | bytes 55300
  14.9 19.7 %copy-start.2 = (bf16[1,32,3840]{2,1,0:T(8,128)(2,1)S(1)}, bf16[1,32,3840]{2,1,0:T(8,128)(2,1)}, u32[]{:S(2)}) copy-start(bf16[1,32,3840]{2,1,0:T(8,128)(2,1)} %param.23) | copy-start | bytes 737284
  14.9 59.0 %all-to-all-start = ((bf16[4,1536,128]{2,1,0:T(8,128)(2,1)}), bf16[4,1536,128]{2,1,0:T(8,128)(2,1)S(1)}, u32[]{:S(2)}, u32[]{:S(2)}) async-start(bf16[4,1536,128]{2,1,0:T(8,128)(2,1)} %pad_maximum_fusion), calls=%async_computation | async-start | bytes 3145728 | tf_op jit(solution)/shard_map/all_to_all | solution.py:250
  33.9 17.0 %collective-permute-start.1 = (bf16[80,512]{1,0:T(8,128)(2,1)S(1)}, bf16[80,512]{1,0:T(8,128)(2,1)S(1)}, u32[]{:S(2)}, u32[]{:S(2)}) collective-permute-start(bf16[80,512]{1,0:T(8,128)(2,1)S(1)} %pad_maximum_fusion.3), channel_id=1, source_target_pairs={{0,0},{2,130},{4,260},{6,390},{8,40},{10,170},{12,300},{14,430},{1... | collective-permute-start | bytes 245768 | tf_op jit(solution)/shard_map/ppermute | solution.py:232
  64.5 9.4 %collective-permute-start.2 = (bf16[4,80,512]{2,1,0:T(8,128)(2,1)S(1)}, bf16[4,80,512]{2,1,0:T(8,128)(2,1)S(1)}, u32[]{:S(2)}, u32[]{:S(2)}) collective-permute-start(bf16[4,80,512]{2,1,0:T(8,128)(2,1)S(1)} %bitcast.55), channel_id=1, source_target_pairs={{0,1},{1,0},{2,3},{3,2},{4,5},{5,4},{6,7},{7,6},{8,9},{9,8},{10,11... | collective-permute-start | bytes 983048 | tf_op jit(solution)/shard_map/ppermute | solution.py:237
  78.4 39.4 %copy-start.7 = (s32[1,1,8]{2,1,0:T(1,128)S(1)}, s32[1,1,8]{2,1,0:T(1,128)}, u32[]{:S(2)}) copy-start(s32[1,1,8]{2,1,0:T(1,128)} %param.21) | copy-start | bytes 100
  78.5 41.1 %all-to-all-start.1 = ((bf16[4,896,128]{2,1,0:T(8,128)(2,1)}), bf16[4,896,128]{2,1,0:T(8,128)(2,1)S(1)}, u32[]{:S(2)}, u32[]{:S(2)}) async-start(bf16[4,896,128]{2,1,0:T(8,128)(2,1)} %shard_map.175), calls=%async_computation.1 | async-start | bytes 1835008 | tf_op jit(solution)/shard_map/all_to_all | solution.py:267
  115.3 4.2 %collective-permute-start.3 = (bf16[4,4,80,160]{3,2,1,0:T(8,128)(2,1)S(1)}, bf16[4,4,80,160]{3,2,1,0:T(8,128)(2,1)S(1)}, u32[]{:S(2)}, u32[]{:S(2)}) collective-permute-start(bf16[4,4,80,160]{3,2,1,0:T(8,128)(2,1)S(1)} %bitcast.53), channel_id=1, source_target_pairs={{0,1},{1,0},{2,3},{3,2},{4,5},{5,4},{6,7},{7,6},{8,9},{9,8},{10,11... | collective-permute-start | bytes 1228808 | tf_op jit(solution)/shard_map/ppermute | solution.py:239
  117.9 8.9 %copy-start.3 = (bf16[1,32,288]{2,1,0:T(8,128)(2,1)S(1)}, bf16[1,32,288]{2,1,0:T(8,128)(2,1)}, u32[]{:S(2)}) copy-start(bf16[1,32,288]{2,1,0:T(8,128)(2,1)} %param.17) | copy-start | bytes 55300
  117.9 19.7 %copy-start = (bf16[16,32,160]{2,1,0:T(8,128)(2,1)S(1)}, bf16[16,32,160]{2,1,0:T(8,128)(2,1)}, u32[]{:S(2)}) copy-start(bf16[16,32,160]{2,1,0:T(8,128)(2,1)} %residual.1) | copy-start | bytes 491524
  117.9 19.7 %copy-start.1 = (bf16[1,32,160]{2,1,0:T(8,128)(2,1)S(1)}, bf16[1,32,160]{2,1,0:T(8,128)(2,1)}, u32[]{:S(2)}) copy-start(bf16[1,32,160]{2,1,0:T(8,128)(2,1)} %long_residual.1) | copy-start | bytes 30724
  122.1 15.6 %all-to-all-start.2 = ((bf16[4,688,128]{2,1,0:T(8,128)(2,1)}), bf16[4,688,128]{2,1,0:T(8,128)(2,1)S(1)}, u32[]{:S(2)}, u32[]{:S(2)}) async-start(bf16[4,688,128]{2,1,0:T(8,128)(2,1)} %shard_map.176), calls=%async_computation.2 | async-start | bytes 1409024 | tf_op jit(solution)/shard_map/all_to_all | solution.py:280

commit v4 on v3

--- a/solution.py
+++ b/solution.py
@@ -151,7 +151,13 @@
 
 
 def project_kernel(place, got, mine, twin, send, weight, rows, sems):
-    copies = place_shards(place[0], mine, twin, weight, sems)
+    c, a = place[0], place[2]
+    copies = []
+    for k in range(5):
+        copies.append(pltpu.make_async_copy(mine.at[:, k], weight.at[k, :, c], sems.at[k]))
+        copies.append(pltpu.make_async_copy(twin.at[:, k], weight.at[k, :, 1 - c], sems.at[5 + k]))
+    for copy in copies:
+        copy.start()
     base = 5 * TREE * (SLICE // 2)
     logs = sum(got[:, base + TREE * i : base + TREE * (i + 1)].astype(F32) for i in range(3))
     share = jnp.exp(logs - jnp.max(logs, axis=0)[None])
@@ -170,16 +176,15 @@
         rows[16 * TREE : 17 * TREE, cols] = jnp.sum(piece, axis=0).astype(BF)
     for copy in copies:
         copy.wait()
-    full = [weight[x].reshape(SPAN, 160) for x in range(4)]
-    for x in range(4):
-        send[x, :TOKENS] = dot(rows[...], full[x][:, :128]).astype(BF)
-    rest = dot(rows[...], jnp.concatenate([part[:, 128:] for part in full], axis=1))
+    rest = dot(rows[...], weight[4].reshape(SPAN, 128))
     lanes = lax.broadcasted_iota(jnp.int32, (QUARTER, 128), 1) // 32
-    for x in range(4):
+    for k in range(4):
+        x = lax.rem(a + 4 - k, 4)
+        send[x, :TOKENS] = dot(rows[...], weight[k].reshape(SPAN, 128)).astype(BF)
         packed = jnp.zeros((QUARTER, 128), F32)
         for g in range(4):
             part = rest[QUARTER * g : QUARTER * (g + 1)]
-            shift = (32 * (g - x)) % 128
+            shift = (32 * (g - k)) % 128
             part = pltpu.roll(part, shift, 1) if shift else part
             packed = jnp.where(lanes == g, part, packed)
         send[x, TOKENS : TOKENS + QUARTER] = packed.astype(BF)
@@ -204,19 +209,64 @@
 PARAMS = pltpu.CompilerParams(vmem_limit_bytes=48 << 20)
 
 
-def slice_queries(queries):
-    heads = queries.reshape(TREE, 4, SLICE, NOPE + ROPE)
-    nope = heads[..., :NOPE].reshape(TREE, 4, SLICE // 2, 128).transpose(1, 2, 0, 3)
-    rope = heads[..., NOPE:].reshape(TREE, 4, SLICE * ROPE)
-    rope = jnp.pad(rope, ((0, 0), (0, 0), (0, 64))).reshape(TREE, 4, 3, 128).transpose(1, 2, 0, 3)
-    return jnp.concatenate([nope, rope], axis=1).reshape(4, 8 * TREE, 128)
-
-
-def tree_block(rows, reach, lengths):
-    extra = jnp.concatenate([reach.astype(BF), jnp.broadcast_to(lengths.astype(BF)[None], (TREE, 2))], axis=1)
-    extra = jnp.pad(extra, ((0, 0), (0, 128 - extra.shape[1])))
-    rope = jnp.concatenate([rows[:, KVR:]] * 4, axis=1)
-    return jnp.concatenate([rows[:, :128], rows[:, 128:KVR], rope, extra], axis=0)
+def onehot(rows, cols, match):
+    row = lax.broadcasted_iota(jnp.int32, (rows, cols), 0)
+    col = lax.broadcasted_iota(jnp.int32, (rows, cols), 1)
+    return jnp.where(match(row, col), 1.0, 0.0).astype(BF)
+
+
+def pack_kernel(place, lengths, queries, queries_l, keys, keys_l, tree, tree_l, reach, block, own_q, own_tree, slices):
+    for d in range(4):
+        block[d, 0:288] = keys[:, :128]
+        block[d, 288:576] = keys[:, 128:]
+        block[d, 576:864] = keys_l[:, :128]
+        block[d, 864:1152] = keys_l[:, 128:]
+    lanes = lax.broadcasted_iota(jnp.int32, (TREE, 128), 1)
+    tile4 = onehot(TREE, 128, lambda row, col: col % 32 == row)
+    widen = onehot(TREE, 128, lambda row, col: col == row)
+    for i, rows in enumerate((tree, tree_l)):
+        extra = dot(reach[i], widen)
+        extra = jnp.where(lanes == 32, lengths[0].astype(F32), extra)
+        extra = jnp.where(lanes == 33, lengths[1].astype(F32), extra).astype(BF)
+        parts = (rows[:, :128], rows[:, 128:KVR], dot(rows[:, KVR:], tile4).astype(BF), extra)
+        for k, part in enumerate(parts):
+            at = slice(TREE * k, TREE * (k + 1))
+            if i == 0:
+                for d in range(4):
+                    block[d, TREE_AT + at.start : TREE_AT + at.stop] = part
+            else:
+                own_tree[at] = part
+
+    def source(col):
+        nope = 96 * (col // NOPE) + col % NOPE
+        rope = 96 * ((col - 256) // ROPE) + NOPE + (col - 256) % ROPE
+        return jnp.where(col < 256, nope, rope)
+
+    sort = onehot(384, 384, lambda row, col: source(col) == row)
+    rope = []
+    for w in range(HEADS // 4):
+        cols = slice(384 * w, 384 * (w + 1))
+        moved = dot(jnp.concatenate([queries[:, cols], queries_l[:, cols]], axis=0), sort)
+        rope.append(moved[:, 256:])
+        for half in range(2):
+            s, p = divmod(2 * w + half, SLICE // 2)
+            part = moved[:, 128 * half : 128 * (half + 1)].astype(BF)
+            block[s, QUERY_AT + TREE * p : QUERY_AT + TREE * (p + 1)] = part[:TREE]
+            slices[s, TREE * p : TREE * (p + 1)] = part[TREE:]
+    wide = lax.broadcasted_iota(jnp.int32, (2 * TREE, 128), 1)
+    for s in range(4):
+        first = SLICE * s // 4
+        for k in range(3):
+            if s % 2 == 0:
+                part = rope[first + k]
+            else:
+                after = pltpu.roll(rope[first + k + 1], 64, 1) if k < 2 else jnp.zeros((2 * TREE, 128), F32)
+                part = jnp.where(wide < 64, pltpu.roll(rope[first + k], 64, 1), after)
+            part = part.astype(BF)
+            at = TREE * (5 + k)
+            block[s, QUERY_AT + at : QUERY_AT + at + TREE] = part[:TREE]
+            slices[s, at : at + TREE] = part[TREE:]
+    own_q[...] = slices[place[1]]
 
 
 def on_device(
@@ -224,33 +274,42 @@
     long_queries, long_tree_latent, long_parents, long_cache, long_plan, long_residual,
     key_up, value_up, out_weight,
 ):
-    nx = 4
-    y, x, c = lax.axis_index("y"), lax.axis_index("x"), lax.axis_index("c")
-    place = c.reshape(1).astype(jnp.int32)
+    y, x, a, c = lax.axis_index("y"), lax.axis_index("x"), lax.axis_index("a"), lax.axis_index("c")
+    place = jnp.stack([c, x, a]).astype(jnp.int32)
+    shard = key_up.shape[0]
     kv = jnp.concatenate([key_up, value_up], axis=1)
     pairs = [(r * 16 + z, ((z % 4) * 4 + z // 4) * 16 + (z + r) % 16) for r in range(16) for z in range(16)]
     kv = lax.ppermute(kv, ("y", "x", "a", "b"), pairs)
-    swapped = lax.ppermute(out_weight, ("x", "a"), [(4 * i + k, 4 * k + i) for i in range(4) for k in range(4)])
-    out_rows = lax.all_gather(swapped, "b")
-    kv, out_rows = lax.optimization_barrier((kv, out_rows))
+    moved = [
+        lax.ppermute(out_weight, ("x", "a"), [(4 * i + j, 4 * j + (i + k) % 4) for i in range(4) for j in range(4)])
+        for k in range(4)
+    ]
+    reach = tree_reach(jnp.concatenate([parents[0], long_parents], axis=0))
+    reach = (reach & ((jnp.arange(2) == 0) | (y == 0))[:, None, None]).astype(BF)
+    lengths = jnp.concatenate([cache_lengths[0], long_plan[0]])
+    rows = 8 * TREE
+    block, query_l, tree_l = pl.pallas_call(
+        pack_kernel,
+        out_shape=(
+            jax.ShapeDtypeStruct((4, BLOCK, 128), BF),
+            jax.ShapeDtypeStruct((rows, 128), BF),
+            jax.ShapeDtypeStruct((4 * TREE, 128), BF),
+        ),
+        in_specs=[SMEM, SMEM] + [VMEM] * 7,
+        out_specs=(VMEM, VMEM, VMEM),
+        scratch_shapes=[pltpu.VMEM((4, rows, 128), BF)],
+        compiler_params=PARAMS,
+    )(
+        place, lengths, queries[0], long_queries[0], cache[0, 0].T, long_cache[0].T,
+        tree_latent[0], long_tree_latent[0], reach,
+    )
+    block, kv, *moved = lax.optimization_barrier((block, kv, *moved))
+    got = lax.all_to_all(block, "x", 0, 0)
     kv = lax.all_gather(kv, "y")
     kv_twin = lax.ppermute(kv, "c", SWAP)
-    out_rows = lax.all_gather(out_rows, "a")
+    tails = jnp.concatenate([part[:, 128:] for part in moved], axis=1)
+    out_rows = lax.all_gather(jnp.stack([part[:, :128] for part in moved] + [tails]), "b")
     out_twin = lax.ppermute(out_rows, "c", SWAP)
-
-    reach = tree_reach(jnp.concatenate([parents[0], long_parents], axis=0))
-    lengths = jnp.concatenate([cache_lengths[0], long_plan[0]])
-    short_t, long_t = cache[0, 0].T, long_cache[0].T
-    keys = jnp.concatenate([short_t[:, :128], short_t[:, 128:], long_t[:, :128], long_t[:, 128:]], axis=0)
-    keys = jnp.concatenate([keys, tree_block(tree_latent[0], reach[0], lengths)], axis=0)
-    block = jnp.concatenate(
-        [jnp.broadcast_to(keys[None], (nx,) + keys.shape), slice_queries(queries[0])], axis=1
-    )
-    block, _ = lax.optimization_barrier((block, swapped))
-    got = lax.all_to_all(block, "x", 0, 0)
-    query_l = lax.dynamic_index_in_dim(slice_queries(long_queries[0]), x, 0, keepdims=False)
-    tree_l = tree_block(long_tree_latent[0], reach[1] & (y == 0), lengths)
-    shard = key_up.shape[0]
 
     heads = pl.pallas_call(
         attend_kernel,
@@ -271,9 +330,9 @@
         in_specs=[SMEM, VMEM, ANY, ANY],
         out_specs=VMEM,
         scratch_shapes=[
-            pltpu.VMEM((4, 4, 2, shard, 160), BF),
+            pltpu.VMEM((5, 4, 2, shard, 128), BF),
             pltpu.VMEM((TOKENS, SPAN), BF),
-            pltpu.SemaphoreType.DMA((2,)),
+            pltpu.SemaphoreType.DMA((10,)),
         ],
         compiler_params=PARAMS,
     )(place, shared, out_rows, out_twin)

time: 140 us -> 123 us (0.88)
  blocking collectives: 61.7 us -> 23.1 us
  starting transfers between devices: 40 us -> 63.4 us
  local copies, waits for them, and re-layouts: 10.6 us -> 5.83 us
  Pallas kernels: 7.89 us -> 11.6 us
    all_gather x2 -> x1, blocking collectives: 48.1 us -> 12.7 us  [on_device(): lax.all_gather(jnp.stack([part[:, :128] for part in moved] + [tails]), 'b')]
    ppermute x1 -> x4, starting transfers between devices: 1.44 us -> 34.9 us  [on_device(): lax.ppermute(out_weight, ('x', 'a'), [(4 * i + j, 4 * j + (i + k) % 4) fo...]
    all_to_all x1, starting transfers between devices: 19 us -> 6.56 us  [on_device(): got = lax.all_to_all(block, 'x', 0, 0)]
    ppermute x1, starting transfers between devices: 2.53 us -> 8.04 us  [on_device(): out_twin = lax.ppermute(out_rows, 'c', SWAP)]
    all_gather x1, blocking collectives: 13.7 us -> 10.4 us  [on_device(): kv = lax.all_gather(kv, 'y')]
    pallas_call x0 -> x1, Pallas kernels: none -> 2.47 us  [on_device(): pl.pallas_call(pack_kernel, out_shape=(jax.ShapeDtypeStruct((4, BLOCK, 12...]
    another operation x2 -> x0, local copies, waits for them, and re-layouts: 2.11 us -> none  [slice_queries(): heads = queries.reshape(TREE, 4, SLICE, NOPE + ROPE)]
    ppermute x1, starting transfers between devices: 8.2 us -> 6.23 us  [on_device(): kv_twin = lax.ppermute(kv, 'c', SWAP)]
  transfers between devices with their start and end apart: 7 -> 10, of which waited for: 3 -> 4; matrix products, arithmetic and copies ran while one was open for 10% -> 3% of each run, Pallas kernels for 0% -> 2%
where the time goes in v4:
time: 123 us; the launch traced here: 122 us
  starting transfers between devices  63.4 us (52%)
  blocking collectives  23.1 us (19%)
  waiting for transfers between devices  12.9 us (10%)
  Pallas kernels  11.6 us (9%)
  local copies, waits for them, and re-layouts  5.83 us (5%)
  other arithmetic  2.44 us (2%)
  between operations  2.19 us (2%)
    ppermute x4, starting transfers between devices, on_device(): lax.ppermute(out_weight, ('x', 'a'), [(4 * i + j, 4 * j + (i + k) % 4) fo...  34.9 us
    all_gather x1, blocking collectives, on_device(): lax.all_gather(jnp.stack([part[:, :128] for part in moved] + [tails]), 'b')  12.7 us
    all_gather x1, blocking collectives, on_device(): kv = lax.all_gather(kv, 'y')  10.4 us
    all_to_all x1, waiting for transfers between devices, on_device(): back = lax.all_to_all(send, 'x', 0, 0)  9.85 us
    ppermute x1, starting transfers between devices, on_device(): out_twin = lax.ppermute(out_rows, 'c', SWAP)  8.04 us
    all_to_all x1, starting transfers between devices, on_device(): got = lax.all_to_all(block, 'x', 0, 0)  6.56 us
    ppermute x1, starting transfers between devices, on_device(): kv_twin = lax.ppermute(kv, 'c', SWAP)  6.23 us
    unnamed x24, local copies, waits for them, and re-layouts  5.24 us
  transfers between devices with their start and end apart: 10, of which 4 were waited for; matrix products, arithmetic and copies ran while one was open for 3% of the time, Pallas kernels for 2%

profile of v4, /device:TPU:1, one launch (start us, length us, event | category | flops | bytes accessed | tf_op | source)
XLA Modules:
  0.0 122.2 jit_solution(5552487895125535153)
XLA Ops:
  0.6 1.4 %collective-permute-start.1 = (bf16[80,160]{1,0:T(8,128)(2,1)}, bf16[80,160]{1,0:T(8,128)(2,1)S(1)}, u32[]{:S(2)}, u32[]{:S(2)}) collective-permute-start(bf16[80,160]{1,0:T(8,128)(2,1)} %param.31), channel_id=1, source_target_pairs={{0,0},{8,32},{16,64},{24,96},{32,8},{40,40},{48,72},{56,104},{64,1... | collective-permute-start | bytes 76808 | tf_op jit(solution)/shard_map/ppermute | solution.py:284
  2.1 10.1 %collective-permute-start.2 = (bf16[80,160]{1,0:T(8,128)(2,1)}, bf16[80,160]{1,0:T(8,128)(2,1)S(1)}, u32[]{:S(2)}, u32[]{:S(2)}) collective-permute-start(bf16[80,160]{1,0:T(8,128)(2,1)} %param.31), channel_id=1, source_target_pairs={{0,8},{8,40},{16,72},{24,104},{32,16},{40,48},{48,80},{56,112},{64... | collective-permute-start | bytes 76808 | tf_op jit(solution)/shard_map/ppermute | solution.py:284
  12.2 16.3 %collective-permute-start.3 = (bf16[80,160]{1,0:T(8,128)(2,1)}, bf16[80,160]{1,0:T(8,128)(2,1)S(1)}, u32[]{:S(2)}, u32[]{:S(2)}) collective-permute-start(bf16[80,160]{1,0:T(8,128)(2,1)} %param.31), channel_id=1, source_target_pairs={{0,16},{8,48},{16,80},{24,112},{32,24},{40,56},{48,88},{56,120},{6... | collective-permute-start | bytes 76808 | tf_op jit(solution)/shard_map/ppermute | solution.py:284
  28.5 7.0 %collective-permute-start.4 = (bf16[80,160]{1,0:T(8,128)(2,1)}, bf16[80,160]{1,0:T(8,128)(2,1)S(1)}, u32[]{:S(2)}, u32[]{:S(2)}) collective-permute-start(bf16[80,160]{1,0:T(8,128)(2,1)} %param.31), channel_id=1, source_target_pairs={{0,24},{8,56},{16,88},{24,120},{32,0},{40,32},{48,64},{56,96},{64,... | collective-permute-start | bytes 76808 | tf_op jit(solution)/shard_map/ppermute | solution.py:284
  35.5 0.8 pad_maximum_fusion
  36.3 0.7 collective-permute-start
  38.3 0.7 pad_add_fusion
  39.0 0.2 fusion
  39.2 0.1 fusion.1
  39.3 0.1 fusion.2
  39.5 0.1 fusion.3
  39.6 0.1 pad_add_fusion.2.lengths
  39.7 0.1 fusion.7.reach
  39.8 0.1 pad_add_fusion.1.place
  39.9 0.9 copy-done.1
  40.8 0.9 copy-done.2
  41.8 0.7 copy-done.3
  42.5 0.9 copy-done.5
  43.4 0.9 copy-done.6
  44.3 0.7 copy-done.7
  45.1 2.5 %shard_map.175 = (bf16[4,1536,128]{2,1,0:T(8,128)(2,1)}, bf16[256,128]{1,0:T(8,128)(2,1)S(1)}, bf16[128,128]{1,0:T(8,128)(2,1)S(1)}) custom-call(s32[3]{0:T(128)S(1)} %pad_add_fusion.1.place, s32[2]{0:T(128)S(1)} %pad_add_fusion.2.lengths, bf16[32,3840]{1,0:T(8,128)(2,1)S(1)} %bitcast.52, bf16[32,3840]{1,0:T(8,128)(2,1)S(1)} %bitcast.53, ...), custom_call_target="tpu_custom_call" | custom-call | tf_op jit(solution)/shard_map/pallas_call | solution.py:291
  47.5 0.0 collective-permute-done.1
  47.5 0.0 collective-permute-done.2
  47.5 0.0 collective-permute-done.3
  47.5 0.0 collective-permute-done.4
  47.6 0.0 collective-permute-done
  47.6 6.6 %all-to-all-start = ((bf16[4,1536,128]{2,1,0:T(8,128)(2,1)}), bf16[4,1536,128]{2,1,0:T(8,128)(2,1)S(1)}, u32[]{:S(2)}, u32[]{:S(2)}) async-start(bf16[4,1536,128]{2,1,0:T(8,128)(2,1)} %get-tuple-element.15), calls=%async_computation | async-start | bytes 3145728 | tf_op jit(solution)/shard_map/all_to_all | solution.py:307
  54.1 10.4 %all-gather = bf16[320,512]{1,0:T(8,128)(2,1)S(1)} all-gather(bf16[80,512]{1,0:T(8,128)(2,1)S(1)} %collective-permute-done), channel_id=2, replica_groups=mesh['y'=4,'x'=4,'a'=4,'b'=4,'c'=2] {'y'}, dimensions={0}, use_global_device_ids=true | all-gather | bytes 409600 | tf_op jit(solution)/shard_map/all_gather | solution.py:308
  64.5 6.2 %collective-permute-start.5 = (bf16[4,80,512]{2,1,0:T(8,128)(2,1)S(1)}, bf16[4,80,512]{2,1,0:T(8,128)(2,1)S(1)}, u32[]{:S(2)}, u32[]{:S(2)}) collective-permute-start(bf16[4,80,512]{2,1,0:T(8,128)(2,1)S(1)} %bitcast.50), channel_id=1, source_target_pairs={{0,1},{1,0},{2,3},{3,2},{4,5},{5,4},{6,7},{7,6},{8,9},{9,8},{10,11... | collective-permute-start | bytes 983048 | tf_op jit(solution)/shard_map/ppermute | solution.py:309
  70.8 1.2 collective-permute-done.5.twin
  72.0 0.5 all-to-all-done.got
  72.5 5.1 %shard_map.176 = bf16[4,896,128]{2,1,0:T(8,128)(2,1)} custom-call(s32[3]{0:T(128)S(1)} %pad_add_fusion.1.place, bf16[4,1536,128]{2,1,0:T(8,128)(2,1)S(1)} %all-to-all-done.got, bf16[256,128]{1,0:T(8,128)(2,1)S(1)} %get-tuple-element.16.query_l, bf16[128,128]{1,0:T(8,128)(2,1)S(1)} %get-tuple-element.17.tree_l, bf16[4,80,512]{2,1,0:T(8,128)(2,1)S(1)} %bitcast.51, ...), custom_call_target="tpu_custom_call" | custom-call | tf_op jit(solution)/shard_map/pallas_call | solution.py:314
  77.6 0.0 copy-start.9
  77.6 3.5 %all-to-all-start.1 = ((bf16[4,896,128]{2,1,0:T(8,128)(2,1)}), bf16[4,896,128]{2,1,0:T(8,128)(2,1)S(1)}, u32[]{:S(2)}, u32[]{:S(2)}) async-start(bf16[4,896,128]{2,1,0:T(8,128)(2,1)} %shard_map.176), calls=%async_computation.1 | async-start | bytes 1835008 | tf_op jit(solution)/shard_map/all_to_all | solution.py:326
  81.2 0.1 fusion.10
  81.3 12.7 %all-gather.1 = bf16[20,80,128]{2,1,0:T(8,128)(2,1)S(1)} all-gather(bf16[5,80,128]{2,1,0:T(8,128)(2,1)S(1)} %fusion.10), channel_id=3, replica_groups=mesh['y'=4,'x'=4,'a'=4,'b'=4,'c'=2] {'b'}, dimensions={0}, use_global_device_ids=true | all-gather | bytes 512000 | tf_op jit(solution)/shard_map/all_gather | solution.py:311
  94.0 8.0 %collective-permute-start.6 = (bf16[4,5,80,128]{3,2,1,0:T(8,128)(2,1)S(1)}, bf16[4,5,80,128]{3,2,1,0:T(8,128)(2,1)S(1)}, u32[]{:S(2)}, u32[]{:S(2)}) collective-permute-start(bf16[4,5,80,128]{3,2,1,0:T(8,128)(2,1)S(1)} %bitcast.48), channel_id=1, source_target_pairs={{0,1},{1,0},{2,3},{3,2},{4,5},{5,4},{6,7},{7,6},{8,9},{9,8},{10,11... | collective-permute-start | bytes 1228808 | tf_op jit(solution)/shard_map/ppermute | solution.py:312
  102.1 0.0 copy-start.4
  102.1 0.0 copy-start
  102.1 0.0 copy-start.8
  102.1 1.3 %collective-permute-done.6.twin = bf16[4,5,80,128]{3,2,1,0:T(8,128)(2,1)S(1)} collective-permute-done((bf16[4,5,80,128]{3,2,1,0:T(8,128)(2,1)S(1)}, bf16[4,5,80,128]{3,2,1,0:T(8,128)(2,1)S(1)}, u32[]{:S(2)}, u32[]{:S(2)}) %collective-permute-start.6) | collective-permute-done | bytes 409632 | tf_op jit(solution)/shard_map/ppermute | solution.py:312
  103.4 0.0 all-to-all-done.1.got
  103.4 3.2 %shard_map.177 = bf16[4,688,128]{2,1,0:T(8,128)(2,1)} custom-call(s32[3]{0:T(128)S(1)} %pad_add_fusion.1.place, bf16[4,896,128]{2,1,0:T(8,128)(2,1)S(1)} %all-to-all-done.1.got, bf16[4,5,80,128]{3,2,1,0:T(8,128)(2,1)S(1)} %bitcast.49, bf16[4,5,80,128]{3,2,1,0:T(8,128)(2,1)S(1)} %collective-permute-done.6.twin), custom_call_target="tpu_custom_call" | custom-call | tf_op jit(solution)/shard_map/pallas_call | solution.py:327
  106.7 3.5 %all-to-all-start.2 = ((bf16[4,688,128]{2,1,0:T(8,128)(2,1)}), bf16[4,688,128]{2,1,0:T(8,128)(2,1)S(1)}, u32[]{:S(2)}, u32[]{:S(2)}) async-start(bf16[4,688,128]{2,1,0:T(8,128)(2,1)} %shard_map.177), calls=%async_computation.2 | async-start | bytes 1409024 | tf_op jit(solution)/shard_map/all_to_all | solution.py:339
  110.2 0.6 gather_fusion
  110.8 0.7 bitcast_select_fusion
  111.4 9.8 %all-to-all-done.2.got = bf16[4,688,128]{2,1,0:T(8,128)(2,1)S(1)} async-done(((bf16[4,688,128]{2,1,0:T(8,128)(2,1)}), bf16[4,688,128]{2,1,0:T(8,128)(2,1)S(1)}, u32[]{:S(2)}, u32[]{:S(2)}) %all-to-all-start.2) | async-done | bytes 704544 | tf_op jit(solution)/shard_map/all_to_all | solution.py:339
  121.3 0.9 shard_map.178
  (23 shorter events, 0.1 us)
Async XLA Ops:
  0.6 46.9 %collective-permute-start.1 = (bf16[80,160]{1,0:T(8,128)(2,1)}, bf16[80,160]{1,0:T(8,128)(2,1)S(1)}, u32[]{:S(2)}, u32[]{:S(2)}) collective-permute-start(bf16[80,160]{1,0:T(8,128)(2,1)} %param.31), channel_id=1, source_target_pairs={{0,0},{8,32},{16,64},{24,96},{32,8},{40,40},{48,72},{56,104},{64,1... | collective-permute-start | bytes 76808 | tf_op jit(solution)/shard_map/ppermute | solution.py:284
  2.1 45.5 %collective-permute-start.2 = (bf16[80,160]{1,0:T(8,128)(2,1)}, bf16[80,160]{1,0:T(8,128)(2,1)S(1)}, u32[]{:S(2)}, u32[]{:S(2)}) collective-permute-start(bf16[80,160]{1,0:T(8,128)(2,1)} %param.31), channel_id=1, source_target_pairs={{0,8},{8,40},{16,72},{24,104},{32,16},{40,48},{48,80},{56,112},{64... | collective-permute-start | bytes 76808 | tf_op jit(solution)/shard_map/ppermute | solution.py:284
  12.2 35.3 %collective-permute-start.3 = (bf16[80,160]{1,0:T(8,128)(2,1)}, bf16[80,160]{1,0:T(8,128)(2,1)S(1)}, u32[]{:S(2)}, u32[]{:S(2)}) collective-permute-start(bf16[80,160]{1,0:T(8,128)(2,1)} %param.31), channel_id=1, source_target_pairs={{0,16},{8,48},{16,80},{24,112},{32,24},{40,56},{48,88},{56,120},{6... | collective-permute-start | bytes 76808 | tf_op jit(solution)/shard_map/ppermute | solution.py:284
  28.5 19.0 %collective-permute-start.4 = (bf16[80,160]{1,0:T(8,128)(2,1)}, bf16[80,160]{1,0:T(8,128)(2,1)S(1)}, u32[]{:S(2)}, u32[]{:S(2)}) collective-permute-start(bf16[80,160]{1,0:T(8,128)(2,1)} %param.31), channel_id=1, source_target_pairs={{0,24},{8,56},{16,88},{24,120},{32,0},{40,32},{48,64},{56,96},{64,... | collective-permute-start | bytes 76808 | tf_op jit(solution)/shard_map/ppermute | solution.py:284
  36.3 11.2 %collective-permute-start = (bf16[80,512]{1,0:T(8,128)(2,1)S(1)}, bf16[80,512]{1,0:T(8,128)(2,1)S(1)}, u32[]{:S(2)}, u32[]{:S(2)}) collective-permute-start(bf16[80,512]{1,0:T(8,128)(2,1)S(1)} %pad_maximum_fusion), channel_id=1, source_target_pairs={{0,0},{2,130},{4,260},{6,390},{8,40},{10,170},{12,300},{14,430},{1... | collective-permute-start | bytes 245768 | tf_op jit(solution)/shard_map/ppermute | solution.py:282
  39.9 0.9 copy-start.1
  40.8 0.9 copy-start.2
  41.8 0.7 copy-start.3
  42.5 0.9 copy-start.5
  43.4 0.9 copy-start.6
  44.3 0.7 copy-start.7
  47.6 25.0 %all-to-all-start = ((bf16[4,1536,128]{2,1,0:T(8,128)(2,1)}), bf16[4,1536,128]{2,1,0:T(8,128)(2,1)S(1)}, u32[]{:S(2)}, u32[]{:S(2)}) async-start(bf16[4,1536,128]{2,1,0:T(8,128)(2,1)} %get-tuple-element.15), calls=%async_computation | async-start | bytes 3145728 | tf_op jit(solution)/shard_map/all_to_all | solution.py:307
  64.5 7.5 %collective-permute-start.5 = (bf16[4,80,512]{2,1,0:T(8,128)(2,1)S(1)}, bf16[4,80,512]{2,1,0:T(8,128)(2,1)S(1)}, u32[]{:S(2)}, u32[]{:S(2)}) collective-permute-start(bf16[4,80,512]{2,1,0:T(8,128)(2,1)S(1)} %bitcast.50), channel_id=1, source_target_pairs={{0,1},{1,0},{2,3},{3,2},{4,5},{5,4},{6,7},{7,6},{8,9},{9,8},{10,11... | collective-permute-start | bytes 983048 | tf_op jit(solution)/shard_map/ppermute | solution.py:309
  77.6 24.5 %copy-start.9 = (s32[1,1,8]{2,1,0:T(1,128)S(1)}, s32[1,1,8]{2,1,0:T(1,128)}, u32[]{:S(2)}) copy-start(s32[1,1,8]{2,1,0:T(1,128)} %param.21) | copy-start | bytes 100
  77.6 25.8 %all-to-all-start.1 = ((bf16[4,896,128]{2,1,0:T(8,128)(2,1)}), bf16[4,896,128]{2,1,0:T(8,128)(2,1)S(1)}, u32[]{:S(2)}, u32[]{:S(2)}) async-start(bf16[4,896,128]{2,1,0:T(8,128)(2,1)} %shard_map.176), calls=%async_computation.1 | async-start | bytes 1835008 | tf_op jit(solution)/shard_map/all_to_all | solution.py:326
  94.0 9.4 %collective-permute-start.6 = (bf16[4,5,80,128]{3,2,1,0:T(8,128)(2,1)S(1)}, bf16[4,5,80,128]{3,2,1,0:T(8,128)(2,1)S(1)}, u32[]{:S(2)}, u32[]{:S(2)}) collective-permute-start(bf16[4,5,80,128]{3,2,1,0:T(8,128)(2,1)S(1)} %bitcast.48), channel_id=1, source_target_pairs={{0,1},{1,0},{2,3},{3,2},{4,5},{5,4},{6,7},{7,6},{8,9},{9,8},{10,11... | collective-permute-start | bytes 1228808 | tf_op jit(solution)/shard_map/ppermute | solution.py:312
  102.1 8.1 %copy-start.4 = (bf16[1,32,288]{2,1,0:T(8,128)(2,1)S(1)}, bf16[1,32,288]{2,1,0:T(8,128)(2,1)}, u32[]{:S(2)}) copy-start(bf16[1,32,288]{2,1,0:T(8,128)(2,1)} %param.17) | copy-start | bytes 55300
  102.1 19.2 %copy-start = (bf16[16,32,160]{2,1,0:T(8,128)(2,1)S(1)}, bf16[16,32,160]{2,1,0:T(8,128)(2,1)}, u32[]{:S(2)}) copy-start(bf16[16,32,160]{2,1,0:T(8,128)(2,1)} %residual.1) | copy-start | bytes 491524
  102.1 19.2 %copy-start.8 = (bf16[1,32,160]{2,1,0:T(8,128)(2,1)S(1)}, bf16[1,32,160]{2,1,0:T(8,128)(2,1)}, u32[]{:S(2)}) copy-start(bf16[1,32,160]{2,1,0:T(8,128)(2,1)} %long_residual.1) | copy-start | bytes 30724
  106.7 14.6 %all-to-all-start.2 = ((bf16[4,688,128]{2,1,0:T(8,128)(2,1)}), bf16[4,688,128]{2,1,0:T(8,128)(2,1)S(1)}, u32[]{:S(2)}, u32[]{:S(2)}) async-start(bf16[4,688,128]{2,1,0:T(8,128)(2,1)} %shard_map.177), calls=%async_computation.2 | async-start | bytes 1409024 | tf_op jit(solution)/shard_map/all_to_all | solution.py:339

commit v5 on v4

--- a/solution.py
+++ b/solution.py
@@ -13,20 +13,8 @@
 TREE = 32
 ROWS = ("y", "x")
 COLS = ("a", "b", "c")
-SWAP = [(0, 1), (1, 0)]
 BF = jnp.bfloat16
 F32 = jnp.float32
-
-
-def tree_reach(parent_ids):
-    tree_count = parent_ids.shape[-1]
-    positions = jnp.arange(tree_count, dtype=jnp.int32)
-    reach = (parent_ids[..., :, None] == positions).astype(F32)
-    reach = reach + (positions[:, None] == positions[None, :]).astype(F32)
-    for _ in range(max(1, (tree_count - 1).bit_length())):
-        product = jnp.einsum("...ij,...jk->...ik", reach, reach, preferred_element_type=F32)
-        reach = jnp.minimum(reach + product, 1.0)
-    return reach > 0.5
 
 
 OVER_LAST = (((1,), (1,)), ((), ()))
@@ -52,18 +40,7 @@
     return lax.dot_general(left, right, OVER_LAST, preferred_element_type=F32)
 
 
-def place_shards(c, mine, twin, target, sems):
-    copies = [
-        pltpu.make_async_copy(mine, target.at[..., c, :, :], sems.at[0]),
-        pltpu.make_async_copy(twin, target.at[..., 1 - c, :, :], sems.at[1]),
-    ]
-    for copy in copies:
-        copy.start()
-    return copies
-
-
-def attend_kernel(place, got, query_l, tree_l, mine, twin, out, kv, lat, sems):
-    copies = place_shards(place[0], mine, twin, kv, sems)
+def attend_kernel(got, query_l, tree_l, kv, out, lat):
     lanes = lax.broadcasted_iota(jnp.int32, (TREE, 128), 1)
     slots = lax.broadcasted_iota(jnp.int32, (1, 256), 1).astype(F32)
     scale = (NOPE + ROPE) ** -0.5
@@ -85,8 +62,6 @@
         reach = jnp.concatenate([reach] * SLICE, axis=0)
         return jnp.where(reach > 0.5, scores * scale, -jnp.inf), keys
 
-    for copy in copies:
-        copy.wait()
     for p in range(SLICE // 2):
         at = TREE * p
         rows = [got[k, QUERY_AT + at : QUERY_AT + at + TREE] for k in range(4)] + [query_l[at : at + TREE]]
@@ -150,14 +125,8 @@
             out[d, base + TREE * i : base + TREE * (i + 1)] = part
 
 
-def project_kernel(place, got, mine, twin, send, weight, rows, sems):
-    c, a = place[0], place[2]
-    copies = []
-    for k in range(5):
-        copies.append(pltpu.make_async_copy(mine.at[:, k], weight.at[k, :, c], sems.at[k]))
-        copies.append(pltpu.make_async_copy(twin.at[:, k], weight.at[k, :, 1 - c], sems.at[5 + k]))
-    for copy in copies:
-        copy.start()
+def project_kernel(place, got, weight, send, rows):
+    a = place[1]
     base = 5 * TREE * (SLICE // 2)
     logs = sum(got[:, base + TREE * i : base + TREE * (i + 1)].astype(F32) for i in range(3))
     share = jnp.exp(logs - jnp.max(logs, axis=0)[None])
@@ -174,13 +143,11 @@
         wide = (dot(high, select) + dot(low, select)).reshape(4, TREE, 128)
         piece = got[:, at + 4 * TREE : at + 5 * TREE].astype(F32) * wide
         rows[16 * TREE : 17 * TREE, cols] = jnp.sum(piece, axis=0).astype(BF)
-    for copy in copies:
-        copy.wait()
-    rest = dot(rows[...], weight[4].reshape(SPAN, 128))
+    rest = dot(rows[...], weight[:, :, 4].reshape(SPAN, 128))
     lanes = lax.broadcasted_iota(jnp.int32, (QUARTER, 128), 1) // 32
     for k in range(4):
-        x = lax.rem(a + 4 - k, 4)
-        send[x, :TOKENS] = dot(rows[...], weight[k].reshape(SPAN, 128)).astype(BF)
+        x = lax.rem(a + k, 4)
+        send[x, :TOKENS] = dot(rows[...], weight[:, :, k].reshape(SPAN, 128)).astype(BF)
         packed = jnp.zeros((QUARTER, 128), F32)
         for g in range(4):
             part = rest[QUARTER * g : QUARTER * (g + 1)]
@@ -205,7 +172,7 @@
 
 SMEM = pl.BlockSpec(memory_space=pltpu.SMEM)
 VMEM = pl.BlockSpec(memory_space=pltpu.VMEM)
-ANY = pl.BlockSpec(memory_space=pl.ANY)
+HBM = pl.BlockSpec(memory_space=pltpu.HBM)
 PARAMS = pltpu.CompilerParams(vmem_limit_bytes=48 << 20)
 
 
@@ -215,20 +182,36 @@
     return jnp.where(match(row, col), 1.0, 0.0).astype(BF)
 
 
-def pack_kernel(place, lengths, queries, queries_l, keys, keys_l, tree, tree_l, reach, block, own_q, own_tree, slices):
+def pack_kernel(place, length, length_l, parents, parents_l, *refs):
+    sources, (block, own_q, own_tree), held, (slices, sems) = refs[:6], refs[6:9], refs[9:15], refs[15:]
+    copies = [pltpu.make_async_copy(sources[i], held[i], sems.at[i]) for i in range(6)]
+    for copy in copies:
+        copy.start()
+    queries, queries_l, keys, keys_l, tree, tree_l = held
+    lanes = lax.broadcasted_iota(jnp.int32, (TREE, 128), 1)
+    tile4 = onehot(TREE, 128, lambda row, col: col % 32 == row)
+    widen = onehot(TREE, 128, lambda row, col: col == row)
+    above = lax.broadcasted_iota(jnp.int32, (TREE, TREE), 0)
+    same = above == lax.broadcasted_iota(jnp.int32, (TREE, TREE), 1)
+    extras = []
+    for i, ids in enumerate((parents, parents_l)):
+        reach = jnp.where(same | (above == ids[...]), 1.0, 0.0).astype(BF)
+        for _ in range((TREE - 1).bit_length()):
+            reach = jnp.minimum(dot(reach, reach), 1.0).astype(BF)
+        extra = lax.dot_general(reach, widen, (((0,), (0,)), ((), ())), preferred_element_type=F32)
+        if i == 1:
+            extra = jnp.where(place[2] == 0, extra, 0.0)
+        extra = jnp.where(lanes == 32, length[0, 0].astype(F32), extra)
+        extras.append(jnp.where(lanes == 33, length_l[0, 0].astype(F32), extra).astype(BF))
+    for copy in copies:
+        copy.wait()
     for d in range(4):
         block[d, 0:288] = keys[:, :128]
         block[d, 288:576] = keys[:, 128:]
         block[d, 576:864] = keys_l[:, :128]
         block[d, 864:1152] = keys_l[:, 128:]
-    lanes = lax.broadcasted_iota(jnp.int32, (TREE, 128), 1)
-    tile4 = onehot(TREE, 128, lambda row, col: col % 32 == row)
-    widen = onehot(TREE, 128, lambda row, col: col == row)
     for i, rows in enumerate((tree, tree_l)):
-        extra = dot(reach[i], widen)
-        extra = jnp.where(lanes == 32, lengths[0].astype(F32), extra)
-        extra = jnp.where(lanes == 33, lengths[1].astype(F32), extra).astype(BF)
-        parts = (rows[:, :128], rows[:, 128:KVR], dot(rows[:, KVR:], tile4).astype(BF), extra)
+        parts = (rows[:, :128], rows[:, 128:KVR], dot(rows[:, KVR:], tile4).astype(BF), extras[i])
         for k, part in enumerate(parts):
             at = slice(TREE * k, TREE * (k + 1))
             if i == 0:
@@ -266,7 +249,7 @@
             at = TREE * (5 + k)
             block[s, QUERY_AT + at : QUERY_AT + at + TREE] = part[:TREE]
             slices[s, at : at + TREE] = part[TREE:]
-    own_q[...] = slices[place[1]]
+    own_q[...] = slices[place[0]]
 
 
 def on_device(
@@ -274,19 +257,10 @@
     long_queries, long_tree_latent, long_parents, long_cache, long_plan, long_residual,
     key_up, value_up, out_weight,
 ):
-    y, x, a, c = lax.axis_index("y"), lax.axis_index("x"), lax.axis_index("a"), lax.axis_index("c")
-    place = jnp.stack([c, x, a]).astype(jnp.int32)
-    shard = key_up.shape[0]
-    kv = jnp.concatenate([key_up, value_up], axis=1)
-    pairs = [(r * 16 + z, ((z % 4) * 4 + z // 4) * 16 + (z + r) % 16) for r in range(16) for z in range(16)]
-    kv = lax.ppermute(kv, ("y", "x", "a", "b"), pairs)
-    moved = [
-        lax.ppermute(out_weight, ("x", "a"), [(4 * i + j, 4 * j + (i + k) % 4) for i in range(4) for j in range(4)])
-        for k in range(4)
-    ]
-    reach = tree_reach(jnp.concatenate([parents[0], long_parents], axis=0))
-    reach = (reach & ((jnp.arange(2) == 0) | (y == 0))[:, None, None]).astype(BF)
-    lengths = jnp.concatenate([cache_lengths[0], long_plan[0]])
+    y, x, a = lax.axis_index("y"), lax.axis_index("x"), lax.axis_index("a")
+    place = jnp.stack([x, a, y]).astype(jnp.int32)
+    moved = jnp.pad(jnp.concatenate([key_up, value_up, out_weight], axis=1), ((0, 0), (0, 96)))
+    moved = lax.ppermute(moved, ("x", "a"), [(4 * i + j, 4 * j + i) for i in range(4) for j in range(4)])
     rows = 8 * TREE
     block, query_l, tree_l = pl.pallas_call(
         pack_kernel,
@@ -295,47 +269,48 @@
             jax.ShapeDtypeStruct((rows, 128), BF),
             jax.ShapeDtypeStruct((4 * TREE, 128), BF),
         ),
-        in_specs=[SMEM, SMEM] + [VMEM] * 7,
+        in_specs=[SMEM] * 3 + [VMEM] * 2 + [HBM] * 6,
         out_specs=(VMEM, VMEM, VMEM),
-        scratch_shapes=[pltpu.VMEM((4, rows, 128), BF)],
+        scratch_shapes=[pltpu.VMEM((TREE, HEADS * (NOPE + ROPE)), BF)] * 2
+        + [pltpu.VMEM((KVR + ROPE, 256), BF)] * 2
+        + [pltpu.VMEM((TREE, KVR + ROPE), BF)] * 2
+        + [pltpu.VMEM((4, rows, 128), BF), pltpu.SemaphoreType.DMA((6,))],
         compiler_params=PARAMS,
     )(
-        place, lengths, queries[0], long_queries[0], cache[0, 0].T, long_cache[0].T,
-        tree_latent[0], long_tree_latent[0], reach,
+        place, cache_lengths, long_plan, parents[0], long_parents, queries[0], long_queries[0],
+        cache[0, 0].T, long_cache[0].T, tree_latent[0], long_tree_latent[0],
     )
-    block, kv, *moved = lax.optimization_barrier((block, kv, *moved))
+    block, moved = lax.optimization_barrier((block, moved))
     got = lax.all_to_all(block, "x", 0, 0)
-    kv = lax.all_gather(kv, "y")
-    kv_twin = lax.ppermute(kv, "c", SWAP)
-    tails = jnp.concatenate([part[:, 128:] for part in moved], axis=1)
-    out_rows = lax.all_gather(jnp.stack([part[:, :128] for part in moved] + [tails]), "b")
-    out_twin = lax.ppermute(out_rows, "c", SWAP)
+    held = moved[None, :, 2 * KVR : 2 * KVR + 160]
+    far = lax.ppermute(held, "a", [((j + 2) % 4, j) for j in range(4)])
+    moved, far = lax.optimization_barrier((moved, far))
+    kv = lax.all_gather(moved[:, : 2 * KVR], ("b", "c")).reshape((4, 2) + key_up.shape[:1] + (2 * KVR,))
+    held = jnp.concatenate([held, far])
+    far = lax.ppermute(held, "a", [((j + 1) % 4, j) for j in range(4)])
+    kv, far = lax.optimization_barrier((kv, far))
+    blocks = [held[0], far[0], held[1], far[1]]
+    tails = jnp.concatenate([part[:, 128:] for part in blocks], axis=1)
+    out_rows = lax.all_gather(jnp.stack([part[:, :128] for part in blocks] + [tails]), ("b", "c"))
+    out_rows = out_rows.reshape((4, 2) + out_rows.shape[1:])
 
     heads = pl.pallas_call(
         attend_kernel,
         out_shape=jax.ShapeDtypeStruct((4, 5 * TREE * (SLICE // 2) + 3 * TREE, 128), BF),
-        in_specs=[SMEM, VMEM, VMEM, VMEM, ANY, ANY],
+        in_specs=[VMEM] * 4,
         out_specs=VMEM,
-        scratch_shapes=[
-            pltpu.VMEM((4, 2, shard, 2 * KVR), BF),
-            pltpu.VMEM((5, SLICE * TREE, KVR), BF),
-            pltpu.SemaphoreType.DMA((2,)),
-        ],
+        scratch_shapes=[pltpu.VMEM((5, SLICE * TREE, KVR), BF)],
         compiler_params=PARAMS,
-    )(place, got, query_l, tree_l, kv, kv_twin)
+    )(got, query_l, tree_l, kv)
     shared = lax.all_to_all(heads, "y", 0, 0)
     send = pl.pallas_call(
         project_kernel,
         out_shape=jax.ShapeDtypeStruct((4, 688, 128), BF),
-        in_specs=[SMEM, VMEM, ANY, ANY],
+        in_specs=[SMEM, VMEM, VMEM],
         out_specs=VMEM,
-        scratch_shapes=[
-            pltpu.VMEM((5, 4, 2, shard, 128), BF),
-            pltpu.VMEM((TOKENS, SPAN), BF),
-            pltpu.SemaphoreType.DMA((10,)),
-        ],
+        scratch_shapes=[pltpu.VMEM((TOKENS, SPAN), BF)],
         compiler_params=PARAMS,
-    )(place, shared, out_rows, out_twin)
+    )(place, shared, out_rows)
     back = lax.all_to_all(send, "x", 0, 0)
     hidden, long_hidden = pl.pallas_call(
         finish_kernel,

time: 123 us -> 121 us (0.984)
  starting transfers between devices: 63.4 us -> 48.3 us
  blocking collectives: 23.1 us -> 35.3 us
  local copies, waits for them, and re-layouts: 5.83 us -> 7.15 us
  Pallas kernels: 11.6 us -> 12.9 us
    ppermute x7 -> x3, starting transfers between devices: 49.8 us -> 21 us  [the longest x1 11.4 us: on_device(): far = lax.ppermute(held, 'a', [((j + 2) % 4, j) for j in range(4)])]
    all_to_all x1, starting transfers between devices: 6.56 us -> 19.6 us  [on_device(): got = lax.all_to_all(block, 'x', 0, 0)]
    all_gather x2, blocking collectives: 23.1 us -> 35.3 us  [the longest x1 19.1 us: on_device(): lax.all_gather(moved[:, :2 * KVR], ('b', 'c'))]
    pallas_call x1, Pallas kernels: 2.47 us -> 4.92 us  [on_device(): pl.pallas_call(pack_kernel, out_shape=(jax.ShapeDtypeStruct((4, BLOCK, 12...]
    unnamed x24 -> x30, local copies, waits for them, and re-layouts: 5.24 us -> 6.54 us
    ppermute x7 -> x3, waiting for transfers between devices: 2.5 us -> 2.16 us  [the longest x1 2.15 us: on_device(): far = lax.ppermute(held, 'a', [((j + 2) % 4, j) for j in range(4)])]
  transfers between devices with their start and end apart: 10 -> 6, of which waited for: 4 -> 2; matrix products, arithmetic and copies ran while one was open for 3% -> 2% of each run, Pallas kernels for 2% -> 4%
where the time goes in v5:
time: 121 us; the launch traced here: 120 us
  starting transfers between devices  48.3 us (40%)
  blocking collectives  35.3 us (29%)
  Pallas kernels  12.9 us (11%)
  waiting for transfers between devices  12.2 us (10%)
  local copies, waits for them, and re-layouts  7.15 us (6%)
  other arithmetic  2.37 us (2%)
  between operations  2.09 us (2%)
    all_to_all x1, starting transfers between devices, on_device(): got = lax.all_to_all(block, 'x', 0, 0)  19.6 us
    all_gather x1, blocking collectives, on_device(): lax.all_gather(moved[:, :2 * KVR], ('b', 'c'))  19.1 us
    all_gather x1, blocking collectives, on_device(): lax.all_gather(jnp.stack([part[:, :128] for part in blocks] + [tails]), (...  16.3 us
    ppermute x1, starting transfers between devices, on_device(): far = lax.ppermute(held, 'a', [((j + 2) % 4, j) for j in range(4)])  11.4 us
    all_to_all x1, waiting for transfers between devices, on_device(): back = lax.all_to_all(send, 'x', 0, 0)  10.1 us
    ppermute x1, starting transfers between devices, on_device(): far = lax.ppermute(held, 'a', [((j + 1) % 4, j) for j in range(4)])  8.91 us
    unnamed x30, local copies, waits for them, and re-layouts  6.54 us
    pallas_call x1, Pallas kernels, on_device(): pl.pallas_call(pack_kernel, out_shape=(jax.ShapeDtypeStruct((4, BLOCK, 12...  4.92 us
  transfers between devices with their start and end apart: 6, of which 2 were waited for; matrix products, arithmetic and copies ran while one was open for 2% of the time, Pallas kernels for 4%

profile of v5, /device:TPU:1, one launch (start us, length us, event | category | flops | bytes accessed | tf_op | source)
XLA Modules:
  0.0 120.4 jit_solution(17078005764214375084)
XLA Ops:
  0.6 0.8 fusion.4
  1.5 0.7 collective-permute-start
  3.4 0.1 pad_add_fusion.place
  3.5 0.9 copy-done.1
  4.5 0.0 copy-start.2
  4.5 0.9 copy-done.2
  5.4 0.0 copy-start.3
  5.4 0.7 copy-done.3
  6.2 0.0 copy-start.5
  6.2 0.9 copy-done.5
  7.1 0.9 copy-done.6
  8.0 0.0 copy-start.7
  8.0 0.7 copy-done.7
  8.7 0.0 copy-start.9
  8.7 0.7 copy-done.9
  9.4 0.0 copy-start.10
  9.4 0.7 copy-done.10
  10.0 4.9 %shard_map.175 = (bf16[4,1536,128]{2,1,0:T(8,128)(2,1)}, bf16[256,128]{1,0:T(8,128)(2,1)S(1)}, bf16[128,128]{1,0:T(8,128)(2,1)S(1)}) custom-call(s32[3]{0:T(128)S(1)} %pad_add_fusion.place, s32[1,1]{1,0:T(1,128)S(6)} %copy.23.length, s32[1,1]{1,0:T(1,128)S(6)} %copy.24.length_l, s32[1,32]{1,0:T(1,128)S(1)} %bitcast.58, s32[1,32]{1,0:T(1,128)S(1)} %copy-done.10, ...), custom_call_target="tpu_custom_call" | custom-call | tf_op jit(solution)/shard_map/pallas_call | solution.py:265
  15.0 0.7 fusion.9
  15.6 0.0 collective-permute-done
  15.6 0.0 copy-start.11
  15.6 19.6 %all-to-all-start = ((bf16[4,1536,128]{2,1,0:T(8,128)(2,1)}), bf16[4,1536,128]{2,1,0:T(8,128)(2,1)S(1)}, u32[]{:S(2)}, u32[]{:S(2)}) async-start(bf16[4,1536,128]{2,1,0:T(8,128)(2,1)} %get-tuple-element.15), calls=%async_computation | async-start | bytes 3145728 | tf_op jit(solution)/shard_map/all_to_all | solution.py:284
  35.2 11.4 %collective-permute-start.1 = (bf16[1,80,160]{2,1,0:T(8,128)(2,1)S(1)}, bf16[1,80,160]{2,1,0:T(8,128)(2,1)S(1)}, u32[]{:S(2)}, u32[]{:S(2)}) collective-permute-start(bf16[1,80,160]{2,1,0:T(8,128)(2,1)S(1)} %slice_bitcast_fusion.2), channel_id=1, source_target_pairs={{16,0},{24,8},{0,16},{8,24},{17,1},{25,9},{1,17},{9,25},{18,2},{26... | collective-permute-start | bytes 76808 | tf_op jit(solution)/shard_map/ppermute | solution.py:286
  46.6 2.2 %collective-permute-done.1 = bf16[1,80,160]{2,1,0:T(8,128)(2,1)S(1)} collective-permute-done((bf16[1,80,160]{2,1,0:T(8,128)(2,1)S(1)}, bf16[1,80,160]{2,1,0:T(8,128)(2,1)S(1)}, u32[]{:S(2)}, u32[]{:S(2)}) %collective-permute-start.1) | collective-permute-done | bytes 25632 | tf_op jit(solution)/shard_map/ppermute | solution.py:286
  48.7 0.0 copy-done.11
  48.8 8.9 %collective-permute-start.2 = (bf16[2,80,160]{2,1,0:T(8,128)(2,1)S(1)}, bf16[2,80,160]{2,1,0:T(8,128)(2,1)S(1)}, u32[]{:S(2)}, u32[]{:S(2)}) collective-permute-start(bf16[2,80,160]{2,1,0:T(8,128)(2,1)S(1)} %pad_maximum_fusion), channel_id=1, source_target_pairs={{8,0},{16,8},{24,16},{0,24},{9,1},{17,9},{25,17},{1,25},{10,2},{18... | collective-permute-start | bytes 153608 | tf_op jit(solution)/shard_map/ppermute | solution.py:290
  57.7 19.1 %all-gather = bf16[640,512]{1,0:T(8,128)(2,1)S(1)} all-gather(bf16[80,512]{1,0:T(8,128)(2,1)S(1)} %slice.39), channel_id=2, replica_groups=mesh['y'=4,'x'=4,'a'=4,'b'=4,'c'=2] {'b','c'}, dimensions={0}, use_global_device_ids=true | all-gather | bytes 737280 | tf_op jit(solution)/shard_map/all_gather | solution.py:288
  76.8 0.0 collective-permute-done.2
  76.8 0.0 all-to-all-done.got
  76.8 4.4 %shard_map.176 = bf16[4,896,128]{2,1,0:T(8,128)(2,1)} custom-call(bf16[4,1536,128]{2,1,0:T(8,128)(2,1)S(1)} %all-to-all-done.got, bf16[256,128]{1,0:T(8,128)(2,1)S(1)} %get-tuple-element.16.query_l, bf16[128,128]{1,0:T(8,128)(2,1)S(1)} %get-tuple-element.17.tree_l, bf16[4,2,80,512]{3,2,1,0:T(8,128)(2,1)S(1)} %bitcast.50), custom_call_target="tpu_custom_call" | custom-call | tf_op jit(solution)/shard_map/pallas_call | solution.py:297
  81.3 0.0 slice-start
  81.3 4.3 %all-to-all-start.1 = ((bf16[4,896,128]{2,1,0:T(8,128)(2,1)}), bf16[4,896,128]{2,1,0:T(8,128)(2,1)S(1)}, u32[]{:S(2)}, u32[]{:S(2)}) async-start(bf16[4,896,128]{2,1,0:T(8,128)(2,1)} %shard_map.176), calls=%async_computation.1 | async-start | bytes 1835008 | tf_op jit(solution)/shard_map/all_to_all | solution.py:305
  85.6 0.0 slice-done
  85.6 0.1 fusion.8
  85.7 16.3 %all-gather.1 = bf16[40,80,128]{2,1,0:T(8,128)(2,1)S(1)} all-gather(bf16[5,80,128]{2,1,0:T(8,128)(2,1)S(1)} %fusion.8), channel_id=3, replica_groups=mesh['y'=4,'x'=4,'a'=4,'b'=4,'c'=2] {'b','c'}, dimensions={0}, use_global_device_ids=true | all-gather | bytes 921600 | tf_op jit(solution)/shard_map/all_gather | solution.py:294
  102.0 0.0 all-to-all-done.1.got
  102.0 0.0 copy-start.4
  102.0 0.0 copy-start.8
  102.0 2.7 %shard_map.177 = bf16[4,688,128]{2,1,0:T(8,128)(2,1)} custom-call(s32[3]{0:T(128)S(1)} %pad_add_fusion.place, bf16[4,896,128]{2,1,0:T(8,128)(2,1)S(1)} %all-to-all-done.1.got, bf16[4,2,5,80,128]{4,3,2,1,0:T(8,128)(2,1)S(1)} %bitcast.49), custom_call_target="tpu_custom_call" | custom-call | tf_op jit(solution)/shard_map/pallas_call | solution.py:306
  104.7 3.5 %all-to-all-start.2 = ((bf16[4,688,128]{2,1,0:T(8,128)(2,1)}), bf16[4,688,128]{2,1,0:T(8,128)(2,1)S(1)}, u32[]{:S(2)}, u32[]{:S(2)}) async-start(bf16[4,688,128]{2,1,0:T(8,128)(2,1)} %shard_map.177), calls=%async_computation.2 | async-start | bytes 1409024 | tf_op jit(solution)/shard_map/all_to_all | solution.py:314
  108.2 0.0 copy-done.4
  108.2 0.6 gather_fusion
  108.8 0.0 copy-done.12
  108.8 0.7 bitcast_select_fusion
  109.4 10.1 %all-to-all-done.2.got = bf16[4,688,128]{2,1,0:T(8,128)(2,1)S(1)} async-done(((bf16[4,688,128]{2,1,0:T(8,128)(2,1)}), bf16[4,688,128]{2,1,0:T(8,128)(2,1)S(1)}, u32[]{:S(2)}, u32[]{:S(2)}) %all-to-all-start.2) | async-done | bytes 704544 | tf_op jit(solution)/shard_map/all_to_all | solution.py:314
  119.5 0.0 copy-done
  119.5 0.0 copy-done.8
  119.5 0.9 shard_map.178
  (17 shorter events, 0.1 us)
Async XLA Ops:
  1.5 14.1 %collective-permute-start = (bf16[80,768]{1,0:T(8,128)(2,1)S(1)}, bf16[80,768]{1,0:T(8,128)(2,1)S(1)}, u32[]{:S(2)}, u32[]{:S(2)}) collective-permute-start(bf16[80,768]{1,0:T(8,128)(2,1)S(1)} %fusion.4), channel_id=1, source_target_pairs={{0,0},{8,32},{16,64},{24,96},{32,8},{40,40},{48,72},{56,104},{64,1... | collective-permute-start | bytes 368648 | tf_op jit(solution)/shard_map/ppermute | solution.py:263
  3.5 0.9 copy-start.1
  4.5 0.9 copy-start.2
  5.4 0.7 copy-start.3
  6.2 0.9 copy-start.5
  7.1 0.9 copy-start.6
  8.0 0.7 copy-start.7
  8.7 0.7 copy-start.9
  9.4 0.7 copy-start.10
  15.6 33.1 %copy-start.11 = (bf16[80,768]{1,0:T(8,128)(2,1)}, bf16[80,768]{1,0:T(8,128)(2,1)S(1)}, u32[]{:S(2)}) copy-start(bf16[80,768]{1,0:T(8,128)(2,1)S(1)} %collective-permute-done) | copy-start | bytes 368644
  15.6 61.2 %all-to-all-start = ((bf16[4,1536,128]{2,1,0:T(8,128)(2,1)}), bf16[4,1536,128]{2,1,0:T(8,128)(2,1)S(1)}, u32[]{:S(2)}, u32[]{:S(2)}) async-start(bf16[4,1536,128]{2,1,0:T(8,128)(2,1)} %get-tuple-element.15), calls=%async_computation | async-start | bytes 3145728 | tf_op jit(solution)/shard_map/all_to_all | solution.py:284
  35.2 13.6 %collective-permute-start.1 = (bf16[1,80,160]{2,1,0:T(8,128)(2,1)S(1)}, bf16[1,80,160]{2,1,0:T(8,128)(2,1)S(1)}, u32[]{:S(2)}, u32[]{:S(2)}) collective-permute-start(bf16[1,80,160]{2,1,0:T(8,128)(2,1)S(1)} %slice_bitcast_fusion.2), channel_id=1, source_target_pairs={{16,0},{24,8},{0,16},{8,24},{17,1},{25,9},{1,17},{9,25},{18,2},{26... | collective-permute-start | bytes 76808 | tf_op jit(solution)/shard_map/ppermute | solution.py:286
  48.8 28.0 %collective-permute-start.2 = (bf16[2,80,160]{2,1,0:T(8,128)(2,1)S(1)}, bf16[2,80,160]{2,1,0:T(8,128)(2,1)S(1)}, u32[]{:S(2)}, u32[]{:S(2)}) collective-permute-start(bf16[2,80,160]{2,1,0:T(8,128)(2,1)S(1)} %pad_maximum_fusion), channel_id=1, source_target_pairs={{8,0},{16,8},{24,16},{0,24},{9,1},{17,9},{25,17},{1,25},{10,2},{18... | collective-permute-start | bytes 153608 | tf_op jit(solution)/shard_map/ppermute | solution.py:290
  81.3 4.3 %slice-start = ((bf16[80,768]{1,0:T(8,128)(2,1)}), bf16[80,32]{1,0:T(8,128)(2,1)S(1)}, s32[]{:S(2)}) async-start(bf16[80,768]{1,0:T(8,128)(2,1)} %copy-done.11), calls=%async_computation.3 | async-start | bytes 40960 | tf_op jit(solution)/shard_map/slice | solution.py:293
  81.3 20.7 %all-to-all-start.1 = ((bf16[4,896,128]{2,1,0:T(8,128)(2,1)}), bf16[4,896,128]{2,1,0:T(8,128)(2,1)S(1)}, u32[]{:S(2)}, u32[]{:S(2)}) async-start(bf16[4,896,128]{2,1,0:T(8,128)(2,1)} %shard_map.176), calls=%async_computation.1 | async-start | bytes 1835008 | tf_op jit(solution)/shard_map/all_to_all | solution.py:305
  102.0 6.2 %copy-start.4 = (bf16[1,32,288]{2,1,0:T(8,128)(2,1)S(1)}, bf16[1,32,288]{2,1,0:T(8,128)(2,1)}, u32[]{:S(2)}) copy-start(bf16[1,32,288]{2,1,0:T(8,128)(2,1)} %param.17) | copy-start | bytes 55300
  102.0 6.8 %copy-start.12 = (s32[1,1,8]{2,1,0:T(1,128)S(1)}, s32[1,1,8]{2,1,0:T(1,128)}, u32[]{:S(2)}) copy-start(s32[1,1,8]{2,1,0:T(1,128)} %param.21) | copy-start | bytes 100
  102.0 17.5 %copy-start = (bf16[16,32,160]{2,1,0:T(8,128)(2,1)S(1)}, bf16[16,32,160]{2,1,0:T(8,128)(2,1)}, u32[]{:S(2)}) copy-start(bf16[16,32,160]{2,1,0:T(8,128)(2,1)} %residual.1) | copy-start | bytes 491524
  102.0 17.5 %copy-start.8 = (bf16[1,32,160]{2,1,0:T(8,128)(2,1)S(1)}, bf16[1,32,160]{2,1,0:T(8,128)(2,1)}, u32[]{:S(2)}) copy-start(bf16[1,32,160]{2,1,0:T(8,128)(2,1)} %long_residual.1) | copy-start | bytes 30724
  104.7 14.9 %all-to-all-start.2 = ((bf16[4,688,128]{2,1,0:T(8,128)(2,1)}), bf16[4,688,128]{2,1,0:T(8,128)(2,1)S(1)}, u32[]{:S(2)}, u32[]{:S(2)}) async-start(bf16[4,688,128]{2,1,0:T(8,128)(2,1)} %shard_map.177), calls=%async_computation.2 | async-start | bytes 1409024 | tf_op jit(solution)/shard_map/all_to_all | solution.py:314

commit v6 on v5

--- a/solution.py
+++ b/solution.py
@@ -20,7 +20,7 @@
 OVER_LAST = (((1,), (1,)), ((), ()))
 SLICE = HEADS // 4
 SPAN = SLICE * VDIM
-LONG_AT, TREE_AT, QUERY_AT, BLOCK = 576, 1152, 1280, 1536
+LONG_AT, TREE_AT, QUERY_AT, OUT_AT, BLOCK = 576, 1152, 1280, 1536, 1696
 TOKENS = 16 * TREE + TREE
 QUARTER = TOKENS // 4
 
@@ -125,8 +125,7 @@
             out[d, base + TREE * i : base + TREE * (i + 1)] = part
 
 
-def project_kernel(place, got, weight, send, rows):
-    a = place[1]
+def project_kernel(got, weight, send, rows):
     base = 5 * TREE * (SLICE // 2)
     logs = sum(got[:, base + TREE * i : base + TREE * (i + 1)].astype(F32) for i in range(3))
     share = jnp.exp(logs - jnp.max(logs, axis=0)[None])
@@ -146,16 +145,15 @@
     rest = dot(rows[...], weight[:, :, 4].reshape(SPAN, 128))
     lanes = lax.broadcasted_iota(jnp.int32, (QUARTER, 128), 1) // 32
     for k in range(4):
-        x = lax.rem(a + k, 4)
-        send[x, :TOKENS] = dot(rows[...], weight[:, :, k].reshape(SPAN, 128)).astype(BF)
+        send[k, :TOKENS] = dot(rows[...], weight[:, :, k].reshape(SPAN, 128)).astype(BF)
         packed = jnp.zeros((QUARTER, 128), F32)
         for g in range(4):
             part = rest[QUARTER * g : QUARTER * (g + 1)]
             shift = (32 * (g - k)) % 128
             part = pltpu.roll(part, shift, 1) if shift else part
             packed = jnp.where(lanes == g, part, packed)
-        send[x, TOKENS : TOKENS + QUARTER] = packed.astype(BF)
-        send[x, TOKENS + QUARTER :] = jnp.zeros((send.shape[1] - TOKENS - QUARTER, 128), BF)
+        send[k, TOKENS : TOKENS + QUARTER] = packed.astype(BF)
+        send[k, TOKENS + QUARTER :] = jnp.zeros((send.shape[1] - TOKENS - QUARTER, 128), BF)
 
 
 def finish_kernel(got, residual, long_residual, hidden, long_hidden, tail):
@@ -173,6 +171,7 @@
 SMEM = pl.BlockSpec(memory_space=pltpu.SMEM)
 VMEM = pl.BlockSpec(memory_space=pltpu.VMEM)
 HBM = pl.BlockSpec(memory_space=pltpu.HBM)
+COST = pl.CostEstimate(flops=6 * 10**9, transcendentals=10**6, bytes_accessed=18 * 10**6)
 PARAMS = pltpu.CompilerParams(vmem_limit_bytes=48 << 20)
 
 
@@ -183,11 +182,11 @@
 
 
 def pack_kernel(place, length, length_l, parents, parents_l, *refs):
-    sources, (block, own_q, own_tree), held, (slices, sems) = refs[:6], refs[6:9], refs[9:15], refs[15:]
-    copies = [pltpu.make_async_copy(sources[i], held[i], sems.at[i]) for i in range(6)]
+    sources, (block, own_q, own_tree), held, (slices, sems) = refs[:7], refs[7:10], refs[10:17], refs[17:]
+    copies = [pltpu.make_async_copy(sources[i], held[i], sems.at[i]) for i in range(7)]
     for copy in copies:
         copy.start()
-    queries, queries_l, keys, keys_l, tree, tree_l = held
+    queries, queries_l, keys, keys_l, tree, tree_l, weight = held
     lanes = lax.broadcasted_iota(jnp.int32, (TREE, 128), 1)
     tile4 = onehot(TREE, 128, lambda row, col: col % 32 == row)
     widen = onehot(TREE, 128, lambda row, col: col == row)
@@ -200,12 +199,15 @@
             reach = jnp.minimum(dot(reach, reach), 1.0).astype(BF)
         extra = lax.dot_general(reach, widen, (((0,), (0,)), ((), ())), preferred_element_type=F32)
         if i == 1:
-            extra = jnp.where(place[2] == 0, extra, 0.0)
+            extra = jnp.where(place[1] == 0, extra, 0.0)
         extra = jnp.where(lanes == 32, length[0, 0].astype(F32), extra)
         extras.append(jnp.where(lanes == 33, length_l[0, 0].astype(F32), extra).astype(BF))
     for copy in copies:
         copy.wait()
+    tail = dot(weight[:, 128:], widen).astype(BF)
     for d in range(4):
+        block[d, OUT_AT : OUT_AT + 80] = weight[:, :128]
+        block[d, OUT_AT + 80 : BLOCK] = tail
         block[d, 0:288] = keys[:, :128]
         block[d, 288:576] = keys[:, 128:]
         block[d, 576:864] = keys_l[:, :128]
@@ -257,10 +259,11 @@
     long_queries, long_tree_latent, long_parents, long_cache, long_plan, long_residual,
     key_up, value_up, out_weight,
 ):
-    y, x, a = lax.axis_index("y"), lax.axis_index("x"), lax.axis_index("a")
-    place = jnp.stack([x, a, y]).astype(jnp.int32)
-    moved = jnp.pad(jnp.concatenate([key_up, value_up, out_weight], axis=1), ((0, 0), (0, 96)))
-    moved = lax.ppermute(moved, ("x", "a"), [(4 * i + j, 4 * j + i) for i in range(4) for j in range(4)])
+    y, x = lax.axis_index("y"), lax.axis_index("x")
+    place = jnp.stack([x, y]).astype(jnp.int32)
+    pairs = [(r * 16 + z, ((z % 4) * 4 + z // 4) * 16 + (z + r) % 16) for r in range(16) for z in range(16)]
+    kv, place = lax.optimization_barrier((jnp.concatenate([key_up, value_up], axis=1), place))
+    kv = lax.ppermute(kv, ("y", "x", "a", "b"), pairs)
     rows = 8 * TREE
     block, query_l, tree_l = pl.pallas_call(
         pack_kernel,
@@ -269,30 +272,35 @@
             jax.ShapeDtypeStruct((rows, 128), BF),
             jax.ShapeDtypeStruct((4 * TREE, 128), BF),
         ),
-        in_specs=[SMEM] * 3 + [VMEM] * 2 + [HBM] * 6,
+        in_specs=[SMEM] * 3 + [VMEM] * 2 + [HBM] * 7,
         out_specs=(VMEM, VMEM, VMEM),
         scratch_shapes=[pltpu.VMEM((TREE, HEADS * (NOPE + ROPE)), BF)] * 2
         + [pltpu.VMEM((KVR + ROPE, 256), BF)] * 2
         + [pltpu.VMEM((TREE, KVR + ROPE), BF)] * 2
-        + [pltpu.VMEM((4, rows, 128), BF), pltpu.SemaphoreType.DMA((6,))],
+        + [pltpu.VMEM(out_weight.shape, BF)]
+        + [pltpu.VMEM((4, rows, 128), BF), pltpu.SemaphoreType.DMA((7,))],
         compiler_params=PARAMS,
+        cost_estimate=COST,
     )(
-        place, cache_lengths, long_plan, parents[0], long_parents, queries[0], long_queries[0],
-        cache[0, 0].T, long_cache[0].T, tree_latent[0], long_tree_latent[0],
+        place, cache_lengths, long_plan, parents[0], long_parents,
+        *[
+            pltpu.with_memory_space_constraint(value, pltpu.HBM)
+            for value in (
+                queries[0], long_queries[0], cache[0, 0].T, long_cache[0].T,
+                tree_latent[0], long_tree_latent[0], out_weight,
+            )
+        ],
     )
-    block, moved = lax.optimization_barrier((block, moved))
+    block, kv = lax.optimization_barrier((block, kv))
     got = lax.all_to_all(block, "x", 0, 0)
-    held = moved[None, :, 2 * KVR : 2 * KVR + 160]
-    far = lax.ppermute(held, "a", [((j + 2) % 4, j) for j in range(4)])
-    moved, far = lax.optimization_barrier((moved, far))
-    kv = lax.all_gather(moved[:, : 2 * KVR], ("b", "c")).reshape((4, 2) + key_up.shape[:1] + (2 * KVR,))
-    held = jnp.concatenate([held, far])
-    far = lax.ppermute(held, "a", [((j + 1) % 4, j) for j in range(4)])
-    kv, far = lax.optimization_barrier((kv, far))
-    blocks = [held[0], far[0], held[1], far[1]]
-    tails = jnp.concatenate([part[:, 128:] for part in blocks], axis=1)
-    out_rows = lax.all_gather(jnp.stack([part[:, :128] for part in blocks] + [tails]), ("b", "c"))
-    out_rows = out_rows.reshape((4, 2) + out_rows.shape[1:])
+    kv = lax.all_gather(kv, ("y", "c"))
+    kv = kv.reshape((4, 2) + kv.shape[1:])
+    shard = out_weight.shape[0]
+    tails = [got[k, OUT_AT + shard : BLOCK, :32] for k in range(4)]
+    out_rows = [got[k, OUT_AT : OUT_AT + shard] for k in range(4)] + [jnp.concatenate(tails, axis=1)]
+    swap = [(4 * i + j, 4 * j + i) for i in range(4) for j in range(4)]
+    got, out_rows = lax.optimization_barrier((got, jnp.stack(out_rows)))
+    out_rows = lax.ppermute(out_rows, ("x", "a"), swap)
 
     heads = pl.pallas_call(
         attend_kernel,
@@ -301,16 +309,20 @@
         out_specs=VMEM,
         scratch_shapes=[pltpu.VMEM((5, SLICE * TREE, KVR), BF)],
         compiler_params=PARAMS,
+        cost_estimate=COST,
     )(got, query_l, tree_l, kv)
+    heads, out_rows = lax.optimization_barrier((heads, out_rows))
     shared = lax.all_to_all(heads, "y", 0, 0)
+    out_rows = lax.all_gather(out_rows, ("b", "c"))
+    out_rows = out_rows.reshape((4, 2) + out_rows.shape[1:])
     send = pl.pallas_call(
         project_kernel,
         out_shape=jax.ShapeDtypeStruct((4, 688, 128), BF),
-        in_specs=[SMEM, VMEM, VMEM],
+        in_specs=[VMEM, VMEM],
         out_specs=VMEM,
         scratch_shapes=[pltpu.VMEM((TOKENS, SPAN), BF)],
         compiler_params=PARAMS,
-    )(place, shared, out_rows)
+    )(shared, out_rows)
     back = lax.all_to_all(send, "x", 0, 0)
     hidden, long_hidden = pl.pallas_call(
         finish_kernel,

time: 121 us -> 116 us (0.959)
  blocking collectives: 35.3 us -> 42 us
  local copies, waits for them, and re-layouts: 7.15 us -> 1.91 us
  starting transfers between devices: 48.3 us -> 46 us
  waiting for transfers between devices: 12.2 us -> 10.4 us
  Pallas kernels: 12.9 us -> 11.3 us
    ppermute x3 -> x2, starting transfers between devices: 21 us -> 1.32 us  [the longest x1 0.67 us: on_device(): out_rows = lax.ppermute(out_rows, ('x', 'a'), swap)]
    all_to_all x1, starting transfers between devices: 3.49 us -> 18.6 us  [on_device(): back = lax.all_to_all(send, 'x', 0, 0)]
    all_gather x2, blocking collectives: 35.3 us -> 42 us  [the longest x1 21.8 us: on_device(): out_rows = lax.all_gather(out_rows, ('b', 'c'))]
    unnamed x30 -> x12, local copies, waits for them, and re-layouts: 6.54 us -> 1.32 us
    all_to_all x1, starting transfers between devices: 4.31 us -> 8.26 us  [on_device(): shared = lax.all_to_all(heads, 'y', 0, 0)]
    ppermute x3 -> x2, waiting for transfers between devices: 2.16 us -> 0.01 us  [the longest x1 0.01 us: on_device(): kv = lax.ppermute(kv, ('y', 'x', 'a', 'b'), pairs)]
    all_to_all x1, starting transfers between devices: 19.6 us -> 17.8 us  [on_device(): got = lax.all_to_all(block, 'x', 0, 0)]
  transfers between devices with their start and end apart: 6 -> 5, of which waited for: 2 -> 2; matrix products, arithmetic and copies ran while one was open for 2% -> 1% of each run, Pallas kernels for 4% -> 7%
where the time goes in v6:
time: 116 us; the launch traced here: 115 us
  starting transfers between devices  46 us (40%)
  blocking collectives  42 us (36%)
  Pallas kernels  11.3 us (10%)
  waiting for transfers between devices  10.4 us (9%)
  between operations  2.02 us (2%)
  local copies, waits for them, and re-layouts  1.91 us (2%)
  other arithmetic  1.67 us (1%)
    all_gather x1, blocking collectives, on_device(): out_rows = lax.all_gather(out_rows, ('b', 'c'))  21.8 us
    all_gather x1, blocking collectives, on_device(): kv = lax.all_gather(kv, ('y', 'c'))  20.2 us
    all_to_all x1, starting transfers between devices, on_device(): back = lax.all_to_all(send, 'x', 0, 0)  18.6 us
    all_to_all x1, starting transfers between devices, on_device(): got = lax.all_to_all(block, 'x', 0, 0)  17.8 us
    all_to_all x1, waiting for transfers between devices, on_device(): back = lax.all_to_all(send, 'x', 0, 0)  9.81 us
    all_to_all x1, starting transfers between devices, on_device(): shared = lax.all_to_all(heads, 'y', 0, 0)  8.26 us
    pallas_call x1, Pallas kernels, on_device(): pl.pallas_call(attend_kernel, out_shape=jax.ShapeDtypeStruct((4, 5 * TREE...  4.41 us
    pallas_call x1, Pallas kernels, on_device(): pl.pallas_call(pack_kernel, out_shape=(jax.ShapeDtypeStruct((4, BLOCK, 12...  3.93 us
  transfers between devices with their start and end apart: 5, of which 2 were waited for; matrix products, arithmetic and copies ran while one was open for 1% of the time, Pallas kernels for 7%

profile of v6, /device:TPU:1, one launch (start us, length us, event | category | flops | bytes accessed | tf_op | source)
XLA Modules:
  0.0 115.3 jit_solution(14145588375536736592)
XLA Ops:
  0.6 0.1 pad_add_fusion.place
  0.7 0.8 pad_maximum_fusion.1
  1.5 0.7 collective-permute-start
  3.5 0.0 copy-start.2
  3.5 0.6 copy-done.2
  4.1 0.0 copy-start.3
  4.1 0.7 copy-done.3
  4.8 3.9 %shard_map.175 = (bf16[4,1696,128]{2,1,0:T(8,128)(2,1)}, bf16[256,128]{1,0:T(8,128)(2,1)S(1)}, bf16[128,128]{1,0:T(8,128)(2,1)S(1)}) custom-call(s32[2]{0:T(128)S(1)} %pad_add_fusion.place, s32[1,1]{1,0:T(1,128)S(6)} %copy.19.length, s32[1,1]{1,0:T(1,128)S(6)} %copy.20.length_l, s32[1,32]{1,0:T(1,128)S(1)} %bitcast.35, s32[1,32]{1,0:T(1,128)S(1)} %copy-done.3, ...), custom_call_target="tpu_custom_call" | custom-call | flops 6000000000 | bytes 18000000 | tf_op jit(solution)/shard_map/pallas_call | solution.py:268
  8.7 0.0 collective-permute-done
  8.7 17.8 %all-to-all-start = ((bf16[4,1696,128]{2,1,0:T(8,128)(2,1)}), bf16[4,1696,128]{2,1,0:T(8,128)(2,1)S(1)}, u32[]{:S(2)}, u32[]{:S(2)}) async-start(bf16[4,1696,128]{2,1,0:T(8,128)(2,1)} %get-tuple-element.19), calls=%async_computation | async-start | bytes 3473408 | tf_op jit(solution)/shard_map/all_to_all | solution.py:295
  26.5 20.2 %all-gather = bf16[640,512]{1,0:T(8,128)(2,1)S(1)} all-gather(bf16[80,512]{1,0:T(8,128)(2,1)S(1)} %collective-permute-done), channel_id=2, replica_groups=mesh['y'=4,'x'=4,'a'=4,'b'=4,'c'=2] {'y','c'}, dimensions={0}, use_global_device_ids=true | all-gather | bytes 737280 | tf_op jit(solution)/shard_map/all_gather | solution.py:296
  46.7 0.6 all-to-all-done.got
  47.3 0.1 maximum_bitcast_fusion
  47.4 0.7 collective-permute-start.1
  48.1 4.4 %shard_map.176 = bf16[4,896,128]{2,1,0:T(8,128)(2,1)} custom-call(bf16[4,1696,128]{2,1,0:T(8,128)(2,1)S(1)} %all-to-all-done.got, bf16[256,128]{1,0:T(8,128)(2,1)S(1)} %get-tuple-element.21.query_l, bf16[128,128]{1,0:T(8,128)(2,1)S(1)} %get-tuple-element.22.tree_l, bf16[4,2,80,512]{3,2,1,0:T(8,128)(2,1)S(1)} %bitcast.34), custom_call_target="tpu_custom_call" | custom-call | flops 6000000000 | bytes 18000000 | tf_op jit(solution)/shard_map/pallas_call | solution.py:305
  52.5 0.0 copy-start.5
  52.5 0.0 collective-permute-done.1
  52.5 8.3 %all-to-all-start.1 = ((bf16[4,896,128]{2,1,0:T(8,128)(2,1)}), bf16[4,896,128]{2,1,0:T(8,128)(2,1)S(1)}, u32[]{:S(2)}, u32[]{:S(2)}) async-start(bf16[4,896,128]{2,1,0:T(8,128)(2,1)} %shard_map.176), calls=%async_computation.1 | async-start | bytes 1835008 | tf_op jit(solution)/shard_map/all_to_all | solution.py:315
  60.8 0.0 copy-done.5
  60.8 21.8 %all-gather.1 = bf16[40,80,128]{2,1,0:T(8,128)(2,1)S(1)} all-gather(bf16[5,80,128]{2,1,0:T(8,128)(2,1)S(1)} %collective-permute-done.1), channel_id=3, replica_groups=mesh['y'=4,'x'=4,'a'=4,'b'=4,'c'=2] {'b','c'}, dimensions={0}, use_global_device_ids=true | all-gather | bytes 921600 | tf_op jit(solution)/shard_map/all_gather | solution.py:316
  82.6 0.0 all-to-all-done.1.got
  82.6 0.0 copy-start.4
  82.6 0.0 copy-start
  82.6 0.0 copy-start.1
  82.6 2.1 %shard_map.177 = bf16[4,688,128]{2,1,0:T(8,128)(2,1)} custom-call(bf16[4,896,128]{2,1,0:T(8,128)(2,1)S(1)} %all-to-all-done.1.got, bf16[4,2,5,80,128]{4,3,2,1,0:T(8,128)(2,1)S(1)} %bitcast.33), custom_call_target="tpu_custom_call" | custom-call | tf_op jit(solution)/shard_map/pallas_call | solution.py:318
  84.7 18.6 %all-to-all-start.2 = ((bf16[4,688,128]{2,1,0:T(8,128)(2,1)}), bf16[4,688,128]{2,1,0:T(8,128)(2,1)S(1)}, u32[]{:S(2)}, u32[]{:S(2)}) async-start(bf16[4,688,128]{2,1,0:T(8,128)(2,1)} %shard_map.177), calls=%async_computation.2 | async-start | bytes 1409024 | tf_op jit(solution)/shard_map/all_to_all | solution.py:326
  103.3 0.0 copy-done.4
  103.3 0.6 gather_fusion
  103.9 0.7 bitcast_select_fusion
  104.6 9.8 %all-to-all-done.2.got = bf16[4,688,128]{2,1,0:T(8,128)(2,1)S(1)} async-done(((bf16[4,688,128]{2,1,0:T(8,128)(2,1)}), bf16[4,688,128]{2,1,0:T(8,128)(2,1)S(1)}, u32[]{:S(2)}, u32[]{:S(2)}) %all-to-all-start.2) | async-done | bytes 704544 | tf_op jit(solution)/shard_map/all_to_all | solution.py:326
  114.4 0.0 copy-done
  114.4 0.0 copy-done.1
  114.4 0.9 shard_map.178
  (6 shorter events, 0.0 us)
Async XLA Ops:
  1.5 7.2 %collective-permute-start = (bf16[80,512]{1,0:T(8,128)(2,1)S(1)}, bf16[80,512]{1,0:T(8,128)(2,1)S(1)}, u32[]{:S(2)}, u32[]{:S(2)}) collective-permute-start(bf16[80,512]{1,0:T(8,128)(2,1)S(1)} %pad_maximum_fusion.1), channel_id=1, source_target_pairs={{0,0},{2,130},{4,260},{6,390},{8,40},{10,170},{12,300},{14,430},{1... | collective-permute-start | bytes 245768 | tf_op jit(solution)/shard_map/ppermute | solution.py:266
  3.5 0.7 copy-start.2
  4.1 0.7 copy-start.3
  8.7 38.5 %all-to-all-start = ((bf16[4,1696,128]{2,1,0:T(8,128)(2,1)}), bf16[4,1696,128]{2,1,0:T(8,128)(2,1)S(1)}, u32[]{:S(2)}, u32[]{:S(2)}) async-start(bf16[4,1696,128]{2,1,0:T(8,128)(2,1)} %get-tuple-element.19), calls=%async_computation | async-start | bytes 3473408 | tf_op jit(solution)/shard_map/all_to_all | solution.py:295
  47.4 5.1 %collective-permute-start.1 = (bf16[5,80,128]{2,1,0:T(8,128)(2,1)S(1)}, bf16[5,80,128]{2,1,0:T(8,128)(2,1)S(1)}, u32[]{:S(2)}, u32[]{:S(2)}) collective-permute-start(bf16[5,80,128]{2,1,0:T(8,128)(2,1)S(1)} %pad_maximum_fusion), channel_id=1, source_target_pairs={{0,0},{8,32},{16,64},{24,96},{32,8},{40,40},{48,72},{56,104},{64,1... | collective-permute-start | bytes 307208 | tf_op jit(solution)/shard_map/ppermute | solution.py:303
  52.5 8.3 %copy-start.5 = (s32[1,1,8]{2,1,0:T(1,128)S(1)}, s32[1,1,8]{2,1,0:T(1,128)}, u32[]{:S(2)}) copy-start(s32[1,1,8]{2,1,0:T(1,128)} %param.21) | copy-start | bytes 100
  52.5 30.1 %all-to-all-start.1 = ((bf16[4,896,128]{2,1,0:T(8,128)(2,1)}), bf16[4,896,128]{2,1,0:T(8,128)(2,1)S(1)}, u32[]{:S(2)}, u32[]{:S(2)}) async-start(bf16[4,896,128]{2,1,0:T(8,128)(2,1)} %shard_map.176), calls=%async_computation.1 | async-start | bytes 1835008 | tf_op jit(solution)/shard_map/all_to_all | solution.py:315
  82.6 20.7 %copy-start.4 = (bf16[1,32,288]{2,1,0:T(8,128)(2,1)S(1)}, bf16[1,32,288]{2,1,0:T(8,128)(2,1)}, u32[]{:S(2)}) copy-start(bf16[1,32,288]{2,1,0:T(8,128)(2,1)} %param.17) | copy-start | bytes 55300
  82.6 31.8 %copy-start = (bf16[16,32,160]{2,1,0:T(8,128)(2,1)S(1)}, bf16[16,32,160]{2,1,0:T(8,128)(2,1)}, u32[]{:S(2)}) copy-start(bf16[16,32,160]{2,1,0:T(8,128)(2,1)} %residual.1) | copy-start | bytes 491524
  82.6 31.8 %copy-start.1 = (bf16[1,32,160]{2,1,0:T(8,128)(2,1)S(1)}, bf16[1,32,160]{2,1,0:T(8,128)(2,1)}, u32[]{:S(2)}) copy-start(bf16[1,32,160]{2,1,0:T(8,128)(2,1)} %long_residual.1) | copy-start | bytes 30724
  84.7 29.7 %all-to-all-start.2 = ((bf16[4,688,128]{2,1,0:T(8,128)(2,1)}), bf16[4,688,128]{2,1,0:T(8,128)(2,1)S(1)}, u32[]{:S(2)}, u32[]{:S(2)}) async-start(bf16[4,688,128]{2,1,0:T(8,128)(2,1)} %shard_map.177), calls=%async_computation.2 | async-start | bytes 1409024 | tf_op jit(solution)/shard_map/all_to_all | solution.py:326

commit v7 on v6

--- a/solution.py
+++ b/solution.py
@@ -20,7 +20,7 @@
 OVER_LAST = (((1,), (1,)), ((), ()))
 SLICE = HEADS // 4
 SPAN = SLICE * VDIM
-LONG_AT, TREE_AT, QUERY_AT, OUT_AT, BLOCK = 576, 1152, 1280, 1536, 1696
+LONG_AT, TREE_AT, QUERY_AT, BLOCK = 576, 1152, 1280, 1536
 TOKENS = 16 * TREE + TREE
 QUARTER = TOKENS // 4
 
@@ -182,11 +182,11 @@
 
 
 def pack_kernel(place, length, length_l, parents, parents_l, *refs):
-    sources, (block, own_q, own_tree), held, (slices, sems) = refs[:7], refs[7:10], refs[10:17], refs[17:]
-    copies = [pltpu.make_async_copy(sources[i], held[i], sems.at[i]) for i in range(7)]
+    sources, (block, own_q, own_tree), held, (slices, sems) = refs[:6], refs[6:9], refs[9:15], refs[15:]
+    copies = [pltpu.make_async_copy(sources[i], held[i], sems.at[i]) for i in range(6)]
     for copy in copies:
         copy.start()
-    queries, queries_l, keys, keys_l, tree, tree_l, weight = held
+    queries, queries_l, keys, keys_l, tree, tree_l = held
     lanes = lax.broadcasted_iota(jnp.int32, (TREE, 128), 1)
     tile4 = onehot(TREE, 128, lambda row, col: col % 32 == row)
     widen = onehot(TREE, 128, lambda row, col: col == row)
@@ -204,10 +204,7 @@
         extras.append(jnp.where(lanes == 33, length_l[0, 0].astype(F32), extra).astype(BF))
     for copy in copies:
         copy.wait()
-    tail = dot(weight[:, 128:], widen).astype(BF)
     for d in range(4):
-        block[d, OUT_AT : OUT_AT + 80] = weight[:, :128]
-        block[d, OUT_AT + 80 : BLOCK] = tail
         block[d, 0:288] = keys[:, :128]
         block[d, 288:576] = keys[:, 128:]
         block[d, 576:864] = keys_l[:, :128]
@@ -272,13 +269,12 @@
             jax.ShapeDtypeStruct((rows, 128), BF),
             jax.ShapeDtypeStruct((4 * TREE, 128), BF),
         ),
-        in_specs=[SMEM] * 3 + [VMEM] * 2 + [HBM] * 7,
+        in_specs=[SMEM] * 3 + [VMEM] * 2 + [HBM] * 6,
         out_specs=(VMEM, VMEM, VMEM),
         scratch_shapes=[pltpu.VMEM((TREE, HEADS * (NOPE + ROPE)), BF)] * 2
         + [pltpu.VMEM((KVR + ROPE, 256), BF)] * 2
         + [pltpu.VMEM((TREE, KVR + ROPE), BF)] * 2
-        + [pltpu.VMEM(out_weight.shape, BF)]
-        + [pltpu.VMEM((4, rows, 128), BF), pltpu.SemaphoreType.DMA((7,))],
+        + [pltpu.VMEM((4, rows, 128), BF), pltpu.SemaphoreType.DMA((6,))],
         compiler_params=PARAMS,
         cost_estimate=COST,
     )(
@@ -287,20 +283,18 @@
             pltpu.with_memory_space_constraint(value, pltpu.HBM)
             for value in (
                 queries[0], long_queries[0], cache[0, 0].T, long_cache[0].T,
-                tree_latent[0], long_tree_latent[0], out_weight,
+                tree_latent[0], long_tree_latent[0],
             )
         ],
     )
-    block, kv = lax.optimization_barrier((block, kv))
+    cols = lax.all_gather(out_weight, "x")
+    out_rows = jnp.stack([cols[k, :, :128] for k in range(4)] + [jnp.concatenate([cols[k, :, 128:] for k in range(4)], axis=1)])
+    block, kv, out_rows = lax.optimization_barrier((block, kv, out_rows))
     got = lax.all_to_all(block, "x", 0, 0)
+    out_rows = lax.ppermute(out_rows, ("x", "a"), [(4 * i + j, 4 * j + i) for i in range(4) for j in range(4)])
     kv = lax.all_gather(kv, ("y", "c"))
+    kv, out_rows = lax.optimization_barrier((kv, out_rows))
     kv = kv.reshape((4, 2) + kv.shape[1:])
-    shard = out_weight.shape[0]
-    tails = [got[k, OUT_AT + shard : BLOCK, :32] for k in range(4)]
-    out_rows = [got[k, OUT_AT : OUT_AT + shard] for k in range(4)] + [jnp.concatenate(tails, axis=1)]
-    swap = [(4 * i + j, 4 * j + i) for i in range(4) for j in range(4)]
-    got, out_rows = lax.optimization_barrier((got, jnp.stack(out_rows)))
-    out_rows = lax.ppermute(out_rows, ("x", "a"), swap)
 
     heads = pl.pallas_call(
         attend_kernel,
@@ -311,7 +305,6 @@
         compiler_params=PARAMS,
         cost_estimate=COST,
     )(got, query_l, tree_l, kv)
-    heads, out_rows = lax.optimization_barrier((heads, out_rows))
     shared = lax.all_to_all(heads, "y", 0, 0)
     out_rows = lax.all_gather(out_rows, ("b", "c"))
     out_rows = out_rows.reshape((4, 2) + out_rows.shape[1:])

time: 116 us -> 106 us (0.914)
  starting transfers between devices: 46 us -> 15.9 us
  blocking collectives: 42 us -> 62.9 us
    all_gather x0 -> x1, blocking collectives: none -> 15.8 us  [on_device(): cols = lax.all_gather(out_weight, 'x')]
    all_to_all x1, starting transfers between devices: 17.8 us -> 4.49 us  [on_device(): got = lax.all_to_all(block, 'x', 0, 0)]
    all_to_all x1, starting transfers between devices: 18.6 us -> 6.47 us  [on_device(): back = lax.all_to_all(send, 'x', 0, 0)]
    all_gather x1, blocking collectives: 20.2 us -> 25.5 us  [on_device(): kv = lax.all_gather(kv, ('y', 'c'))]
    all_to_all x1, starting transfers between devices: 8.26 us -> 3.64 us  [on_device(): shared = lax.all_to_all(heads, 'y', 0, 0)]
  transfers between devices with their start and end apart: 5 -> 5, of which waited for: 2 -> 1; matrix products, arithmetic and copies ran while one was open for 1% -> 1% of each run, Pallas kernels for 7% -> 4%
where the time goes in v7:
time: 106 us
  blocking collectives  62.9 us (59%)
  starting transfers between devices  15.9 us (15%)
  Pallas kernels  11.2 us (11%)
  waiting for transfers between devices  9.82 us (9%)
  between operations  2.05 us (2%)
  local copies, waits for them, and re-layouts  1.93 us (2%)
  other arithmetic  1.67 us (2%)
    all_gather x1, blocking collectives, on_device(): kv = lax.all_gather(kv, ('y', 'c'))  25.5 us
    all_gather x1, blocking collectives, on_device(): out_rows = lax.all_gather(out_rows, ('b', 'c'))  21.6 us
    all_gather x1, blocking collectives, on_device(): cols = lax.all_gather(out_weight, 'x')  15.8 us
    all_to_all x1, waiting for transfers between devices, on_device(): back = lax.all_to_all(send, 'x', 0, 0)  9.81 us
    all_to_all x1, starting transfers between devices, on_device(): back = lax.all_to_all(send, 'x', 0, 0)  6.47 us
    all_to_all x1, starting transfers between devices, on_device(): got = lax.all_to_all(block, 'x', 0, 0)  4.49 us
    pallas_call x1, Pallas kernels, on_device(): pl.pallas_call(attend_kernel, out_shape=jax.ShapeDtypeStruct((4, 5 * TREE...  4.41 us
    pallas_call x1, Pallas kernels, on_device(): pl.pallas_call(pack_kernel, out_shape=(jax.ShapeDtypeStruct((4, BLOCK, 12...  3.84 us
  transfers between devices with their start and end apart: 5, of which 1 were waited for; matrix products, arithmetic and copies ran while one was open for 1% of the time, Pallas kernels for 4%

profile of v7, /device:TPU:1, one launch (start us, length us, event | category | flops | bytes accessed | tf_op | source)
XLA Modules:
  0.0 105.5 jit_solution(9838132151878154886)
XLA Ops:
  0.6 0.8 pad_maximum_fusion.1
  1.4 0.1 pad_add_fusion.place
  1.5 0.7 collective-permute-start
  2.2 15.8 %all-gather = bf16[320,160]{1,0:T(8,128)(2,1)S(1)} all-gather(bf16[80,160]{1,0:T(8,128)(2,1)} %param.31), channel_id=2, replica_groups=mesh['y'=4,'x'=4,'a'=4,'b'=4,'c'=2] {'x'}, dimensions={0}, use_global_device_ids=true | all-gather | bytes 128000 | tf_op jit(solution)/shard_map/all_gather | solution.py:290
  19.3 0.1 maximum_bitcast_fusion
  19.4 0.0 copy-start.2
  19.4 0.6 copy-done.2
  20.1 0.0 copy-start.3
  20.1 0.7 copy-done.3
  20.8 3.8 %shard_map.175 = (bf16[4,1536,128]{2,1,0:T(8,128)(2,1)}, bf16[256,128]{1,0:T(8,128)(2,1)S(1)}, bf16[128,128]{1,0:T(8,128)(2,1)S(1)}) custom-call(s32[2]{0:T(128)S(1)} %pad_add_fusion.place, s32[1,1]{1,0:T(1,128)S(6)} %copy.19.length, s32[1,1]{1,0:T(1,128)S(6)} %copy.20.length_l, s32[1,32]{1,0:T(1,128)S(1)} %bitcast.37, s32[1,32]{1,0:T(1,128)S(1)} %copy-done.3, ...), custom_call_target="tpu_custom_call" | custom-call | flops 6000000000 | bytes 18000000 | tf_op jit(solution)/shard_map/pallas_call | solution.py:265
  24.6 0.0 collective-permute-done
  24.6 4.5 %all-to-all-start = ((bf16[4,1536,128]{2,1,0:T(8,128)(2,1)}), bf16[4,1536,128]{2,1,0:T(8,128)(2,1)S(1)}, u32[]{:S(2)}, u32[]{:S(2)}) async-start(bf16[4,1536,128]{2,1,0:T(8,128)(2,1)} %get-tuple-element.18), calls=%async_computation | async-start | bytes 3145728 | tf_op jit(solution)/shard_map/all_to_all | solution.py:293
  29.1 0.7 collective-permute-start.1
  29.8 25.5 %all-gather.1 = bf16[640,512]{1,0:T(8,128)(2,1)S(1)} all-gather(bf16[80,512]{1,0:T(8,128)(2,1)S(1)} %collective-permute-done), channel_id=3, replica_groups=mesh['y'=4,'x'=4,'a'=4,'b'=4,'c'=2] {'y','c'}, dimensions={0}, use_global_device_ids=true | all-gather | bytes 737280 | tf_op jit(solution)/shard_map/all_gather | solution.py:295
  55.3 0.0 collective-permute-done.1
  55.3 0.0 all-to-all-done.got
  55.3 4.4 %shard_map.176 = bf16[4,896,128]{2,1,0:T(8,128)(2,1)} custom-call(bf16[4,1536,128]{2,1,0:T(8,128)(2,1)S(1)} %all-to-all-done.got, bf16[256,128]{1,0:T(8,128)(2,1)S(1)} %get-tuple-element.19.query_l, bf16[128,128]{1,0:T(8,128)(2,1)S(1)} %get-tuple-element.20.tree_l, bf16[4,2,80,512]{3,2,1,0:T(8,128)(2,1)S(1)} %bitcast.36), custom_call_target="tpu_custom_call" | custom-call | flops 6000000000 | bytes 18000000 | tf_op jit(solution)/shard_map/pallas_call | solution.py:299
  59.7 0.0 copy-start.5
  59.7 3.6 %all-to-all-start.1 = ((bf16[4,896,128]{2,1,0:T(8,128)(2,1)}), bf16[4,896,128]{2,1,0:T(8,128)(2,1)S(1)}, u32[]{:S(2)}, u32[]{:S(2)}) async-start(bf16[4,896,128]{2,1,0:T(8,128)(2,1)} %shard_map.176), calls=%async_computation.1 | async-start | bytes 1835008 | tf_op jit(solution)/shard_map/all_to_all | solution.py:308
  63.3 0.0 copy-done.5
  63.4 21.6 %all-gather.2 = bf16[40,80,128]{2,1,0:T(8,128)(2,1)S(1)} all-gather(bf16[5,80,128]{2,1,0:T(8,128)(2,1)S(1)} %collective-permute-done.1), channel_id=4, replica_groups=mesh['y'=4,'x'=4,'a'=4,'b'=4,'c'=2] {'b','c'}, dimensions={0}, use_global_device_ids=true | all-gather | bytes 921600 | tf_op jit(solution)/shard_map/all_gather | solution.py:309
  85.0 0.0 all-to-all-done.1.got
  85.0 0.0 copy-start.4
  85.0 0.0 copy-start
  85.0 0.0 copy-start.1
  85.0 2.1 %shard_map.177 = bf16[4,688,128]{2,1,0:T(8,128)(2,1)} custom-call(bf16[4,896,128]{2,1,0:T(8,128)(2,1)S(1)} %all-to-all-done.1.got, bf16[4,2,5,80,128]{4,3,2,1,0:T(8,128)(2,1)S(1)} %bitcast.35), custom_call_target="tpu_custom_call" | custom-call | tf_op jit(solution)/shard_map/pallas_call | solution.py:311
  87.1 6.5 %all-to-all-start.2 = ((bf16[4,688,128]{2,1,0:T(8,128)(2,1)}), bf16[4,688,128]{2,1,0:T(8,128)(2,1)S(1)}, u32[]{:S(2)}, u32[]{:S(2)}) async-start(bf16[4,688,128]{2,1,0:T(8,128)(2,1)} %shard_map.177), calls=%async_computation.2 | async-start | bytes 1409024 | tf_op jit(solution)/shard_map/all_to_all | solution.py:319
  93.6 0.0 copy-done.4
  93.6 0.6 gather_fusion
  94.2 0.7 bitcast_select_fusion
  94.9 9.8 %all-to-all-done.2.got = bf16[4,688,128]{2,1,0:T(8,128)(2,1)S(1)} async-done(((bf16[4,688,128]{2,1,0:T(8,128)(2,1)}), bf16[4,688,128]{2,1,0:T(8,128)(2,1)S(1)}, u32[]{:S(2)}, u32[]{:S(2)}) %all-to-all-start.2) | async-done | bytes 704544 | tf_op jit(solution)/shard_map/all_to_all | solution.py:319
  104.7 0.0 copy-done
  104.7 0.0 copy-done.1
  104.7 0.9 shard_map.178
  (6 shorter events, 0.1 us)
Async XLA Ops:
  1.5 23.1 %collective-permute-start = (bf16[80,512]{1,0:T(8,128)(2,1)S(1)}, bf16[80,512]{1,0:T(8,128)(2,1)S(1)}, u32[]{:S(2)}, u32[]{:S(2)}) collective-permute-start(bf16[80,512]{1,0:T(8,128)(2,1)S(1)} %pad_maximum_fusion.1), channel_id=1, source_target_pairs={{0,0},{2,130},{4,260},{6,390},{8,40},{10,170},{12,300},{14,430},{1... | collective-permute-start | bytes 245768 | tf_op jit(solution)/shard_map/ppermute | solution.py:263
  19.4 0.7 copy-start.2
  20.1 0.7 copy-start.3
  24.6 30.7 %all-to-all-start = ((bf16[4,1536,128]{2,1,0:T(8,128)(2,1)}), bf16[4,1536,128]{2,1,0:T(8,128)(2,1)S(1)}, u32[]{:S(2)}, u32[]{:S(2)}) async-start(bf16[4,1536,128]{2,1,0:T(8,128)(2,1)} %get-tuple-element.18), calls=%async_computation | async-start | bytes 3145728 | tf_op jit(solution)/shard_map/all_to_all | solution.py:293
  29.1 26.2 %collective-permute-start.1 = (bf16[5,80,128]{2,1,0:T(8,128)(2,1)S(1)}, bf16[5,80,128]{2,1,0:T(8,128)(2,1)S(1)}, u32[]{:S(2)}, u32[]{:S(2)}) collective-permute-start(bf16[5,80,128]{2,1,0:T(8,128)(2,1)S(1)} %pad_maximum_fusion), channel_id=1, source_target_pairs={{0,0},{8,32},{16,64},{24,96},{32,8},{40,40},{48,72},{56,104},{64,1... | collective-permute-start | bytes 307208 | tf_op jit(solution)/shard_map/ppermute | solution.py:294
  59.7 3.6 %copy-start.5 = (s32[1,1,8]{2,1,0:T(1,128)S(1)}, s32[1,1,8]{2,1,0:T(1,128)}, u32[]{:S(2)}) copy-start(s32[1,1,8]{2,1,0:T(1,128)} %param.21) | copy-start | bytes 100
  59.7 25.3 %all-to-all-start.1 = ((bf16[4,896,128]{2,1,0:T(8,128)(2,1)}), bf16[4,896,128]{2,1,0:T(8,128)(2,1)S(1)}, u32[]{:S(2)}, u32[]{:S(2)}) async-start(bf16[4,896,128]{2,1,0:T(8,128)(2,1)} %shard_map.176), calls=%async_computation.1 | async-start | bytes 1835008 | tf_op jit(solution)/shard_map/all_to_all | solution.py:308
  85.0 8.6 %copy-start.4 = (bf16[1,32,288]{2,1,0:T(8,128)(2,1)S(1)}, bf16[1,32,288]{2,1,0:T(8,128)(2,1)}, u32[]{:S(2)}) copy-start(bf16[1,32,288]{2,1,0:T(8,128)(2,1)} %param.17) | copy-start | bytes 55300
  85.0 19.7 %copy-start = (bf16[16,32,160]{2,1,0:T(8,128)(2,1)S(1)}, bf16[16,32,160]{2,1,0:T(8,128)(2,1)}, u32[]{:S(2)}) copy-start(bf16[16,32,160]{2,1,0:T(8,128)(2,1)} %residual.1) | copy-start | bytes 491524
  85.0 19.7 %copy-start.1 = (bf16[1,32,160]{2,1,0:T(8,128)(2,1)S(1)}, bf16[1,32,160]{2,1,0:T(8,128)(2,1)}, u32[]{:S(2)}) copy-start(bf16[1,32,160]{2,1,0:T(8,128)(2,1)} %long_residual.1) | copy-start | bytes 30724
  87.1 17.6 %all-to-all-start.2 = ((bf16[4,688,128]{2,1,0:T(8,128)(2,1)}), bf16[4,688,128]{2,1,0:T(8,128)(2,1)S(1)}, u32[]{:S(2)}, u32[]{:S(2)}) async-start(bf16[4,688,128]{2,1,0:T(8,128)(2,1)} %shard_map.177), calls=%async_computation.2 | async-start | bytes 1409024 | tf_op jit(solution)/shard_map/all_to_all | solution.py:319

commit v8 on v7

--- a/solution.py
+++ b/solution.py
@@ -181,18 +181,20 @@
     return jnp.where(match(row, col), 1.0, 0.0).astype(BF)
 
 
-def pack_kernel(place, length, length_l, parents, parents_l, *refs):
-    sources, (block, own_q, own_tree), held, (slices, sems) = refs[:6], refs[6:9], refs[9:15], refs[15:]
-    copies = [pltpu.make_async_copy(sources[i], held[i], sems.at[i]) for i in range(6)]
+def pack_kernel(place, length, length_l, *refs):
+    sources, (block, own_q, own_tree), held, (slices, sems) = refs[:8], refs[8:11], refs[11:19], refs[19:]
+    copies = [pltpu.make_async_copy(sources[i], held[i], sems.at[i]) for i in range(8)]
     for copy in copies:
         copy.start()
-    queries, queries_l, keys, keys_l, tree, tree_l = held
+    parents, parents_l, queries, queries_l, keys, keys_l, tree, tree_l = held
     lanes = lax.broadcasted_iota(jnp.int32, (TREE, 128), 1)
     tile4 = onehot(TREE, 128, lambda row, col: col % 32 == row)
     widen = onehot(TREE, 128, lambda row, col: col == row)
     above = lax.broadcasted_iota(jnp.int32, (TREE, TREE), 0)
     same = above == lax.broadcasted_iota(jnp.int32, (TREE, TREE), 1)
     extras = []
+    for copy in copies[:2]:
+        copy.wait()
     for i, ids in enumerate((parents, parents_l)):
         reach = jnp.where(same | (above == ids[...]), 1.0, 0.0).astype(BF)
         for _ in range((TREE - 1).bit_length()):
@@ -202,7 +204,7 @@
             extra = jnp.where(place[1] == 0, extra, 0.0)
         extra = jnp.where(lanes == 32, length[0, 0].astype(F32), extra)
         extras.append(jnp.where(lanes == 33, length_l[0, 0].astype(F32), extra).astype(BF))
-    for copy in copies:
+    for copy in copies[2:]:
         copy.wait()
     for d in range(4):
         block[d, 0:288] = keys[:, :128]
@@ -269,27 +271,29 @@
             jax.ShapeDtypeStruct((rows, 128), BF),
             jax.ShapeDtypeStruct((4 * TREE, 128), BF),
         ),
-        in_specs=[SMEM] * 3 + [VMEM] * 2 + [HBM] * 6,
+        in_specs=[SMEM] * 3 + [HBM] * 8,
         out_specs=(VMEM, VMEM, VMEM),
-        scratch_shapes=[pltpu.VMEM((TREE, HEADS * (NOPE + ROPE)), BF)] * 2
+        scratch_shapes=[pltpu.VMEM((1, TREE), jnp.int32)] * 2
+        + [pltpu.VMEM((TREE, HEADS * (NOPE + ROPE)), BF)] * 2
         + [pltpu.VMEM((KVR + ROPE, 256), BF)] * 2
         + [pltpu.VMEM((TREE, KVR + ROPE), BF)] * 2
-        + [pltpu.VMEM((4, rows, 128), BF), pltpu.SemaphoreType.DMA((6,))],
+        + [pltpu.VMEM((4, rows, 128), BF), pltpu.SemaphoreType.DMA((8,))],
         compiler_params=PARAMS,
         cost_estimate=COST,
     )(
-        place, cache_lengths, long_plan, parents[0], long_parents,
+        place, cache_lengths, long_plan,
         *[
             pltpu.with_memory_space_constraint(value, pltpu.HBM)
             for value in (
-                queries[0], long_queries[0], cache[0, 0].T, long_cache[0].T,
+                parents[0], long_parents, queries[0], long_queries[0], cache[0, 0].T, long_cache[0].T,
                 tree_latent[0], long_tree_latent[0],
             )
         ],
     )
+    block, out_weight = lax.optimization_barrier((block, out_weight))
     cols = lax.all_gather(out_weight, "x")
     out_rows = jnp.stack([cols[k, :, :128] for k in range(4)] + [jnp.concatenate([cols[k, :, 128:] for k in range(4)], axis=1)])
-    block, kv, out_rows = lax.optimization_barrier((block, kv, out_rows))
+    kv, out_rows = lax.optimization_barrier((kv, out_rows))
     got = lax.all_to_all(block, "x", 0, 0)
     out_rows = lax.ppermute(out_rows, ("x", "a"), [(4 * i + j, 4 * j + i) for i in range(4) for j in range(4)])
     kv = lax.all_gather(kv, ("y", "c"))

time: 106 us -> 115 us (1.085)
  starting transfers between devices: 15.9 us -> 26.9 us
  blocking collectives: 62.9 us -> 61.1 us
  local copies, waits for them, and re-layouts: 1.93 us -> 0.63 us
    all_to_all x1, starting transfers between devices: 6.47 us -> 16.8 us  [on_device(): back = lax.all_to_all(send, 'x', 0, 0)]
    all_gather x1, blocking collectives: 15.8 us -> 22.6 us  [on_device(): cols = lax.all_gather(out_weight, 'x')]
    all_gather x1, blocking collectives: 21.6 us -> 16.5 us  [on_device(): out_rows = lax.all_gather(out_rows, ('b', 'c'))]
    all_gather x1, blocking collectives: 25.5 us -> 21.9 us  [on_device(): kv = lax.all_gather(kv, ('y', 'c'))]
    unnamed x12 -> x10, local copies, waits for them, and re-layouts: 1.32 us -> 0.02 us
  transfers between devices with their start and end apart: 5 -> 5, of which waited for: 1 -> 1; matrix products, arithmetic and copies ran while one was open for 1% -> 1% of each run, Pallas kernels for 4% -> 0%
where the time goes in v8:
time: 115 us; the launch traced here: 114 us
  blocking collectives  61.1 us (53%)
  starting transfers between devices  26.9 us (23%)
  Pallas kernels  11.9 us (10%)
  waiting for transfers between devices  9.82 us (9%)
  between operations  2.04 us (2%)
  other arithmetic  1.67 us (1%)
    all_gather x1, blocking collectives, on_device(): cols = lax.all_gather(out_weight, 'x')  22.6 us
    all_gather x1, blocking collectives, on_device(): kv = lax.all_gather(kv, ('y', 'c'))  21.9 us
    all_to_all x1, starting transfers between devices, on_device(): back = lax.all_to_all(send, 'x', 0, 0)  16.8 us
    all_gather x1, blocking collectives, on_device(): out_rows = lax.all_gather(out_rows, ('b', 'c'))  16.5 us
    all_to_all x1, waiting for transfers between devices, on_device(): back = lax.all_to_all(send, 'x', 0, 0)  9.81 us
    all_to_all x1, starting transfers between devices, on_device(): got = lax.all_to_all(block, 'x', 0, 0)  4.85 us
    pallas_call x1, Pallas kernels, on_device(): pl.pallas_call(pack_kernel, out_shape=(jax.ShapeDtypeStruct((4, BLOCK, 12...  4.52 us
    pallas_call x1, Pallas kernels, on_device(): pl.pallas_call(attend_kernel, out_shape=jax.ShapeDtypeStruct((4, 5 * TREE...  4.41 us
  transfers between devices with their start and end apart: 5, of which 1 were waited for; matrix products, arithmetic and copies ran while one was open for 1% of the time, Pallas kernels for 0%

profile of v8, /device:TPU:1, one launch (start us, length us, event | category | flops | bytes accessed | tf_op | source)
XLA Modules:
  0.0 114.1 jit_solution(4227097019223093571)
XLA Ops:
  0.6 0.8 pad_maximum_fusion.1
  1.4 0.1 pad_add_fusion.place
  2.8 4.5 %shard_map.175 = (bf16[4,1536,128]{2,1,0:T(8,128)(2,1)}, bf16[256,128]{1,0:T(8,128)(2,1)S(1)}, bf16[128,128]{1,0:T(8,128)(2,1)S(1)}) custom-call(s32[2]{0:T(128)S(1)} %pad_add_fusion.place, s32[1,1]{1,0:T(1,128)S(6)} %copy.19.length, s32[1,1]{1,0:T(1,128)S(6)} %copy.20.length_l, s32[1,32]{1,0:T(1,128)} %bitcast.46, s32[1,32]{1,0:T(1,128)} %refs_1_.1, ...), custom_call_target="tpu_custom_call" | custom-call | flops 6000000000 | bytes 18000000 | tf_op jit(solution)/shard_map/pallas_call | solution.py:267
  7.3 0.0 copy-start.3
  7.4 4.9 %all-to-all-start = ((bf16[4,1536,128]{2,1,0:T(8,128)(2,1)}), bf16[4,1536,128]{2,1,0:T(8,128)(2,1)S(1)}, u32[]{:S(2)}, u32[]{:S(2)}) async-start(bf16[4,1536,128]{2,1,0:T(8,128)(2,1)} %get-tuple-element.18), calls=%async_computation | async-start | bytes 3145728 | tf_op jit(solution)/shard_map/all_to_all | solution.py:297
  12.2 0.7 collective-permute-start
  12.9 0.0 copy-done.3
  12.9 22.6 %all-gather = bf16[320,160]{1,0:T(8,128)(2,1)S(1)} all-gather(bf16[80,160]{1,0:T(8,128)(2,1)S(1)} %copy-done.3), channel_id=2, replica_groups=mesh['y'=4,'x'=4,'a'=4,'b'=4,'c'=2] {'x'}, dimensions={0}, use_global_device_ids=true | all-gather | bytes 128000 | tf_op jit(solution)/shard_map/all_gather | solution.py:294
  35.5 0.1 maximum_bitcast_fusion
  35.7 0.0 collective-permute-done
  35.7 0.7 collective-permute-start.1
  36.3 21.9 %all-gather.1 = bf16[640,512]{1,0:T(8,128)(2,1)S(1)} all-gather(bf16[80,512]{1,0:T(8,128)(2,1)S(1)} %collective-permute-done), channel_id=3, replica_groups=mesh['y'=4,'x'=4,'a'=4,'b'=4,'c'=2] {'y','c'}, dimensions={0}, use_global_device_ids=true | all-gather | bytes 737280 | tf_op jit(solution)/shard_map/all_gather | solution.py:299
  58.3 0.0 collective-permute-done.1
  58.3 0.0 all-to-all-done.got
  58.3 4.4 %shard_map.176 = bf16[4,896,128]{2,1,0:T(8,128)(2,1)} custom-call(bf16[4,1536,128]{2,1,0:T(8,128)(2,1)S(1)} %all-to-all-done.got, bf16[256,128]{1,0:T(8,128)(2,1)S(1)} %get-tuple-element.19.query_l, bf16[128,128]{1,0:T(8,128)(2,1)S(1)} %get-tuple-element.20.tree_l, bf16[4,2,80,512]{3,2,1,0:T(8,128)(2,1)S(1)} %bitcast.36), custom_call_target="tpu_custom_call" | custom-call | flops 6000000000 | bytes 18000000 | tf_op jit(solution)/shard_map/pallas_call | solution.py:303
  62.7 0.0 copy-start.4
  62.7 3.9 %all-to-all-start.1 = ((bf16[4,896,128]{2,1,0:T(8,128)(2,1)}), bf16[4,896,128]{2,1,0:T(8,128)(2,1)S(1)}, u32[]{:S(2)}, u32[]{:S(2)}) async-start(bf16[4,896,128]{2,1,0:T(8,128)(2,1)} %shard_map.176), calls=%async_computation.1 | async-start | bytes 1835008 | tf_op jit(solution)/shard_map/all_to_all | solution.py:312
  66.6 0.0 copy-done.4
  66.6 16.5 %all-gather.2 = bf16[40,80,128]{2,1,0:T(8,128)(2,1)S(1)} all-gather(bf16[5,80,128]{2,1,0:T(8,128)(2,1)S(1)} %collective-permute-done.1), channel_id=4, replica_groups=mesh['y'=4,'x'=4,'a'=4,'b'=4,'c'=2] {'b','c'}, dimensions={0}, use_global_device_ids=true | all-gather | bytes 921600 | tf_op jit(solution)/shard_map/all_gather | solution.py:313
  83.2 0.0 all-to-all-done.1.got
  83.2 0.0 copy-start.2
  83.2 0.0 copy-start
  83.2 0.0 copy-start.1
  83.2 2.1 %shard_map.177 = bf16[4,688,128]{2,1,0:T(8,128)(2,1)} custom-call(bf16[4,896,128]{2,1,0:T(8,128)(2,1)S(1)} %all-to-all-done.1.got, bf16[4,2,5,80,128]{4,3,2,1,0:T(8,128)(2,1)S(1)} %bitcast.35), custom_call_target="tpu_custom_call" | custom-call | tf_op jit(solution)/shard_map/pallas_call | solution.py:315
  85.3 16.8 %all-to-all-start.2 = ((bf16[4,688,128]{2,1,0:T(8,128)(2,1)}), bf16[4,688,128]{2,1,0:T(8,128)(2,1)S(1)}, u32[]{:S(2)}, u32[]{:S(2)}) async-start(bf16[4,688,128]{2,1,0:T(8,128)(2,1)} %shard_map.177), calls=%async_computation.2 | async-start | bytes 1409024 | tf_op jit(solution)/shard_map/all_to_all | solution.py:323
  102.1 0.0 copy-done.2
  102.1 0.6 gather_fusion
  102.7 0.7 bitcast_select_fusion
  103.4 9.8 %all-to-all-done.2.got = bf16[4,688,128]{2,1,0:T(8,128)(2,1)S(1)} async-done(((bf16[4,688,128]{2,1,0:T(8,128)(2,1)}), bf16[4,688,128]{2,1,0:T(8,128)(2,1)S(1)}, u32[]{:S(2)}, u32[]{:S(2)}) %all-to-all-start.2) | async-done | bytes 704544 | tf_op jit(solution)/shard_map/all_to_all | solution.py:323
  113.2 0.0 copy-done
  113.2 0.0 copy-done.1
  113.2 0.9 shard_map.178
  (6 shorter events, 0.1 us)
Async XLA Ops:
  7.3 5.5 %copy-start.3 = (bf16[80,160]{1,0:T(8,128)(2,1)S(1)}, bf16[80,160]{1,0:T(8,128)(2,1)}, u32[]{:S(2)}) copy-start(bf16[80,160]{1,0:T(8,128)(2,1)} %param.31) | copy-start | bytes 76804
  7.4 50.9 %all-to-all-start = ((bf16[4,1536,128]{2,1,0:T(8,128)(2,1)}), bf16[4,1536,128]{2,1,0:T(8,128)(2,1)S(1)}, u32[]{:S(2)}, u32[]{:S(2)}) async-start(bf16[4,1536,128]{2,1,0:T(8,128)(2,1)} %get-tuple-element.18), calls=%async_computation | async-start | bytes 3145728 | tf_op jit(solution)/shard_map/all_to_all | solution.py:297
  12.2 23.4 %collective-permute-start = (bf16[80,512]{1,0:T(8,128)(2,1)S(1)}, bf16[80,512]{1,0:T(8,128)(2,1)S(1)}, u32[]{:S(2)}, u32[]{:S(2)}) collective-permute-start(bf16[80,512]{1,0:T(8,128)(2,1)S(1)} %pad_maximum_fusion.1), channel_id=1, source_target_pairs={{0,0},{2,130},{4,260},{6,390},{8,40},{10,170},{12,300},{14,430},{1... | collective-permute-start | bytes 245768 | tf_op jit(solution)/shard_map/ppermute | solution.py:265
  35.7 22.6 %collective-permute-start.1 = (bf16[5,80,128]{2,1,0:T(8,128)(2,1)S(1)}, bf16[5,80,128]{2,1,0:T(8,128)(2,1)S(1)}, u32[]{:S(2)}, u32[]{:S(2)}) collective-permute-start(bf16[5,80,128]{2,1,0:T(8,128)(2,1)S(1)} %pad_maximum_fusion), channel_id=1, source_target_pairs={{0,0},{8,32},{16,64},{24,96},{32,8},{40,40},{48,72},{56,104},{64,1... | collective-permute-start | bytes 307208 | tf_op jit(solution)/shard_map/ppermute | solution.py:298
  62.7 3.9 %copy-start.4 = (s32[1,1,8]{2,1,0:T(1,128)S(1)}, s32[1,1,8]{2,1,0:T(1,128)}, u32[]{:S(2)}) copy-start(s32[1,1,8]{2,1,0:T(1,128)} %param.21) | copy-start | bytes 100
  62.7 20.5 %all-to-all-start.1 = ((bf16[4,896,128]{2,1,0:T(8,128)(2,1)}), bf16[4,896,128]{2,1,0:T(8,128)(2,1)S(1)}, u32[]{:S(2)}, u32[]{:S(2)}) async-start(bf16[4,896,128]{2,1,0:T(8,128)(2,1)} %shard_map.176), calls=%async_computation.1 | async-start | bytes 1835008 | tf_op jit(solution)/shard_map/all_to_all | solution.py:312
  83.2 19.0 %copy-start.2 = (bf16[1,32,288]{2,1,0:T(8,128)(2,1)S(1)}, bf16[1,32,288]{2,1,0:T(8,128)(2,1)}, u32[]{:S(2)}) copy-start(bf16[1,32,288]{2,1,0:T(8,128)(2,1)} %param.17) | copy-start | bytes 55300
  83.2 30.0 %copy-start = (bf16[16,32,160]{2,1,0:T(8,128)(2,1)S(1)}, bf16[16,32,160]{2,1,0:T(8,128)(2,1)}, u32[]{:S(2)}) copy-start(bf16[16,32,160]{2,1,0:T(8,128)(2,1)} %residual.1) | copy-start | bytes 491524
  83.2 30.0 %copy-start.1 = (bf16[1,32,160]{2,1,0:T(8,128)(2,1)S(1)}, bf16[1,32,160]{2,1,0:T(8,128)(2,1)}, u32[]{:S(2)}) copy-start(bf16[1,32,160]{2,1,0:T(8,128)(2,1)} %long_residual.1) | copy-start | bytes 30724
  85.3 27.9 %all-to-all-start.2 = ((bf16[4,688,128]{2,1,0:T(8,128)(2,1)}), bf16[4,688,128]{2,1,0:T(8,128)(2,1)S(1)}, u32[]{:S(2)}, u32[]{:S(2)}) async-start(bf16[4,688,128]{2,1,0:T(8,128)(2,1)} %shard_map.177), calls=%async_computation.2 | async-start | bytes 1409024 | tf_op jit(solution)/shard_map/all_to_all | solution.py:323

commit v9 on v8

--- a/solution.py
+++ b/solution.py
@@ -193,7 +193,7 @@
     above = lax.broadcasted_iota(jnp.int32, (TREE, TREE), 0)
     same = above == lax.broadcasted_iota(jnp.int32, (TREE, TREE), 1)
     extras = []
-    for copy in copies[:2]:
+    for copy in copies:
         copy.wait()
     for i, ids in enumerate((parents, parents_l)):
         reach = jnp.where(same | (above == ids[...]), 1.0, 0.0).astype(BF)
@@ -204,8 +204,6 @@
             extra = jnp.where(place[1] == 0, extra, 0.0)
         extra = jnp.where(lanes == 32, length[0, 0].astype(F32), extra)
         extras.append(jnp.where(lanes == 33, length_l[0, 0].astype(F32), extra).astype(BF))
-    for copy in copies[2:]:
-        copy.wait()
     for d in range(4):
         block[d, 0:288] = keys[:, :128]
         block[d, 288:576] = keys[:, 128:]
@@ -290,10 +288,9 @@
             )
         ],
     )
-    block, out_weight = lax.optimization_barrier((block, out_weight))
     cols = lax.all_gather(out_weight, "x")
     out_rows = jnp.stack([cols[k, :, :128] for k in range(4)] + [jnp.concatenate([cols[k, :, 128:] for k in range(4)], axis=1)])
-    kv, out_rows = lax.optimization_barrier((kv, out_rows))
+    block, kv, out_rows = lax.optimization_barrier((block, kv, out_rows))
     got = lax.all_to_all(block, "x", 0, 0)
     out_rows = lax.ppermute(out_rows, ("x", "a"), [(4 * i + j, 4 * j + i) for i in range(4) for j in range(4)])
     kv = lax.all_gather(kv, ("y", "c"))

time: 115 us -> 106 us (0.922)
  starting transfers between devices: 26.9 us -> 16.1 us
  blocking collectives: 61.1 us -> 62.9 us
    all_to_all x1, starting transfers between devices: 16.8 us -> 6.7 us  [on_device(): back = lax.all_to_all(send, 'x', 0, 0)]
    all_gather x1, blocking collectives: 22.6 us -> 15.8 us  [on_device(): cols = lax.all_gather(out_weight, 'x')]
    all_gather x1, blocking collectives: 16.5 us -> 21.6 us  [on_device(): out_rows = lax.all_gather(out_rows, ('b', 'c'))]
    all_gather x1, blocking collectives: 21.9 us -> 25.5 us  [on_device(): kv = lax.all_gather(kv, ('y', 'c'))]
  transfers between devices with their start and end apart: 5 -> 5, of which waited for: 1 -> 1; matrix products, arithmetic and copies ran while one was open for 1% -> 1% of each run, Pallas kernels for 0% -> 5%
where the time goes in v9:
time: 106 us
  blocking collectives  62.9 us (59%)
  starting transfers between devices  16.1 us (15%)
  Pallas kernels  12.3 us (12%)
  waiting for transfers between devices  9.82 us (9%)
  between operations  2.04 us (2%)
  other arithmetic  1.67 us (2%)
    all_gather x1, blocking collectives, on_device(): kv = lax.all_gather(kv, ('y', 'c'))  25.5 us
    all_gather x1, blocking collectives, on_device(): out_rows = lax.all_gather(out_rows, ('b', 'c'))  21.6 us
    all_gather x1, blocking collectives, on_device(): cols = lax.all_gather(out_weight, 'x')  15.8 us
    all_to_all x1, waiting for transfers between devices, on_device(): back = lax.all_to_all(send, 'x', 0, 0)  9.81 us
    all_to_all x1, starting transfers between devices, on_device(): back = lax.all_to_all(send, 'x', 0, 0)  6.7 us
    pallas_call x1, Pallas kernels, on_device(): pl.pallas_call(pack_kernel, out_shape=(jax.ShapeDtypeStruct((4, BLOCK, 12...  4.93 us
    all_to_all x1, starting transfers between devices, on_device(): got = lax.all_to_all(block, 'x', 0, 0)  4.49 us
    pallas_call x1, Pallas kernels, on_device(): pl.pallas_call(attend_kernel, out_shape=jax.ShapeDtypeStruct((4, 5 * TREE...  4.42 us
  transfers between devices with their start and end apart: 5, of which 1 were waited for; matrix products, arithmetic and copies ran while one was open for 1% of the time, Pallas kernels for 5%

profile of v9, /device:TPU:1, one launch (start us, length us, event | category | flops | bytes accessed | tf_op | source)
XLA Modules:
  0.0 105.5 jit_solution(16794102777830818639)
XLA Ops:
  0.6 0.8 pad_maximum_fusion.1
  1.4 0.1 pad_add_fusion.place
  1.5 0.7 collective-permute-start
  2.2 15.8 %all-gather = bf16[320,160]{1,0:T(8,128)(2,1)S(1)} all-gather(bf16[80,160]{1,0:T(8,128)(2,1)} %param.31), channel_id=2, replica_groups=mesh['y'=4,'x'=4,'a'=4,'b'=4,'c'=2] {'x'}, dimensions={0}, use_global_device_ids=true | all-gather | bytes 128000 | tf_op jit(solution)/shard_map/all_gather | solution.py:291
  19.3 0.1 maximum_bitcast_fusion
  19.4 4.9 %shard_map.175 = (bf16[4,1536,128]{2,1,0:T(8,128)(2,1)}, bf16[256,128]{1,0:T(8,128)(2,1)S(1)}, bf16[128,128]{1,0:T(8,128)(2,1)S(1)}) custom-call(s32[2]{0:T(128)S(1)} %pad_add_fusion.place, s32[1,1]{1,0:T(1,128)S(6)} %copy.19.length, s32[1,1]{1,0:T(1,128)S(6)} %copy.20.length_l, s32[1,32]{1,0:T(1,128)} %bitcast.46, s32[1,32]{1,0:T(1,128)} %refs_1_.1, ...), custom_call_target="tpu_custom_call" | custom-call | flops 6000000000 | bytes 18000000 | tf_op jit(solution)/shard_map/pallas_call | solution.py:265
  24.4 0.0 collective-permute-done
  24.4 4.5 %all-to-all-start = ((bf16[4,1536,128]{2,1,0:T(8,128)(2,1)}), bf16[4,1536,128]{2,1,0:T(8,128)(2,1)S(1)}, u32[]{:S(2)}, u32[]{:S(2)}) async-start(bf16[4,1536,128]{2,1,0:T(8,128)(2,1)} %get-tuple-element.18), calls=%async_computation | async-start | bytes 3145728 | tf_op jit(solution)/shard_map/all_to_all | solution.py:294
  28.9 0.7 collective-permute-start.1
  29.6 25.5 %all-gather.1 = bf16[640,512]{1,0:T(8,128)(2,1)S(1)} all-gather(bf16[80,512]{1,0:T(8,128)(2,1)S(1)} %collective-permute-done), channel_id=3, replica_groups=mesh['y'=4,'x'=4,'a'=4,'b'=4,'c'=2] {'y','c'}, dimensions={0}, use_global_device_ids=true | all-gather | bytes 737280 | tf_op jit(solution)/shard_map/all_gather | solution.py:296
  55.1 0.0 collective-permute-done.1
  55.1 0.0 all-to-all-done.got
  55.1 4.4 %shard_map.176 = bf16[4,896,128]{2,1,0:T(8,128)(2,1)} custom-call(bf16[4,1536,128]{2,1,0:T(8,128)(2,1)S(1)} %all-to-all-done.got, bf16[256,128]{1,0:T(8,128)(2,1)S(1)} %get-tuple-element.19.query_l, bf16[128,128]{1,0:T(8,128)(2,1)S(1)} %get-tuple-element.20.tree_l, bf16[4,2,80,512]{3,2,1,0:T(8,128)(2,1)S(1)} %bitcast.36), custom_call_target="tpu_custom_call" | custom-call | flops 6000000000 | bytes 18000000 | tf_op jit(solution)/shard_map/pallas_call | solution.py:300
  59.5 0.0 copy-start.3
  59.5 3.6 %all-to-all-start.1 = ((bf16[4,896,128]{2,1,0:T(8,128)(2,1)}), bf16[4,896,128]{2,1,0:T(8,128)(2,1)S(1)}, u32[]{:S(2)}, u32[]{:S(2)}) async-start(bf16[4,896,128]{2,1,0:T(8,128)(2,1)} %shard_map.176), calls=%async_computation.1 | async-start | bytes 1835008 | tf_op jit(solution)/shard_map/all_to_all | solution.py:309
  63.1 0.0 copy-done.3
  63.1 21.6 %all-gather.2 = bf16[40,80,128]{2,1,0:T(8,128)(2,1)S(1)} all-gather(bf16[5,80,128]{2,1,0:T(8,128)(2,1)S(1)} %collective-permute-done.1), channel_id=4, replica_groups=mesh['y'=4,'x'=4,'a'=4,'b'=4,'c'=2] {'b','c'}, dimensions={0}, use_global_device_ids=true | all-gather | bytes 921600 | tf_op jit(solution)/shard_map/all_gather | solution.py:310
  84.8 0.0 all-to-all-done.1.got
  84.8 0.0 copy-start.2
  84.8 0.0 copy-start
  84.8 0.0 copy-start.1
  84.8 2.1 %shard_map.177 = bf16[4,688,128]{2,1,0:T(8,128)(2,1)} custom-call(bf16[4,896,128]{2,1,0:T(8,128)(2,1)S(1)} %all-to-all-done.1.got, bf16[4,2,5,80,128]{4,3,2,1,0:T(8,128)(2,1)S(1)} %bitcast.35), custom_call_target="tpu_custom_call" | custom-call | tf_op jit(solution)/shard_map/pallas_call | solution.py:312
  86.9 6.7 %all-to-all-start.2 = ((bf16[4,688,128]{2,1,0:T(8,128)(2,1)}), bf16[4,688,128]{2,1,0:T(8,128)(2,1)S(1)}, u32[]{:S(2)}, u32[]{:S(2)}) async-start(bf16[4,688,128]{2,1,0:T(8,128)(2,1)} %shard_map.177), calls=%async_computation.2 | async-start | bytes 1409024 | tf_op jit(solution)/shard_map/all_to_all | solution.py:320
  93.6 0.0 copy-done.2
  93.6 0.6 gather_fusion
  94.2 0.7 bitcast_select_fusion
  94.9 9.8 %all-to-all-done.2.got = bf16[4,688,128]{2,1,0:T(8,128)(2,1)S(1)} async-done(((bf16[4,688,128]{2,1,0:T(8,128)(2,1)}), bf16[4,688,128]{2,1,0:T(8,128)(2,1)S(1)}, u32[]{:S(2)}, u32[]{:S(2)}) %all-to-all-start.2) | async-done | bytes 704544 | tf_op jit(solution)/shard_map/all_to_all | solution.py:320
  104.7 0.0 copy-done
  104.7 0.0 copy-done.1
  104.7 0.9 shard_map.178
  (6 shorter events, 0.1 us)
Async XLA Ops:
  1.5 22.9 %collective-permute-start = (bf16[80,512]{1,0:T(8,128)(2,1)S(1)}, bf16[80,512]{1,0:T(8,128)(2,1)S(1)}, u32[]{:S(2)}, u32[]{:S(2)}) collective-permute-start(bf16[80,512]{1,0:T(8,128)(2,1)S(1)} %pad_maximum_fusion.1), channel_id=1, source_target_pairs={{0,0},{2,130},{4,260},{6,390},{8,40},{10,170},{12,300},{14,430},{1... | collective-permute-start | bytes 245768 | tf_op jit(solution)/shard_map/ppermute | solution.py:263
  24.4 30.7 %all-to-all-start = ((bf16[4,1536,128]{2,1,0:T(8,128)(2,1)}), bf16[4,1536,128]{2,1,0:T(8,128)(2,1)S(1)}, u32[]{:S(2)}, u32[]{:S(2)}) async-start(bf16[4,1536,128]{2,1,0:T(8,128)(2,1)} %get-tuple-element.18), calls=%async_computation | async-start | bytes 3145728 | tf_op jit(solution)/shard_map/all_to_all | solution.py:294
  28.9 26.2 %collective-permute-start.1 = (bf16[5,80,128]{2,1,0:T(8,128)(2,1)S(1)}, bf16[5,80,128]{2,1,0:T(8,128)(2,1)S(1)}, u32[]{:S(2)}, u32[]{:S(2)}) collective-permute-start(bf16[5,80,128]{2,1,0:T(8,128)(2,1)S(1)} %pad_maximum_fusion), channel_id=1, source_target_pairs={{0,0},{8,32},{16,64},{24,96},{32,8},{40,40},{48,72},{56,104},{64,1... | collective-permute-start | bytes 307208 | tf_op jit(solution)/shard_map/ppermute | solution.py:295
  59.5 3.6 %copy-start.3 = (s32[1,1,8]{2,1,0:T(1,128)S(1)}, s32[1,1,8]{2,1,0:T(1,128)}, u32[]{:S(2)}) copy-start(s32[1,1,8]{2,1,0:T(1,128)} %param.21) | copy-start | bytes 100
  59.5 25.3 %all-to-all-start.1 = ((bf16[4,896,128]{2,1,0:T(8,128)(2,1)}), bf16[4,896,128]{2,1,0:T(8,128)(2,1)S(1)}, u32[]{:S(2)}, u32[]{:S(2)}) async-start(bf16[4,896,128]{2,1,0:T(8,128)(2,1)} %shard_map.176), calls=%async_computation.1 | async-start | bytes 1835008 | tf_op jit(solution)/shard_map/all_to_all | solution.py:309
  84.8 8.8 %copy-start.2 = (bf16[1,32,288]{2,1,0:T(8,128)(2,1)S(1)}, bf16[1,32,288]{2,1,0:T(8,128)(2,1)}, u32[]{:S(2)}) copy-start(bf16[1,32,288]{2,1,0:T(8,128)(2,1)} %param.17) | copy-start | bytes 55300
  84.8 19.9 %copy-start = (bf16[16,32,160]{2,1,0:T(8,128)(2,1)S(1)}, bf16[16,32,160]{2,1,0:T(8,128)(2,1)}, u32[]{:S(2)}) copy-start(bf16[16,32,160]{2,1,0:T(8,128)(2,1)} %residual.1) | copy-start | bytes 491524
  84.8 19.9 %copy-start.1 = (bf16[1,32,160]{2,1,0:T(8,128)(2,1)S(1)}, bf16[1,32,160]{2,1,0:T(8,128)(2,1)}, u32[]{:S(2)}) copy-start(bf16[1,32,160]{2,1,0:T(8,128)(2,1)} %long_residual.1) | copy-start | bytes 30724
  86.9 17.8 %all-to-all-start.2 = ((bf16[4,688,128]{2,1,0:T(8,128)(2,1)}), bf16[4,688,128]{2,1,0:T(8,128)(2,1)S(1)}, u32[]{:S(2)}, u32[]{:S(2)}) async-start(bf16[4,688,128]{2,1,0:T(8,128)(2,1)} %shard_map.177), calls=%async_computation.2 | async-start | bytes 1409024 | tf_op jit(solution)/shard_map/all_to_all | solution.py:320

commit v10 on v8

--- a/solution.py
+++ b/solution.py
@@ -142,10 +142,14 @@
         wide = (dot(high, select) + dot(low, select)).reshape(4, TREE, 128)
         piece = got[:, at + 4 * TREE : at + 5 * TREE].astype(F32) * wide
         rows[16 * TREE : 17 * TREE, cols] = jnp.sum(piece, axis=0).astype(BF)
-    rest = dot(rows[...], weight[:, :, 4].reshape(SPAN, 128))
+    blocks = [weight[:, :, k].reshape(SPAN, 128) for k in range(5)]
+    for k in (0, 2):
+        both = dot(rows[...], jnp.concatenate(blocks[k : k + 2], axis=1)).astype(BF)
+        send[k, :TOKENS] = both[:, :128]
+        send[k + 1, :TOKENS] = both[:, 128:]
+    rest = dot(rows[...], blocks[4])
     lanes = lax.broadcasted_iota(jnp.int32, (QUARTER, 128), 1) // 32
     for k in range(4):
-        send[k, :TOKENS] = dot(rows[...], weight[:, :, k].reshape(SPAN, 128)).astype(BF)
         packed = jnp.zeros((QUARTER, 128), F32)
         for g in range(4):
             part = rest[QUARTER * g : QUARTER * (g + 1)]
@@ -227,10 +231,11 @@
         return jnp.where(col < 256, nope, rope)
 
     sort = onehot(384, 384, lambda row, col: source(col) == row)
+    windows = [slice(384 * w, 384 * (w + 1)) for w in range(HEADS // 4)]
+    sorted_all = dot(jnp.concatenate([q[:, cols] for cols in windows for q in (queries, queries_l)], axis=0), sort)
     rope = []
     for w in range(HEADS // 4):
-        cols = slice(384 * w, 384 * (w + 1))
-        moved = dot(jnp.concatenate([queries[:, cols], queries_l[:, cols]], axis=0), sort)
+        moved = sorted_all[2 * TREE * w : 2 * TREE * (w + 1)]
         rope.append(moved[:, 256:])
         for half in range(2):
             s, p = divmod(2 * w + half, SLICE // 2)
@@ -290,10 +295,9 @@
             )
         ],
     )
-    block, out_weight = lax.optimization_barrier((block, out_weight))
     cols = lax.all_gather(out_weight, "x")
     out_rows = jnp.stack([cols[k, :, :128] for k in range(4)] + [jnp.concatenate([cols[k, :, 128:] for k in range(4)], axis=1)])
-    kv, out_rows = lax.optimization_barrier((kv, out_rows))
+    block, kv, out_rows = lax.optimization_barrier((block, kv, out_rows))
     got = lax.all_to_all(block, "x", 0, 0)
     out_rows = lax.ppermute(out_rows, ("x", "a"), [(4 * i + j, 4 * j + i) for i in range(4) for j in range(4)])
     kv = lax.all_gather(kv, ("y", "c"))

time: 115 us -> 106 us (0.922)
  starting transfers between devices: 26.9 us -> 16.6 us
  blocking collectives: 61.1 us -> 62.9 us
    all_to_all x1, starting transfers between devices: 16.8 us -> 7.15 us  [on_device(): back = lax.all_to_all(send, 'x', 0, 0)]
    all_gather x1, blocking collectives: 22.6 us -> 15.8 us  [on_device(): cols = lax.all_gather(out_weight, 'x')]
    all_gather x1, blocking collectives: 16.5 us -> 21.6 us  [on_device(): out_rows = lax.all_gather(out_rows, ('b', 'c'))]
    all_gather x1, blocking collectives: 21.9 us -> 25.5 us  [on_device(): kv = lax.all_gather(kv, ('y', 'c'))]
  transfers between devices with their start and end apart: 5 -> 5, of which waited for: 1 -> 1; matrix products, arithmetic and copies ran while one was open for 1% -> 1% of each run, Pallas kernels for 0% -> 4%
where the time goes in v10:
time: 106 us; the launch traced here: 105 us
  blocking collectives  62.9 us (59%)
  starting transfers between devices  16.6 us (16%)
  Pallas kernels  11.6 us (11%)
  waiting for transfers between devices  9.82 us (9%)
  between operations  2.04 us (2%)
  other arithmetic  1.67 us (2%)
    all_gather x1, blocking collectives, on_device(): kv = lax.all_gather(kv, ('y', 'c'))  25.5 us
    all_gather x1, blocking collectives, on_device(): out_rows = lax.all_gather(out_rows, ('b', 'c'))  21.6 us
    all_gather x1, blocking collectives, on_device(): cols = lax.all_gather(out_weight, 'x')  15.8 us
    all_to_all x1, waiting for transfers between devices, on_device(): back = lax.all_to_all(send, 'x', 0, 0)  9.81 us
    all_to_all x1, starting transfers between devices, on_device(): back = lax.all_to_all(send, 'x', 0, 0)  7.15 us
    all_to_all x1, starting transfers between devices, on_device(): got = lax.all_to_all(block, 'x', 0, 0)  4.49 us
    pallas_call x1, Pallas kernels, on_device(): pl.pallas_call(attend_kernel, out_shape=jax.ShapeDtypeStruct((4, 5 * TREE...  4.42 us
    pallas_call x1, Pallas kernels, on_device(): pl.pallas_call(pack_kernel, out_shape=(jax.ShapeDtypeStruct((4, BLOCK, 12...  4.4 us
  transfers between devices with their start and end apart: 5, of which 1 were waited for; matrix products, arithmetic and copies ran while one was open for 1% of the time, Pallas kernels for 4%

profile of v10, /device:TPU:1, one launch (start us, length us, event | category | flops | bytes accessed | tf_op | source)
XLA Modules:
  0.0 105.2 jit_solution(5089275840760425529)
XLA Ops:
  0.6 0.8 pad_maximum_fusion.1
  1.4 0.1 pad_add_fusion.place
  1.5 0.7 collective-permute-start
  2.2 15.8 %all-gather = bf16[320,160]{1,0:T(8,128)(2,1)S(1)} all-gather(bf16[80,160]{1,0:T(8,128)(2,1)} %param.31), channel_id=2, replica_groups=mesh['y'=4,'x'=4,'a'=4,'b'=4,'c'=2] {'x'}, dimensions={0}, use_global_device_ids=true | all-gather | bytes 128000 | tf_op jit(solution)/shard_map/all_gather | solution.py:298
  19.3 0.1 maximum_bitcast_fusion
  19.4 4.4 %shard_map.175 = (bf16[4,1536,128]{2,1,0:T(8,128)(2,1)}, bf16[256,128]{1,0:T(8,128)(2,1)S(1)}, bf16[128,128]{1,0:T(8,128)(2,1)S(1)}) custom-call(s32[2]{0:T(128)S(1)} %pad_add_fusion.place, s32[1,1]{1,0:T(1,128)S(6)} %copy.19.length, s32[1,1]{1,0:T(1,128)S(6)} %copy.20.length_l, s32[1,32]{1,0:T(1,128)} %bitcast.46, s32[1,32]{1,0:T(1,128)} %refs_1_.1, ...), custom_call_target="tpu_custom_call" | custom-call | flops 6000000000 | bytes 18000000 | tf_op jit(solution)/shard_map/pallas_call | solution.py:272
  23.9 0.0 collective-permute-done
  23.9 4.5 %all-to-all-start = ((bf16[4,1536,128]{2,1,0:T(8,128)(2,1)}), bf16[4,1536,128]{2,1,0:T(8,128)(2,1)S(1)}, u32[]{:S(2)}, u32[]{:S(2)}) async-start(bf16[4,1536,128]{2,1,0:T(8,128)(2,1)} %get-tuple-element.18), calls=%async_computation | async-start | bytes 3145728 | tf_op jit(solution)/shard_map/all_to_all | solution.py:301
  28.4 0.7 collective-permute-start.1
  29.0 25.5 %all-gather.1 = bf16[640,512]{1,0:T(8,128)(2,1)S(1)} all-gather(bf16[80,512]{1,0:T(8,128)(2,1)S(1)} %collective-permute-done), channel_id=3, replica_groups=mesh['y'=4,'x'=4,'a'=4,'b'=4,'c'=2] {'y','c'}, dimensions={0}, use_global_device_ids=true | all-gather | bytes 737280 | tf_op jit(solution)/shard_map/all_gather | solution.py:303
  54.5 0.0 collective-permute-done.1
  54.5 0.0 all-to-all-done.got
  54.5 4.4 %shard_map.176 = bf16[4,896,128]{2,1,0:T(8,128)(2,1)} custom-call(bf16[4,1536,128]{2,1,0:T(8,128)(2,1)S(1)} %all-to-all-done.got, bf16[256,128]{1,0:T(8,128)(2,1)S(1)} %get-tuple-element.19.query_l, bf16[128,128]{1,0:T(8,128)(2,1)S(1)} %get-tuple-element.20.tree_l, bf16[4,2,80,512]{3,2,1,0:T(8,128)(2,1)S(1)} %bitcast.36), custom_call_target="tpu_custom_call" | custom-call | flops 6000000000 | bytes 18000000 | tf_op jit(solution)/shard_map/pallas_call | solution.py:307
  58.9 0.0 copy-start.3
  58.9 3.6 %all-to-all-start.1 = ((bf16[4,896,128]{2,1,0:T(8,128)(2,1)}), bf16[4,896,128]{2,1,0:T(8,128)(2,1)S(1)}, u32[]{:S(2)}, u32[]{:S(2)}) async-start(bf16[4,896,128]{2,1,0:T(8,128)(2,1)} %shard_map.176), calls=%async_computation.1 | async-start | bytes 1835008 | tf_op jit(solution)/shard_map/all_to_all | solution.py:316
  62.6 0.0 copy-done.3
  62.6 21.6 %all-gather.2 = bf16[40,80,128]{2,1,0:T(8,128)(2,1)S(1)} all-gather(bf16[5,80,128]{2,1,0:T(8,128)(2,1)S(1)} %collective-permute-done.1), channel_id=4, replica_groups=mesh['y'=4,'x'=4,'a'=4,'b'=4,'c'=2] {'b','c'}, dimensions={0}, use_global_device_ids=true | all-gather | bytes 921600 | tf_op jit(solution)/shard_map/all_gather | solution.py:317
  84.2 0.0 all-to-all-done.1.got
  84.2 0.0 copy-start.2
  84.2 0.0 copy-start
  84.2 0.0 copy-start.1
  84.2 1.9 %shard_map.177 = bf16[4,688,128]{2,1,0:T(8,128)(2,1)} custom-call(bf16[4,896,128]{2,1,0:T(8,128)(2,1)S(1)} %all-to-all-done.1.got, bf16[4,2,5,80,128]{4,3,2,1,0:T(8,128)(2,1)S(1)} %bitcast.35), custom_call_target="tpu_custom_call" | custom-call | tf_op jit(solution)/shard_map/pallas_call | solution.py:319
  86.1 7.1 %all-to-all-start.2 = ((bf16[4,688,128]{2,1,0:T(8,128)(2,1)}), bf16[4,688,128]{2,1,0:T(8,128)(2,1)S(1)}, u32[]{:S(2)}, u32[]{:S(2)}) async-start(bf16[4,688,128]{2,1,0:T(8,128)(2,1)} %shard_map.177), calls=%async_computation.2 | async-start | bytes 1409024 | tf_op jit(solution)/shard_map/all_to_all | solution.py:327
  93.3 0.0 copy-done.2
  93.3 0.6 gather_fusion
  93.9 0.7 bitcast_select_fusion
  94.5 9.8 %all-to-all-done.2.got = bf16[4,688,128]{2,1,0:T(8,128)(2,1)S(1)} async-done(((bf16[4,688,128]{2,1,0:T(8,128)(2,1)}), bf16[4,688,128]{2,1,0:T(8,128)(2,1)S(1)}, u32[]{:S(2)}, u32[]{:S(2)}) %all-to-all-start.2) | async-done | bytes 704544 | tf_op jit(solution)/shard_map/all_to_all | solution.py:327
  104.3 0.0 copy-done
  104.3 0.0 copy-done.1
  104.3 0.9 shard_map.178
  (6 shorter events, 0.1 us)
Async XLA Ops:
  1.5 22.3 %collective-permute-start = (bf16[80,512]{1,0:T(8,128)(2,1)S(1)}, bf16[80,512]{1,0:T(8,128)(2,1)S(1)}, u32[]{:S(2)}, u32[]{:S(2)}) collective-permute-start(bf16[80,512]{1,0:T(8,128)(2,1)S(1)} %pad_maximum_fusion.1), channel_id=1, source_target_pairs={{0,0},{2,130},{4,260},{6,390},{8,40},{10,170},{12,300},{14,430},{1... | collective-permute-start | bytes 245768 | tf_op jit(solution)/shard_map/ppermute | solution.py:270
  23.9 30.7 %all-to-all-start = ((bf16[4,1536,128]{2,1,0:T(8,128)(2,1)}), bf16[4,1536,128]{2,1,0:T(8,128)(2,1)S(1)}, u32[]{:S(2)}, u32[]{:S(2)}) async-start(bf16[4,1536,128]{2,1,0:T(8,128)(2,1)} %get-tuple-element.18), calls=%async_computation | async-start | bytes 3145728 | tf_op jit(solution)/shard_map/all_to_all | solution.py:301
  28.4 26.2 %collective-permute-start.1 = (bf16[5,80,128]{2,1,0:T(8,128)(2,1)S(1)}, bf16[5,80,128]{2,1,0:T(8,128)(2,1)S(1)}, u32[]{:S(2)}, u32[]{:S(2)}) collective-permute-start(bf16[5,80,128]{2,1,0:T(8,128)(2,1)S(1)} %pad_maximum_fusion), channel_id=1, source_target_pairs={{0,0},{8,32},{16,64},{24,96},{32,8},{40,40},{48,72},{56,104},{64,1... | collective-permute-start | bytes 307208 | tf_op jit(solution)/shard_map/ppermute | solution.py:302
  58.9 3.6 %copy-start.3 = (s32[1,1,8]{2,1,0:T(1,128)S(1)}, s32[1,1,8]{2,1,0:T(1,128)}, u32[]{:S(2)}) copy-start(s32[1,1,8]{2,1,0:T(1,128)} %param.21) | copy-start | bytes 100
  58.9 25.3 %all-to-all-start.1 = ((bf16[4,896,128]{2,1,0:T(8,128)(2,1)}), bf16[4,896,128]{2,1,0:T(8,128)(2,1)S(1)}, u32[]{:S(2)}, u32[]{:S(2)}) async-start(bf16[4,896,128]{2,1,0:T(8,128)(2,1)} %shard_map.176), calls=%async_computation.1 | async-start | bytes 1835008 | tf_op jit(solution)/shard_map/all_to_all | solution.py:316
  84.2 9.0 %copy-start.2 = (bf16[1,32,288]{2,1,0:T(8,128)(2,1)S(1)}, bf16[1,32,288]{2,1,0:T(8,128)(2,1)}, u32[]{:S(2)}) copy-start(bf16[1,32,288]{2,1,0:T(8,128)(2,1)} %param.17) | copy-start | bytes 55300
  84.2 20.1 %copy-start = (bf16[16,32,160]{2,1,0:T(8,128)(2,1)S(1)}, bf16[16,32,160]{2,1,0:T(8,128)(2,1)}, u32[]{:S(2)}) copy-start(bf16[16,32,160]{2,1,0:T(8,128)(2,1)} %residual.1) | copy-start | bytes 491524
  84.2 20.1 %copy-start.1 = (bf16[1,32,160]{2,1,0:T(8,128)(2,1)S(1)}, bf16[1,32,160]{2,1,0:T(8,128)(2,1)}, u32[]{:S(2)}) copy-start(bf16[1,32,160]{2,1,0:T(8,128)(2,1)} %long_residual.1) | copy-start | bytes 30724
  86.1 18.2 %all-to-all-start.2 = ((bf16[4,688,128]{2,1,0:T(8,128)(2,1)}), bf16[4,688,128]{2,1,0:T(8,128)(2,1)S(1)}, u32[]{:S(2)}, u32[]{:S(2)}) async-start(bf16[4,688,128]{2,1,0:T(8,128)(2,1)} %shard_map.177), calls=%async_computation.2 | async-start | bytes 1409024 | tf_op jit(solution)/shard_map/all_to_all | solution.py:327

commit v11 on v10

--- a/solution.py
+++ b/solution.py
@@ -266,8 +266,6 @@
     y, x = lax.axis_index("y"), lax.axis_index("x")
     place = jnp.stack([x, y]).astype(jnp.int32)
     pairs = [(r * 16 + z, ((z % 4) * 4 + z // 4) * 16 + (z + r) % 16) for r in range(16) for z in range(16)]
-    kv, place = lax.optimization_barrier((jnp.concatenate([key_up, value_up], axis=1), place))
-    kv = lax.ppermute(kv, ("y", "x", "a", "b"), pairs)
     rows = 8 * TREE
     block, query_l, tree_l = pl.pallas_call(
         pack_kernel,
@@ -295,6 +293,8 @@
             )
         ],
     )
+    kv, block = lax.optimization_barrier((jnp.concatenate([key_up, value_up], axis=1), block))
+    kv = lax.ppermute(kv, ("y", "x", "a", "b"), pairs)
     cols = lax.all_gather(out_weight, "x")
     out_rows = jnp.stack([cols[k, :, :128] for k in range(4)] + [jnp.concatenate([cols[k, :, 128:] for k in range(4)], axis=1)])
     block, kv, out_rows = lax.optimization_barrier((block, kv, out_rows))

time: 106 us -> 111 us (1.047)
  starting transfers between devices: 16.6 us -> 26 us
  blocking collectives: 62.9 us -> 59.2 us
    all_to_all x1, starting transfers between devices: 7.15 us -> 11.9 us  [on_device(): back = lax.all_to_all(send, 'x', 0, 0)]
    all_to_all x1, starting transfers between devices: 4.49 us -> 8.85 us  [on_device(): got = lax.all_to_all(block, 'x', 0, 0)]
    all_gather x1, blocking collectives: 25.5 us -> 21.4 us  [on_device(): kv = lax.all_gather(kv, ('y', 'c'))]
  transfers between devices with their start and end apart: 5 -> 5, of which waited for: 1 -> 1; matrix products, arithmetic and copies ran while one was open for 1% -> 1% of each run, Pallas kernels for 4% -> 0%
where the time goes in v11:
time: 111 us
  blocking collectives  59.2 us (53%)
  starting transfers between devices  26 us (23%)
  Pallas kernels  11.5 us (10%)
  waiting for transfers between devices  9.82 us (9%)
  between operations  2.02 us (2%)
  other arithmetic  1.67 us (2%)
    all_gather x1, blocking collectives, on_device(): out_rows = lax.all_gather(out_rows, ('b', 'c'))  22.5 us
    all_gather x1, blocking collectives, on_device(): kv = lax.all_gather(kv, ('y', 'c'))  21.4 us
    all_gather x1, blocking collectives, on_device(): cols = lax.all_gather(out_weight, 'x')  15.3 us
    all_to_all x1, starting transfers between devices, on_device(): back = lax.all_to_all(send, 'x', 0, 0)  11.9 us
    all_to_all x1, waiting for transfers between devices, on_device(): back = lax.all_to_all(send, 'x', 0, 0)  9.81 us
    all_to_all x1, starting transfers between devices, on_device(): got = lax.all_to_all(block, 'x', 0, 0)  8.85 us
    pallas_call x1, Pallas kernels, on_device(): pl.pallas_call(attend_kernel, out_shape=jax.ShapeDtypeStruct((4, 5 * TREE...  4.41 us
    pallas_call x1, Pallas kernels, on_device(): pl.pallas_call(pack_kernel, out_shape=(jax.ShapeDtypeStruct((4, BLOCK, 12...  4.39 us
  transfers between devices with their start and end apart: 5, of which 1 were waited for; matrix products, arithmetic and copies ran while one was open for 1% of the time, Pallas kernels for 0%

profile of v11, /device:TPU:1, one launch (start us, length us, event | category | flops | bytes accessed | tf_op | source)
XLA Modules:
  0.0 110.9 jit_solution(2425929899489574160)
XLA Ops:
  1.9 0.8 pad_maximum_fusion.1
  2.7 0.1 pad_add_fusion.place
  2.8 0.0 copy-start.3
  2.8 4.4 %shard_map.175 = (bf16[4,1536,128]{2,1,0:T(8,128)(2,1)}, bf16[256,128]{1,0:T(8,128)(2,1)S(1)}, bf16[128,128]{1,0:T(8,128)(2,1)S(1)}) custom-call(s32[2]{0:T(128)S(1)} %pad_add_fusion.place, s32[1,1]{1,0:T(1,128)S(6)} %copy.19.length, s32[1,1]{1,0:T(1,128)S(6)} %copy.20.length_l, s32[1,32]{1,0:T(1,128)} %bitcast.46, s32[1,32]{1,0:T(1,128)} %refs_1_.1, ...), custom_call_target="tpu_custom_call" | custom-call | flops 6000000000 | bytes 18000000 | tf_op jit(solution)/shard_map/pallas_call | solution.py:270
  7.2 0.7 collective-permute-start
  7.9 0.0 copy-done.3
  7.9 15.3 %all-gather = bf16[320,160]{1,0:T(8,128)(2,1)S(1)} all-gather(bf16[80,160]{1,0:T(8,128)(2,1)S(1)} %copy-done.3), channel_id=2, replica_groups=mesh['y'=4,'x'=4,'a'=4,'b'=4,'c'=2] {'x'}, dimensions={0}, use_global_device_ids=true | all-gather | bytes 128000 | tf_op jit(solution)/shard_map/all_gather | solution.py:298
  23.2 0.1 maximum_bitcast_fusion
  23.4 0.0 collective-permute-done
  23.4 8.9 %all-to-all-start = ((bf16[4,1536,128]{2,1,0:T(8,128)(2,1)}), bf16[4,1536,128]{2,1,0:T(8,128)(2,1)S(1)}, u32[]{:S(2)}, u32[]{:S(2)}) async-start(bf16[4,1536,128]{2,1,0:T(8,128)(2,1)} %get-tuple-element.18), calls=%async_computation | async-start | bytes 3145728 | tf_op jit(solution)/shard_map/all_to_all | solution.py:301
  32.2 0.7 collective-permute-start.1
  32.9 21.4 %all-gather.1 = bf16[640,512]{1,0:T(8,128)(2,1)S(1)} all-gather(bf16[80,512]{1,0:T(8,128)(2,1)S(1)} %collective-permute-done), channel_id=3, replica_groups=mesh['y'=4,'x'=4,'a'=4,'b'=4,'c'=2] {'y','c'}, dimensions={0}, use_global_device_ids=true | all-gather | bytes 737280 | tf_op jit(solution)/shard_map/all_gather | solution.py:303
  54.3 0.0 collective-permute-done.1
  54.3 0.0 all-to-all-done.got
  54.3 4.4 %shard_map.176 = bf16[4,896,128]{2,1,0:T(8,128)(2,1)} custom-call(bf16[4,1536,128]{2,1,0:T(8,128)(2,1)S(1)} %all-to-all-done.got, bf16[256,128]{1,0:T(8,128)(2,1)S(1)} %get-tuple-element.19.query_l, bf16[128,128]{1,0:T(8,128)(2,1)S(1)} %get-tuple-element.20.tree_l, bf16[4,2,80,512]{3,2,1,0:T(8,128)(2,1)S(1)} %bitcast.36), custom_call_target="tpu_custom_call" | custom-call | flops 6000000000 | bytes 18000000 | tf_op jit(solution)/shard_map/pallas_call | solution.py:307
  58.7 0.0 copy-start.4
  58.7 4.0 %all-to-all-start.1 = ((bf16[4,896,128]{2,1,0:T(8,128)(2,1)}), bf16[4,896,128]{2,1,0:T(8,128)(2,1)S(1)}, u32[]{:S(2)}, u32[]{:S(2)}) async-start(bf16[4,896,128]{2,1,0:T(8,128)(2,1)} %shard_map.176), calls=%async_computation.1 | async-start | bytes 1835008 | tf_op jit(solution)/shard_map/all_to_all | solution.py:316
  62.7 0.0 copy-done.4
  62.7 22.5 %all-gather.2 = bf16[40,80,128]{2,1,0:T(8,128)(2,1)S(1)} all-gather(bf16[5,80,128]{2,1,0:T(8,128)(2,1)S(1)} %collective-permute-done.1), channel_id=4, replica_groups=mesh['y'=4,'x'=4,'a'=4,'b'=4,'c'=2] {'b','c'}, dimensions={0}, use_global_device_ids=true | all-gather | bytes 921600 | tf_op jit(solution)/shard_map/all_gather | solution.py:317
  85.2 0.0 all-to-all-done.1.got
  85.2 0.0 copy-start.2
  85.2 0.0 copy-start
  85.2 0.0 copy-start.1
  85.2 1.9 %shard_map.177 = bf16[4,688,128]{2,1,0:T(8,128)(2,1)} custom-call(bf16[4,896,128]{2,1,0:T(8,128)(2,1)S(1)} %all-to-all-done.1.got, bf16[4,2,5,80,128]{4,3,2,1,0:T(8,128)(2,1)S(1)} %bitcast.35), custom_call_target="tpu_custom_call" | custom-call | tf_op jit(solution)/shard_map/pallas_call | solution.py:319
  87.1 11.9 %all-to-all-start.2 = ((bf16[4,688,128]{2,1,0:T(8,128)(2,1)}), bf16[4,688,128]{2,1,0:T(8,128)(2,1)S(1)}, u32[]{:S(2)}, u32[]{:S(2)}) async-start(bf16[4,688,128]{2,1,0:T(8,128)(2,1)} %shard_map.177), calls=%async_computation.2 | async-start | bytes 1409024 | tf_op jit(solution)/shard_map/all_to_all | solution.py:327
  99.0 0.0 copy-done.2
  99.0 0.6 gather_fusion
  99.6 0.7 bitcast_select_fusion
  100.2 9.8 %all-to-all-done.2.got = bf16[4,688,128]{2,1,0:T(8,128)(2,1)S(1)} async-done(((bf16[4,688,128]{2,1,0:T(8,128)(2,1)}), bf16[4,688,128]{2,1,0:T(8,128)(2,1)S(1)}, u32[]{:S(2)}, u32[]{:S(2)}) %all-to-all-start.2) | async-done | bytes 704544 | tf_op jit(solution)/shard_map/all_to_all | solution.py:327
  110.0 0.0 copy-done
  110.0 0.0 copy-done.1
  110.0 0.9 shard_map.178
  (6 shorter events, 0.1 us)
Async XLA Ops:
  2.8 5.1 %copy-start.3 = (bf16[80,160]{1,0:T(8,128)(2,1)S(1)}, bf16[80,160]{1,0:T(8,128)(2,1)}, u32[]{:S(2)}) copy-start(bf16[80,160]{1,0:T(8,128)(2,1)} %param.31) | copy-start | bytes 76804
  7.2 16.2 %collective-permute-start = (bf16[80,512]{1,0:T(8,128)(2,1)S(1)}, bf16[80,512]{1,0:T(8,128)(2,1)S(1)}, u32[]{:S(2)}, u32[]{:S(2)}) collective-permute-start(bf16[80,512]{1,0:T(8,128)(2,1)S(1)} %pad_maximum_fusion.1), channel_id=1, source_target_pairs={{0,0},{2,130},{4,260},{6,390},{8,40},{10,170},{12,300},{14,430},{1... | collective-permute-start | bytes 245768 | tf_op jit(solution)/shard_map/ppermute | solution.py:297
  23.4 30.9 %all-to-all-start = ((bf16[4,1536,128]{2,1,0:T(8,128)(2,1)}), bf16[4,1536,128]{2,1,0:T(8,128)(2,1)S(1)}, u32[]{:S(2)}, u32[]{:S(2)}) async-start(bf16[4,1536,128]{2,1,0:T(8,128)(2,1)} %get-tuple-element.18), calls=%async_computation | async-start | bytes 3145728 | tf_op jit(solution)/shard_map/all_to_all | solution.py:301
  32.2 22.1 %collective-permute-start.1 = (bf16[5,80,128]{2,1,0:T(8,128)(2,1)S(1)}, bf16[5,80,128]{2,1,0:T(8,128)(2,1)S(1)}, u32[]{:S(2)}, u32[]{:S(2)}) collective-permute-start(bf16[5,80,128]{2,1,0:T(8,128)(2,1)S(1)} %pad_maximum_fusion), channel_id=1, source_target_pairs={{0,0},{8,32},{16,64},{24,96},{32,8},{40,40},{48,72},{56,104},{64,1... | collective-permute-start | bytes 307208 | tf_op jit(solution)/shard_map/ppermute | solution.py:302
  58.7 4.0 %copy-start.4 = (s32[1,1,8]{2,1,0:T(1,128)S(1)}, s32[1,1,8]{2,1,0:T(1,128)}, u32[]{:S(2)}) copy-start(s32[1,1,8]{2,1,0:T(1,128)} %param.21) | copy-start | bytes 100
  58.7 26.5 %all-to-all-start.1 = ((bf16[4,896,128]{2,1,0:T(8,128)(2,1)}), bf16[4,896,128]{2,1,0:T(8,128)(2,1)S(1)}, u32[]{:S(2)}, u32[]{:S(2)}) async-start(bf16[4,896,128]{2,1,0:T(8,128)(2,1)} %shard_map.176), calls=%async_computation.1 | async-start | bytes 1835008 | tf_op jit(solution)/shard_map/all_to_all | solution.py:316
  85.2 13.8 %copy-start.2 = (bf16[1,32,288]{2,1,0:T(8,128)(2,1)S(1)}, bf16[1,32,288]{2,1,0:T(8,128)(2,1)}, u32[]{:S(2)}) copy-start(bf16[1,32,288]{2,1,0:T(8,128)(2,1)} %param.17) | copy-start | bytes 55300
  85.2 24.8 %copy-start = (bf16[16,32,160]{2,1,0:T(8,128)(2,1)S(1)}, bf16[16,32,160]{2,1,0:T(8,128)(2,1)}, u32[]{:S(2)}) copy-start(bf16[16,32,160]{2,1,0:T(8,128)(2,1)} %residual.1) | copy-start | bytes 491524
  85.2 24.8 %copy-start.1 = (bf16[1,32,160]{2,1,0:T(8,128)(2,1)S(1)}, bf16[1,32,160]{2,1,0:T(8,128)(2,1)}, u32[]{:S(2)}) copy-start(bf16[1,32,160]{2,1,0:T(8,128)(2,1)} %long_residual.1) | copy-start | bytes 30724
  87.1 23.0 %all-to-all-start.2 = ((bf16[4,688,128]{2,1,0:T(8,128)(2,1)}), bf16[4,688,128]{2,1,0:T(8,128)(2,1)S(1)}, u32[]{:S(2)}, u32[]{:S(2)}) async-start(bf16[4,688,128]{2,1,0:T(8,128)(2,1)} %shard_map.177), calls=%async_computation.2 | async-start | bytes 1409024 | tf_op jit(solution)/shard_map/all_to_all | solution.py:327

commit v12 on v10

--- a/solution.py
+++ b/solution.py
@@ -186,11 +186,11 @@
 
 
 def pack_kernel(place, length, length_l, *refs):
-    sources, (block, own_q, own_tree), held, (slices, sems) = refs[:8], refs[8:11], refs[11:19], refs[19:]
-    copies = [pltpu.make_async_copy(sources[i], held[i], sems.at[i]) for i in range(8)]
+    sources, (block, own_q, own_tree, kept), held, (slices, sems) = refs[:9], refs[9:13], refs[13:22], refs[22:]
+    copies = [pltpu.make_async_copy(sources[i], held[i], sems.at[i]) for i in range(9)]
     for copy in copies:
         copy.start()
-    parents, parents_l, queries, queries_l, keys, keys_l, tree, tree_l = held
+    parents, parents_l, chosen, queries, queries_l, keys, keys_l, tree, tree_l = held
     lanes = lax.broadcasted_iota(jnp.int32, (TREE, 128), 1)
     tile4 = onehot(TREE, 128, lambda row, col: col % 32 == row)
     widen = onehot(TREE, 128, lambda row, col: col == row)
@@ -210,6 +210,9 @@
         extras.append(jnp.where(lanes == 33, length_l[0, 0].astype(F32), extra).astype(BF))
     for copy in copies[2:]:
         copy.wait()
+    count = chosen.shape[1]
+    pick = jnp.where(lax.broadcasted_iota(jnp.int32, (TREE, count), 0) == chosen[...], 1.0, 0.0).astype(BF)
+    kept[...] = lax.dot_general(pick, tree[...], (((0,), (0,)), ((), ())), preferred_element_type=F32).astype(BF)
     for d in range(4):
         block[d, 0:288] = keys[:, :128]
         block[d, 288:576] = keys[:, 128:]
@@ -269,20 +272,22 @@
     kv, place = lax.optimization_barrier((jnp.concatenate([key_up, value_up], axis=1), place))
     kv = lax.ppermute(kv, ("y", "x", "a", "b"), pairs)
     rows = 8 * TREE
-    block, query_l, tree_l = pl.pallas_call(
+    block, query_l, tree_l, accepted_cache = pl.pallas_call(
         pack_kernel,
         out_shape=(
             jax.ShapeDtypeStruct((4, BLOCK, 128), BF),
             jax.ShapeDtypeStruct((rows, 128), BF),
             jax.ShapeDtypeStruct((4 * TREE, 128), BF),
+            jax.ShapeDtypeStruct((accepted.shape[2], KVR + ROPE), BF),
         ),
-        in_specs=[SMEM] * 3 + [HBM] * 8,
-        out_specs=(VMEM, VMEM, VMEM),
+        in_specs=[SMEM] * 3 + [HBM] * 9,
+        out_specs=(VMEM, VMEM, VMEM, VMEM),
         scratch_shapes=[pltpu.VMEM((1, TREE), jnp.int32)] * 2
+        + [pltpu.VMEM((1, accepted.shape[2]), jnp.int32)]
         + [pltpu.VMEM((TREE, HEADS * (NOPE + ROPE)), BF)] * 2
         + [pltpu.VMEM((KVR + ROPE, 256), BF)] * 2
         + [pltpu.VMEM((TREE, KVR + ROPE), BF)] * 2
-        + [pltpu.VMEM((4, rows, 128), BF), pltpu.SemaphoreType.DMA((8,))],
+        + [pltpu.VMEM((4, rows, 128), BF), pltpu.SemaphoreType.DMA((9,))],
         compiler_params=PARAMS,
         cost_estimate=COST,
     )(
@@ -290,7 +295,7 @@
         *[
             pltpu.with_memory_space_constraint(value, pltpu.HBM)
             for value in (
-                parents[0], long_parents, queries[0], long_queries[0], cache[0, 0].T, long_cache[0].T,
+                parents[0], long_parents, accepted[0], queries[0], long_queries[0], cache[0, 0].T, long_cache[0].T,
                 tree_latent[0], long_tree_latent[0],
             )
         ],
@@ -336,8 +341,7 @@
         scratch_shapes=[pltpu.VMEM((TOKENS, 128), F32)],
         compiler_params=PARAMS,
     )(back, residual, long_residual)
-    accepted_cache = jnp.take_along_axis(tree_latent[0], accepted[0, 0][:, None], axis=0)[None, None]
-    return hidden, accepted_cache, long_hidden
+    return hidden, accepted_cache[None, None], long_hidden
 
 
 def solution(mesh):

time: 106 us -> 105 us (level)
  blocking collectives: 62.9 us -> 80.8 us
  waiting for transfers between devices: 9.82 us -> 0.01 us
  starting transfers between devices: 16.6 us -> 9.3 us
    all_to_all x0 -> x1, blocking collectives: none -> 17.9 us  [on_device(): back = lax.all_to_all(send, 'x', 0, 0)]
    all_to_all x1 -> x0, waiting for transfers between devices: 9.81 us -> none  [on_device(): back = lax.all_to_all(send, 'x', 0, 0)]
    all_to_all x1 -> x0, starting transfers between devices: 7.15 us -> none  [on_device(): back = lax.all_to_all(send, 'x', 0, 0)]
  transfers between devices with their start and end apart: 5 -> 4, of which waited for: 1 -> 0; matrix products, arithmetic and copies ran while one was open for 1% -> 0% of each run, Pallas kernels for 4% -> 4%
where the time goes in v12:
time: 105 us; the launch traced here: 104 us
  blocking collectives  80.8 us (77%)
  Pallas kernels  10.8 us (10%)
  starting transfers between devices  9.3 us (9%)
  between operations  2.01 us (2%)
    all_gather x1, blocking collectives, on_device(): kv = lax.all_gather(kv, ('y', 'c'))  25.5 us
    all_gather x1, blocking collectives, on_device(): out_rows = lax.all_gather(out_rows, ('b', 'c'))  21.6 us
    all_to_all x1, blocking collectives, on_device(): back = lax.all_to_all(send, 'x', 0, 0)  17.9 us
    all_gather x1, blocking collectives, on_device(): cols = lax.all_gather(out_weight, 'x')  15.8 us
    all_to_all x1, starting transfers between devices, on_device(): got = lax.all_to_all(block, 'x', 0, 0)  4.49 us
    pallas_call x1, Pallas kernels, on_device(): pl.pallas_call(pack_kernel, out_shape=(jax.ShapeDtypeStruct((4, BLOCK, 12...  4.46 us
    pallas_call x1, Pallas kernels, on_device(): pl.pallas_call(attend_kernel, out_shape=jax.ShapeDtypeStruct((4, 5 * TREE...  4.42 us
    all_to_all x1, starting transfers between devices, on_device(): shared = lax.all_to_all(heads, 'y', 0, 0)  3.5 us
  transfers between devices with their start and end apart: 4, of which 0 were waited for; matrix products, arithmetic and copies ran while one was open for 0% of the time, Pallas kernels for 4%

profile of v12, /device:TPU:1, one launch (start us, length us, event | category | flops | bytes accessed | tf_op | source)
XLA Modules:
  0.0 103.9 jit_solution(4040292931178059997)
XLA Ops:
  0.6 0.1 pad_add_fusion.place
  0.7 0.8 pad_maximum_fusion.1
  1.5 0.7 collective-permute-start
  2.2 15.8 %all-gather = bf16[320,160]{1,0:T(8,128)(2,1)S(1)} all-gather(bf16[80,160]{1,0:T(8,128)(2,1)} %param.31), channel_id=2, replica_groups=mesh['y'=4,'x'=4,'a'=4,'b'=4,'c'=2] {'x'}, dimensions={0}, use_global_device_ids=true | all-gather | bytes 128000 | tf_op jit(solution)/shard_map/all_gather | solution.py:303
  19.3 0.1 maximum_bitcast_fusion
  19.4 4.5 %shard_map.175 = (bf16[4,1536,128]{2,1,0:T(8,128)(2,1)}, bf16[256,128]{1,0:T(8,128)(2,1)S(1)}, bf16[128,128]{1,0:T(8,128)(2,1)S(1)}, bf16[8,288]{1,0:T(8,128)(2,1)}) custom-call(s32[2]{0:T(128)S(1)} %pad_add_fusion.place, s32[1,1]{1,0:T(1,128)S(6)} %copy.19.length, s32[1,1]{1,0:T(1,128)S(6)} %copy.20.length_l, s32[1,32]{1,0:T(1,128)} %bitcast.39, ...), custom_call_target="tpu_custom_call" | custom-call | flops 6000000000 | bytes 18000000 | tf_op jit(solution)/shard_map/pallas_call | solution.py:275
  23.9 0.0 collective-permute-done
  23.9 4.5 %all-to-all-start = ((bf16[4,1536,128]{2,1,0:T(8,128)(2,1)}), bf16[4,1536,128]{2,1,0:T(8,128)(2,1)S(1)}, u32[]{:S(2)}, u32[]{:S(2)}) async-start(bf16[4,1536,128]{2,1,0:T(8,128)(2,1)} %get-tuple-element.19), calls=%async_computation | async-start | bytes 3145728 | tf_op jit(solution)/shard_map/all_to_all | solution.py:306
  28.4 0.7 collective-permute-start.1
  29.1 25.5 %all-gather.1 = bf16[640,512]{1,0:T(8,128)(2,1)S(1)} all-gather(bf16[80,512]{1,0:T(8,128)(2,1)S(1)} %collective-permute-done), channel_id=3, replica_groups=mesh['y'=4,'x'=4,'a'=4,'b'=4,'c'=2] {'y','c'}, dimensions={0}, use_global_device_ids=true | all-gather | bytes 737280 | tf_op jit(solution)/shard_map/all_gather | solution.py:308
  54.6 0.0 collective-permute-done.1
  54.6 0.0 all-to-all-done.got
  54.6 4.4 %shard_map.176 = bf16[4,896,128]{2,1,0:T(8,128)(2,1)} custom-call(bf16[4,1536,128]{2,1,0:T(8,128)(2,1)S(1)} %all-to-all-done.got, bf16[256,128]{1,0:T(8,128)(2,1)S(1)} %get-tuple-element.20.query_l, bf16[128,128]{1,0:T(8,128)(2,1)S(1)} %get-tuple-element.21.tree_l, bf16[4,2,80,512]{3,2,1,0:T(8,128)(2,1)S(1)} %bitcast.30), custom_call_target="tpu_custom_call" | custom-call | flops 6000000000 | bytes 18000000 | tf_op jit(solution)/shard_map/pallas_call | solution.py:312
  59.0 3.5 %all-to-all-start.1 = ((bf16[4,896,128]{2,1,0:T(8,128)(2,1)}), bf16[4,896,128]{2,1,0:T(8,128)(2,1)S(1)}, u32[]{:S(2)}, u32[]{:S(2)}) async-start(bf16[4,896,128]{2,1,0:T(8,128)(2,1)} %shard_map.176), calls=%async_computation.1 | async-start | bytes 1835008 | tf_op jit(solution)/shard_map/all_to_all | solution.py:321
  62.5 21.6 %all-gather.2 = bf16[40,80,128]{2,1,0:T(8,128)(2,1)S(1)} all-gather(bf16[5,80,128]{2,1,0:T(8,128)(2,1)S(1)} %collective-permute-done.1), channel_id=4, replica_groups=mesh['y'=4,'x'=4,'a'=4,'b'=4,'c'=2] {'b','c'}, dimensions={0}, use_global_device_ids=true | all-gather | bytes 921600 | tf_op jit(solution)/shard_map/all_gather | solution.py:322
  84.1 0.0 all-to-all-done.1.got
  84.1 0.0 copy-start
  84.1 0.0 copy-start.1
  84.1 1.0 shard_map.177
  85.2 17.9 %all_to_all.15.got = bf16[4,688,128]{2,1,0:T(8,128)(2,1)S(1)} all-to-all(bf16[4,688,128]{2,1,0:T(8,128)(2,1)S(1)} %shard_map.177), channel_id=1, replica_groups=mesh['y'=4,'x'=4,'a'=4,'b'=4,'c'=2] {'x'}, dimensions={0} | all-to-all | bytes 1409024 | tf_op jit(solution)/shard_map/all_to_all | solution.py:332
  103.0 0.0 copy-done
  103.0 0.0 copy-done.1
  103.1 0.9 shard_map.178
  (3 shorter events, 0.0 us)
Async XLA Ops:
  1.5 22.4 %collective-permute-start = (bf16[80,512]{1,0:T(8,128)(2,1)S(1)}, bf16[80,512]{1,0:T(8,128)(2,1)S(1)}, u32[]{:S(2)}, u32[]{:S(2)}) collective-permute-start(bf16[80,512]{1,0:T(8,128)(2,1)S(1)} %pad_maximum_fusion.1), channel_id=1, source_target_pairs={{0,0},{2,130},{4,260},{6,390},{8,40},{10,170},{12,300},{14,430},{1... | collective-permute-start | bytes 245768 | tf_op jit(solution)/shard_map/ppermute | solution.py:273
  23.9 30.7 %all-to-all-start = ((bf16[4,1536,128]{2,1,0:T(8,128)(2,1)}), bf16[4,1536,128]{2,1,0:T(8,128)(2,1)S(1)}, u32[]{:S(2)}, u32[]{:S(2)}) async-start(bf16[4,1536,128]{2,1,0:T(8,128)(2,1)} %get-tuple-element.19), calls=%async_computation | async-start | bytes 3145728 | tf_op jit(solution)/shard_map/all_to_all | solution.py:306
  28.4 26.2 %collective-permute-start.1 = (bf16[5,80,128]{2,1,0:T(8,128)(2,1)S(1)}, bf16[5,80,128]{2,1,0:T(8,128)(2,1)S(1)}, u32[]{:S(2)}, u32[]{:S(2)}) collective-permute-start(bf16[5,80,128]{2,1,0:T(8,128)(2,1)S(1)} %pad_maximum_fusion), channel_id=1, source_target_pairs={{0,0},{8,32},{16,64},{24,96},{32,8},{40,40},{48,72},{56,104},{64,1... | collective-permute-start | bytes 307208 | tf_op jit(solution)/shard_map/ppermute | solution.py:307
  59.0 25.1 %all-to-all-start.1 = ((bf16[4,896,128]{2,1,0:T(8,128)(2,1)}), bf16[4,896,128]{2,1,0:T(8,128)(2,1)S(1)}, u32[]{:S(2)}, u32[]{:S(2)}) async-start(bf16[4,896,128]{2,1,0:T(8,128)(2,1)} %shard_map.176), calls=%async_computation.1 | async-start | bytes 1835008 | tf_op jit(solution)/shard_map/all_to_all | solution.py:321
  84.1 18.9 %copy-start = (bf16[16,32,160]{2,1,0:T(8,128)(2,1)S(1)}, bf16[16,32,160]{2,1,0:T(8,128)(2,1)}, u32[]{:S(2)}) copy-start(bf16[16,32,160]{2,1,0:T(8,128)(2,1)} %residual.1) | copy-start | bytes 491524
  84.1 18.9 %copy-start.1 = (bf16[1,32,160]{2,1,0:T(8,128)(2,1)S(1)}, bf16[1,32,160]{2,1,0:T(8,128)(2,1)}, u32[]{:S(2)}) copy-start(bf16[1,32,160]{2,1,0:T(8,128)(2,1)} %long_residual.1) | copy-start | bytes 30724

commit v13 on v12

--- a/solution.py
+++ b/solution.py
@@ -185,12 +185,17 @@
     return jnp.where(match(row, col), 1.0, 0.0).astype(BF)
 
 
-def pack_kernel(place, length, length_l, *refs):
-    sources, (block, own_q, own_tree, kept), held, (slices, sems) = refs[:9], refs[9:13], refs[13:22], refs[22:]
+def pack_kernel(place, length, length_l, cols, *refs):
+    sources, (block, own_q, own_tree, kept, weight), held, (slices, sems) = refs[:9], refs[9:14], refs[14:23], refs[23:]
     copies = [pltpu.make_async_copy(sources[i], held[i], sems.at[i]) for i in range(9)]
     for copy in copies:
         copy.start()
     parents, parents_l, chosen, queries, queries_l, keys, keys_l, tree, tree_l = held
+    tails = 0.0
+    for k in range(4):
+        weight[k] = cols[k, :, :128]
+        tails += dot(cols[k, :, 128:], onehot(32, 128, lambda row, col: col == row + 32 * k))
+    weight[4] = tails.astype(BF)
     lanes = lax.broadcasted_iota(jnp.int32, (TREE, 128), 1)
     tile4 = onehot(TREE, 128, lambda row, col: col % 32 == row)
     widen = onehot(TREE, 128, lambda row, col: col == row)
@@ -272,16 +277,18 @@
     kv, place = lax.optimization_barrier((jnp.concatenate([key_up, value_up], axis=1), place))
     kv = lax.ppermute(kv, ("y", "x", "a", "b"), pairs)
     rows = 8 * TREE
-    block, query_l, tree_l, accepted_cache = pl.pallas_call(
+    cols = lax.all_gather(out_weight, "x")
+    block, query_l, tree_l, accepted_cache, out_rows = pl.pallas_call(
         pack_kernel,
         out_shape=(
             jax.ShapeDtypeStruct((4, BLOCK, 128), BF),
             jax.ShapeDtypeStruct((rows, 128), BF),
             jax.ShapeDtypeStruct((4 * TREE, 128), BF),
             jax.ShapeDtypeStruct((accepted.shape[2], KVR + ROPE), BF),
+            jax.ShapeDtypeStruct((5, out_weight.shape[0], 128), BF),
         ),
-        in_specs=[SMEM] * 3 + [HBM] * 9,
-        out_specs=(VMEM, VMEM, VMEM, VMEM),
+        in_specs=[SMEM] * 3 + [VMEM] + [HBM] * 9,
+        out_specs=(VMEM,) * 5,
         scratch_shapes=[pltpu.VMEM((1, TREE), jnp.int32)] * 2
         + [pltpu.VMEM((1, accepted.shape[2]), jnp.int32)]
         + [pltpu.VMEM((TREE, HEADS * (NOPE + ROPE)), BF)] * 2
@@ -291,7 +298,7 @@
         compiler_params=PARAMS,
         cost_estimate=COST,
     )(
-        place, cache_lengths, long_plan,
+        place, cache_lengths, long_plan, cols,
         *[
             pltpu.with_memory_space_constraint(value, pltpu.HBM)
             for value in (
@@ -300,8 +307,6 @@
             )
         ],
     )
-    cols = lax.all_gather(out_weight, "x")
-    out_rows = jnp.stack([cols[k, :, :128] for k in range(4)] + [jnp.concatenate([cols[k, :, 128:] for k in range(4)], axis=1)])
     block, kv, out_rows = lax.optimization_barrier((block, kv, out_rows))
     got = lax.all_to_all(block, "x", 0, 0)
     out_rows = lax.ppermute(out_rows, ("x", "a"), [(4 * i + j, 4 * j + i) for i in range(4) for j in range(4)])

time: 105 us -> 105 us (level)
    all_gather x1, blocking collectives: 15.8 us -> 17.7 us  [on_device(): cols = lax.all_gather(out_weight, 'x')]
where the time goes in v13:
time: 105 us; the launch traced here: 104 us
  blocking collectives  81.7 us (78%)
  Pallas kernels  10.9 us (10%)
  starting transfers between devices  8.4 us (8%)
  between operations  1.99 us (2%)
    all_gather x1, blocking collectives, on_device(): kv = lax.all_gather(kv, ('y', 'c'))  24.5 us
    all_gather x1, blocking collectives, on_device(): out_rows = lax.all_gather(out_rows, ('b', 'c'))  20.9 us
    all_to_all x1, blocking collectives, on_device(): back = lax.all_to_all(send, 'x', 0, 0)  18.6 us
    all_gather x1, blocking collectives, on_device(): cols = lax.all_gather(out_weight, 'x')  17.7 us
    pallas_call x1, Pallas kernels, on_device(): pl.pallas_call(pack_kernel, out_shape=(jax.ShapeDtypeStruct((4, BLOCK, 12...  4.58 us
    pallas_call x1, Pallas kernels, on_device(): pl.pallas_call(attend_kernel, out_shape=jax.ShapeDtypeStruct((4, 5 * TREE...  4.43 us
    all_to_all x1, starting transfers between devices, on_device(): got = lax.all_to_all(block, 'x', 0, 0)  3.57 us
    all_to_all x1, starting transfers between devices, on_device(): shared = lax.all_to_all(heads, 'y', 0, 0)  3.5 us
  transfers between devices with their start and end apart: 4, of which 0 were waited for; matrix products, arithmetic and copies ran while one was open for 0% of the time, Pallas kernels for 4%

profile of v13, /device:TPU:1, one launch (start us, length us, event | category | flops | bytes accessed | tf_op | source)
XLA Modules:
  0.0 103.9 jit_solution(16145690699315234065)
XLA Ops:
  0.6 0.1 pad_add_fusion.place
  0.7 0.8 pad_maximum_fusion
  1.5 0.7 collective-permute-start
  3.5 17.7 %all-gather = bf16[320,160]{1,0:T(8,128)(2,1)S(1)} all-gather(bf16[80,160]{1,0:T(8,128)(2,1)} %param.31), channel_id=2, replica_groups=mesh['y'=4,'x'=4,'a'=4,'b'=4,'c'=2] {'x'}, dimensions={0}, use_global_device_ids=true | all-gather | bytes 128000 | tf_op jit(solution)/shard_map/all_gather | solution.py:280
  21.2 4.6 %shard_map.175 = (bf16[4,1536,128]{2,1,0:T(8,128)(2,1)}, bf16[256,128]{1,0:T(8,128)(2,1)S(1)}, bf16[128,128]{1,0:T(8,128)(2,1)S(1)}, bf16[8,288]{1,0:T(8,128)(2,1)}, bf16[5,80,128]{2,1,0:T(8,128)(2,1)S(1)}) custom-call(s32[2]{0:T(128)S(1)} %pad_add_fusion.place, s32[1,1]{1,0:T(1,128)S(6)} %copy.19.length, s32[1,1]{1,0:T(1,128)S(6)} %copy.20.length_l, ...), custom_call_target="tpu_custom_call" | custom-call | flops 6000000000 | bytes 18000000 | tf_op jit(solution)/shard_map/pallas_call | solution.py:281
  25.8 0.0 collective-permute-done
  25.8 3.6 %all-to-all-start = ((bf16[4,1536,128]{2,1,0:T(8,128)(2,1)}), bf16[4,1536,128]{2,1,0:T(8,128)(2,1)S(1)}, u32[]{:S(2)}, u32[]{:S(2)}) async-start(bf16[4,1536,128]{2,1,0:T(8,128)(2,1)} %get-tuple-element.21), calls=%async_computation | async-start | bytes 3145728 | tf_op jit(solution)/shard_map/all_to_all | solution.py:311
  29.4 0.7 collective-permute-start.1
  30.0 24.5 %all-gather.1 = bf16[640,512]{1,0:T(8,128)(2,1)S(1)} all-gather(bf16[80,512]{1,0:T(8,128)(2,1)S(1)} %collective-permute-done), channel_id=3, replica_groups=mesh['y'=4,'x'=4,'a'=4,'b'=4,'c'=2] {'y','c'}, dimensions={0}, use_global_device_ids=true | all-gather | bytes 737280 | tf_op jit(solution)/shard_map/all_gather | solution.py:313
  54.5 0.0 collective-permute-done.1
  54.5 0.0 all-to-all-done.got
  54.5 4.4 %shard_map.176 = bf16[4,896,128]{2,1,0:T(8,128)(2,1)} custom-call(bf16[4,1536,128]{2,1,0:T(8,128)(2,1)S(1)} %all-to-all-done.got, bf16[256,128]{1,0:T(8,128)(2,1)S(1)} %get-tuple-element.22.query_l, bf16[128,128]{1,0:T(8,128)(2,1)S(1)} %get-tuple-element.23.tree_l, bf16[4,2,80,512]{3,2,1,0:T(8,128)(2,1)S(1)} %bitcast.20), custom_call_target="tpu_custom_call" | custom-call | flops 6000000000 | bytes 18000000 | tf_op jit(solution)/shard_map/pallas_call | solution.py:317
  59.0 3.5 %all-to-all-start.1 = ((bf16[4,896,128]{2,1,0:T(8,128)(2,1)}), bf16[4,896,128]{2,1,0:T(8,128)(2,1)S(1)}, u32[]{:S(2)}, u32[]{:S(2)}) async-start(bf16[4,896,128]{2,1,0:T(8,128)(2,1)} %shard_map.176), calls=%async_computation.1 | async-start | bytes 1835008 | tf_op jit(solution)/shard_map/all_to_all | solution.py:326
  62.5 20.9 %all-gather.2 = bf16[40,80,128]{2,1,0:T(8,128)(2,1)S(1)} all-gather(bf16[5,80,128]{2,1,0:T(8,128)(2,1)S(1)} %collective-permute-done.1), channel_id=4, replica_groups=mesh['y'=4,'x'=4,'a'=4,'b'=4,'c'=2] {'b','c'}, dimensions={0}, use_global_device_ids=true | all-gather | bytes 921600 | tf_op jit(solution)/shard_map/all_gather | solution.py:327
  83.4 0.0 all-to-all-done.1.got
  83.4 0.0 copy-start
  83.4 0.0 copy-start.1
  83.4 1.0 shard_map.177
  84.4 18.6 %all_to_all.15.got = bf16[4,688,128]{2,1,0:T(8,128)(2,1)S(1)} all-to-all(bf16[4,688,128]{2,1,0:T(8,128)(2,1)S(1)} %shard_map.177), channel_id=1, replica_groups=mesh['y'=4,'x'=4,'a'=4,'b'=4,'c'=2] {'x'}, dimensions={0} | all-to-all | bytes 1409024 | tf_op jit(solution)/shard_map/all_to_all | solution.py:337
  103.1 0.0 copy-done
  103.1 0.0 copy-done.1
  103.1 0.9 shard_map.178
Async XLA Ops:
  1.5 24.3 %collective-permute-start = (bf16[80,512]{1,0:T(8,128)(2,1)S(1)}, bf16[80,512]{1,0:T(8,128)(2,1)S(1)}, u32[]{:S(2)}, u32[]{:S(2)}) collective-permute-start(bf16[80,512]{1,0:T(8,128)(2,1)S(1)} %pad_maximum_fusion), channel_id=1, source_target_pairs={{0,0},{2,130},{4,260},{6,390},{8,40},{10,170},{12,300},{14,430},{1... | collective-permute-start | bytes 245768 | tf_op jit(solution)/shard_map/ppermute | solution.py:278
  25.8 28.8 %all-to-all-start = ((bf16[4,1536,128]{2,1,0:T(8,128)(2,1)}), bf16[4,1536,128]{2,1,0:T(8,128)(2,1)S(1)}, u32[]{:S(2)}, u32[]{:S(2)}) async-start(bf16[4,1536,128]{2,1,0:T(8,128)(2,1)} %get-tuple-element.21), calls=%async_computation | async-start | bytes 3145728 | tf_op jit(solution)/shard_map/all_to_all | solution.py:311
  29.4 25.2 %collective-permute-start.1 = (bf16[5,80,128]{2,1,0:T(8,128)(2,1)S(1)}, bf16[5,80,128]{2,1,0:T(8,128)(2,1)S(1)}, u32[]{:S(2)}, u32[]{:S(2)}) collective-permute-start(bf16[5,80,128]{2,1,0:T(8,128)(2,1)S(1)} %get-tuple-element.25), channel_id=1, source_target_pairs={{0,0},{8,32},{16,64},{24,96},{32,8},{40,40},{48,72},{56,104},{64,1... | collective-permute-start | bytes 307208 | tf_op jit(solution)/shard_map/ppermute | solution.py:312
  59.0 24.4 %all-to-all-start.1 = ((bf16[4,896,128]{2,1,0:T(8,128)(2,1)}), bf16[4,896,128]{2,1,0:T(8,128)(2,1)S(1)}, u32[]{:S(2)}, u32[]{:S(2)}) async-start(bf16[4,896,128]{2,1,0:T(8,128)(2,1)} %shard_map.176), calls=%async_computation.1 | async-start | bytes 1835008 | tf_op jit(solution)/shard_map/all_to_all | solution.py:326
  83.4 19.7 %copy-start = (bf16[16,32,160]{2,1,0:T(8,128)(2,1)S(1)}, bf16[16,32,160]{2,1,0:T(8,128)(2,1)}, u32[]{:S(2)}) copy-start(bf16[16,32,160]{2,1,0:T(8,128)(2,1)} %residual.1) | copy-start | bytes 491524
  83.4 19.7 %copy-start.1 = (bf16[1,32,160]{2,1,0:T(8,128)(2,1)S(1)}, bf16[1,32,160]{2,1,0:T(8,128)(2,1)}, u32[]{:S(2)}) copy-start(bf16[1,32,160]{2,1,0:T(8,128)(2,1)} %long_residual.1) | copy-start | bytes 30724
